TPU v7x, 128 devices: a whole 4x4x4 slice. The times are simulated.
128 devices in a mesh: slot: 32 (over y, z, core), hid: 4 (over x).
Axes of the slice: x: 4, y: 4, z: 4, core: 2. Of those that a mesh axis runs over, the one named last changes fastest.
Arguments:
- master: float32 [16, 3, 4, 393216], P(None, None, 'hid', 'slot'), may hold values from -0.125 to 0.125
- first_moment: float32 [16, 3, 4, 393216], P(None, None, 'hid', 'slot'), may hold values from -0.3 to 0.3
- second_moment: float32 [16, 3, 4, 393216], P(None, None, 'hid', 'slot'), may hold values from 0.0001 to 0.01
- slot_weights: bfloat16 [32, 3, 768, 2048], P('slot', None, 'hid'), may hold values from -0.125 to 0.125
- back_rows: bfloat16 [32, 1024, 2048], P('slot'), may hold values from -6 to 6
- readout: bfloat16 [32, 1024, 2048], P('slot'), may hold values from -0.25 to 0.25
- ref_logratio: float32 [32, 1024], P('slot'), may hold values from -9 to 0
- labels: int32 [32, 1024], P('slot'), may hold values 0 or 1
- place_cur: int32 [32], replicated, may hold values from 0 to 15, as said below
- place_next: int32 [32], replicated, may hold values from 0 to 15, as said below
- fwd_rows: bfloat16 [8192, 2048], P('slot', 'hid'), may hold values from -6 to 6
- routes: int32 [8192, 1], P('slot'), may hold values from 0 to 31; in each aligned block of 256 rows (0 to 255, 256 to 511, ...) at most 16 rows name the same one
Outputs:
- out_rows: bfloat16 [8192, 2048], P('slot', 'hid')
- new_master: float32 [16, 3, 4, 393216], P(None, None, 'hid', 'slot')
- new_first: float32 [16, 3, 4, 393216], P(None, None, 'hid', 'slot')
- new_second: float32 [16, 3, 4, 393216], P(None, None, 'hid', 'slot')
Inputs may be any that keep to these rules, and one draw needn't show every extreme that they name: `place_cur`: every expert 0 to 15 is held by at least one slot. `place_next`: every expert 0 to 15 is held by at least one slot. `routes`: the rows of one slot name any one slot at most 16 times, a bound that some block reaches.
All inputs are finite; a program needn't handle non-finite values. No bound on the sum of `labels` on one device may be relied on, other than what follows from the above.
Results may differ from a plain program's by a relative error of at most 0.008.
Values may be sent and summed in bfloat16 or wider, within the bound.
No kernel may reach another device: no remote copies, remote signals or barrier semaphores. Data moves between devices by JAX's collectives and lax.ppermute only.
A program may use at most 128 MiB of HBM per device.

v0:
```python
import jax
import jax.numpy as jnp
from jax import lax
from jax.sharding import PartitionSpec as P

beta_kto = 1.0
desired_weight = 1.0
undesired_weight = 1.33
learn_rate = 0.004
decay_first = 0.9
decay_second = 0.999
correct_first = 0.9999734386011124
correct_second = 0.09520785288629043
adam_eps = 1e-08
weight_decay = 0.1


def expert_pass(inputs, weights):
    across = (((1,), (1,)), ((), ()))
    gate_vals = lax.dot_general(inputs, weights[0], across, preferred_element_type=jnp.float32)
    up_vals = lax.dot_general(inputs, weights[1], across, preferred_element_type=jnp.float32)
    hidden = (gate_vals * jax.nn.sigmoid(gate_vals) * up_vals).astype(jnp.bfloat16)
    produced = jnp.dot(hidden, weights[2], preferred_element_type=jnp.float32)
    return (gate_vals, up_vals, hidden, produced)


def kto_slope(scores, labels, center):
    sigma_v = jax.nn.sigmoid(beta_kto * (scores - center))
    signed = jnp.where(labels == 1, -desired_weight, undesired_weight)
    return beta_kto * sigma_v * (1.0 - sigma_v) * signed


def expert_backward(inputs, direction, weights, slope, gate_vals, up_vals, hidden):
    d_expert = (slope[:, None] * direction.astype(jnp.float32)).astype(jnp.bfloat16)
    d_hidden = lax.dot_general(
        d_expert, weights[2], (((1,), (1,)), ((), ())), preferred_element_type=jnp.float32
    )
    sigma_g = jax.nn.sigmoid(gate_vals)
    d_gate = (d_hidden * up_vals * sigma_g * (1.0 + gate_vals * (1.0 - sigma_g))).astype(
        jnp.bfloat16
    )
    d_up = (d_hidden * gate_vals * sigma_g).astype(jnp.bfloat16)
    contract = (((0,), (0,)), ((), ()))
    grad_gate = lax.dot_general(d_gate, inputs, contract, preferred_element_type=jnp.float32)
    grad_up = lax.dot_general(d_up, inputs, contract, preferred_element_type=jnp.float32)
    grad_down = lax.dot_general(hidden, d_expert, contract, preferred_element_type=jnp.float32)
    return jnp.stack([grad_gate, grad_up, grad_down])


def adamw_update(master, first_moment, second_moment, summed):
    new_first = decay_first * first_moment + (1.0 - decay_first) * summed
    new_second = decay_second * second_moment + (1.0 - decay_second) * summed * summed
    update = new_first / correct_first / (jnp.sqrt(new_second / correct_second) + adam_eps)
    new_master = master - learn_rate * (update + weight_decay * master)
    return (new_master, new_first, new_second)


def shards(
    master,
    first_moment,
    second_moment,
    slot_weights,
    back_rows,
    readout,
    ref_logratio,
    labels,
    place_cur,
    place_next,
    fwd_rows,
    routes,
):
    slot_count = lax.axis_size("slot")
    experts_here = master.shape[0]
    weights = slot_weights[0]
    width = weights.shape[2]
    owned_units = master.shape[3] // width
    inputs = back_rows[0]
    direction = readout[0]
    gate_vals, up_vals, hidden, partial_value = expert_pass(inputs, weights)
    row_part = jnp.sum(partial_value * direction.astype(jnp.float32), axis=1)
    policy = lax.psum(row_part, "hid")
    scores = policy - ref_logratio[0]
    row_total = slot_count * inputs.shape[0]
    center = lax.psum(jnp.sum(scores), "slot") / row_total
    slope = kto_slope(scores, labels[0], center)
    grads = expert_backward(inputs, direction, weights, slope, gate_vals, up_vals, hidden)
    arrived = lax.all_to_all(
        grads[None].astype(jnp.bfloat16), "slot", split_axis=2, concat_axis=0, tiled=True
    ).astype(jnp.float32)
    arrived = arrived.reshape(slot_count, 3, 1, owned_units * width)
    owner_map = (place_cur[None, :] == jnp.arange(experts_here, dtype=jnp.int32)[:, None]).astype(
        jnp.float32
    )
    summed = jnp.einsum("es,sabc->eabc", owner_map, arrived, precision=lax.Precision.HIGHEST)
    new_master, new_first, new_second = adamw_update(master, first_moment, second_moment, summed)
    refreshed = new_master.astype(jnp.bfloat16)
    pick_map = (place_next[:, None] == jnp.arange(experts_here, dtype=jnp.int32)[None, :]).astype(
        jnp.bfloat16
    )
    picked = jnp.einsum(
        "se,eabc->sabc", pick_map, refreshed, preferred_element_type=jnp.float32
    ).astype(jnp.bfloat16)
    picked = picked.reshape(slot_count, 3, owned_units, width)
    resident = lax.all_to_all(picked, "slot", split_axis=0, concat_axis=2, tiled=True)[0]
    capacity = 2 * fwd_rows.shape[0] // slot_count
    quarter = fwd_rows.shape[1]
    target = routes[:, 0]
    target_map = (target[:, None] == jnp.arange(slot_count, dtype=jnp.int32)[None, :]).astype(
        jnp.int32
    )
    earlier = jnp.cumsum(target_map, axis=0) - target_map
    position = jnp.sum(earlier * target_map, axis=1)
    slot_place = target * capacity + position
    place_map = (
        slot_place[None, :] == jnp.arange(slot_count * capacity, dtype=jnp.int32)[:, None]
    ).astype(jnp.bfloat16)
    widened = lax.all_gather(fwd_rows, "hid", axis=1, tiled=True)
    buffer_rows = jnp.dot(place_map, widened, preferred_element_type=jnp.float32).astype(
        jnp.bfloat16
    )
    buffer_rows = buffer_rows.reshape(slot_count, capacity, widened.shape[1])
    arrived_rows = lax.all_to_all(
        buffer_rows, "slot", split_axis=0, concat_axis=0, tiled=True
    ).reshape(slot_count * capacity, widened.shape[1])
    fwd_partial = expert_pass(arrived_rows, resident)[3]
    totals = lax.psum(fwd_partial, "hid")
    shares = lax.dynamic_slice_in_dim(totals, lax.axis_index("hid") * quarter, quarter, 1)
    outgoing = shares.astype(jnp.bfloat16).reshape(slot_count, capacity, quarter)
    returned = lax.all_to_all(outgoing, "slot", split_axis=0, concat_axis=0, tiled=True).reshape(
        slot_count * capacity, quarter
    )
    out_rows = lax.dot_general(
        place_map, returned, (((0,), (0,)), ((), ())), preferred_element_type=jnp.float32
    ).astype(jnp.bfloat16)
    return (out_rows, new_master, new_first, new_second)


def solution(mesh):
    return jax.shard_map(
        shards,
        mesh=mesh,
        in_specs=(
            P(None, None, "hid", "slot"),
            P(None, None, "hid", "slot"),
            P(None, None, "hid", "slot"),
            P("slot", None, "hid", None),
            P("slot", None, None),
            P("slot", None, None),
            P("slot", None),
            P("slot", None),
            P(),
            P(),
            P("slot", "hid"),
            P("slot", None),
        ),
        out_specs=(
            P("slot", "hid"),
            P(None, None, "hid", "slot"),
            P(None, None, "hid", "slot"),
            P(None, None, "hid", "slot"),
        ),
        check_vma=False,
    )
```

profile of v0, /device:TPU:1, one launch (start us, length us, event | category | flops | bytes accessed | tf_op | source)
XLA Modules:
  0.0 364.6 jit_solution(15891182138285590733)
XLA Ops:
  7.2 4.1 %fusion.16 = f32[1024,192]{0,1:T(8,128)S(1)} fusion(bf16[1,1024,2048]{2,1,0:T(8,128)(2,1)} %param.16, bf16[1,3,192,2048]{3,2,1,0:T(8,128)(2,1)} %param.15), kind=kOutput, calls=%fused_computation.17 | convolution fusion | flops 805306368 | bytes 5767168 | tf_op jit(solution)/shard_map/dot_general | solution.py:20
  11.6 2.5 multiply_convert_fusion.2
  14.1 1.4 fusion.2
  15.5 9.3 %psum.21 = f32[1024]{0:T(1024)S(1)} all-reduce(f32[1024]{0:T(1024)S(1)} %fusion.2), channel_id=1, replica_groups=mesh['slot'=32,'hid'=4] {'hid'}, use_global_device_ids=true, to_apply=%region_4.5 | all-reduce | flops 1024 | bytes 8192 | tf_op jit(solution)/shard_map/psum | solution.py:81
  25.4 66.9 %psum.22 = f32[]{:T(128)} all-reduce(f32[]{:T(128)} %get-tuple-element.19), channel_id=1, replica_groups=mesh['slot'=32,'hid'=4] {'slot'}, use_global_device_ids=true, to_apply=%region_6.7 | all-reduce | flops 1 | bytes 8 | tf_op jit(solution)/shard_map/psum | solution.py:84
  93.0 4.0 %fusion.6 = f32[1024,192]{0,1:T(8,128)S(1)} fusion(bf16[1,1024,2048]{2,1,0:T(8,128)(2,1)} %param.17, f32[1024]{0:T(1024)S(1)} %fusion.71, bf16[1,3,192,2048]{3,2,1,0:T(8,128)(2,1)S(1)} %copy-done.13), kind=kOutput, calls=%fused_computation.9 | convolution fusion | flops 811597824 | bytes 5771264 | tf_op jit(solution)/shard_map/dot_general | solution.py:35
  101.7 2.0 copy.33
  103.8 45.2 %all_to_all.40 = bf16[1,3,192,2048]{3,1,0,2:T(4,128)(2,1)S(1)} all-to-all(bf16[1,3,192,2048]{3,1,0,2:T(4,128)(2,1)S(1)} %copy.33), channel_id=1, replica_groups=mesh['slot'=32,'hid'=4] {'slot'}, dimensions={2} | all-to-all | bytes 4718592 | tf_op jit(solution)/shard_map/all_to_all | solution.py:87
  148.9 1.7 copy.55
  150.7 4.5 %reshape.144 = bf16[32,3,12288]{2,0,1:T(8,128)(2,1)} reshape(bf16[32,1,3,6,2048]{4,3,0,2,1:T(8,128)(2,1)S(1)} %bitcast.131) | data formatting | bytes 4718592 | tf_op jit(solution)/shard_map/reshape.20
  155.2 11.4 %multiply_subtract_fusion = (f32[16,3,1,12288]{3,0,1,2:T(8,128)S(1)}, f32[16,3,1,12288]{3,0,1,2:T(8,128)}, f32[16,3,1,12288]{3,0,1,2:T(8,128)}) fusion(f32[16,3,1,12288]{3,2,1,0:T(1,128)} %param.12, f32[16,3,1,12288]{3,2,1,0:T(1,128)} %param.13, f32[16,3,1,12288]{3,2,1,0:T(1,128)} %param.14, bf16[32,3,12288]{2,0,1:T(8,128)(2,1)} %reshape.144, ...), kind=kOutput, calls=%fused_computation.36 | convolution fusion | flops 46596608 | bytes 16515200 | tf_op jit(solution)/shard_map/es,sabc->eabc/dot_general | solution.py:94
  166.5 1.4 copy-done
  167.9 2.2 convolution_convert_fusion
  170.2 5.0 %reshape.146 = bf16[32,3,6,2048]{3,2,0,1:T(8,128)(2,1)S(1)} reshape(bf16[32,3,12288]{2,0,1:T(8,128)(2,1)} %convolution_convert_fusion) | data formatting | bytes 4718592 | tf_op jit(solution)/shard_map/reshape | solution.py:103
  175.1 1.9 copy.38
  177.0 4.0 %all-to-all-start.2 = ((bf16[32,3,6,2048]{3,2,1,0:T(8,128)(2,1)}), bf16[32,3,6,2048]{3,2,1,0:T(8,128)(2,1)S(1)}, u32[]{:S(2)}, u32[]{:S(2)}) async-start(bf16[32,3,6,2048]{3,2,1,0:T(8,128)(2,1)} %copy.38), calls=%async_computation.2 | async-start | bytes 6291456 | tf_op jit(solution)/shard_map/all_to_all | solution.py:104
  182.8 21.8 %all-gather.2.cloned.1.call-done = bf16[256,2048]{1,0:T(8,128)(2,1)} async-done(((bf16[256,512]{1,0:T(8,128)(2,1)}), bf16[256,2048]{1,0:T(8,128)(2,1)}) %all-gather.2.cloned.1.call-update) | async-done | bytes 1048592 | tf_op jit(solution)/shard_map/all_gather | solution.py:117
  204.6 3.3 convolution_convert_fusion.1
  207.9 13.0 %all-to-all-done.2 = bf16[32,3,6,2048]{3,2,1,0:T(8,128)(2,1)S(1)} async-done(((bf16[32,3,6,2048]{3,2,1,0:T(8,128)(2,1)}), bf16[32,3,6,2048]{3,2,1,0:T(8,128)(2,1)S(1)}, u32[]{:S(2)}, u32[]{:S(2)}) %all-to-all-start.2) | async-done | bytes 2359328 | tf_op jit(solution)/shard_map/all_to_all | solution.py:104
  220.8 5.3 %all-to-all-start = ((bf16[32,16,2048]{2,1,0:T(8,128)(2,1)}), bf16[32,16,2048]{2,1,0:T(8,128)(2,1)}, u32[]{:S(2)}, u32[]{:S(2)}) async-start(bf16[32,16,2048]{2,1,0:T(8,128)(2,1)} %bitcast.132), calls=%async_computation | async-start | bytes 4194304 | tf_op jit(solution)/shard_map/all_to_all | solution.py:122
  226.1 1.8 fusion.79
  227.9 1.5 squeeze.38
  229.4 1.4 squeeze.39
  231.0 23.5 %all-to-all-done = bf16[32,16,2048]{2,1,0:T(8,128)(2,1)} async-done(((bf16[32,16,2048]{2,1,0:T(8,128)(2,1)}), bf16[32,16,2048]{2,1,0:T(8,128)(2,1)}, u32[]{:S(2)}, u32[]{:S(2)}) %all-to-all-start) | async-done | bytes 2097184 | tf_op jit(solution)/shard_map/all_to_all | solution.py:122
  254.6 2.4 fusion.80
  257.0 5.1 %fusion.43 = f32[512,2048]{1,0:T(8,128)} fusion(bf16[192,2048]{1,0:T(8,128)(2,1)S(1)} %squeeze.40, bf16[512,2048]{1,0:T(8,128)(2,1)} %bitcast.4, bf16[192,2048]{1,0:T(8,128)(2,1)S(1)} %squeeze.39, f32[512,192]{0,1:T(8,128)S(1)} %fusion.80), kind=kOutput, calls=%fused_computation.42 | convolution fusion | flops 805896192 | bytes 8257536 | tf_op jit(solution)/shard_map/dot_general | solution.py:23
  262.1 75.4 %all-reduce.1 = bf16[512,2048]{1,0:T(8,128)(2,1)} all-reduce(f32[512,2048]{1,0:T(8,128)} %fusion.43), channel_id=1, replica_groups=mesh['slot'=32,'hid'=4] {'hid'}, use_global_device_ids=true, to_apply=%region_7.8 | all-reduce | flops 1048576 | bytes 6291456 | tf_op jit(solution)/shard_map/psum | solution.py:126
  337.6 1.9 dynamic-slice_convert_fusion
  339.4 5.5 %all-to-all-start.3 = ((bf16[32,16,512]{2,1,0:T(8,128)(2,1)}), bf16[32,16,512]{2,1,0:T(8,128)(2,1)S(1)}, u32[]{:S(2)}, u32[]{:S(2)}) async-start(bf16[32,16,512]{2,1,0:T(8,128)(2,1)} %bitcast.26), calls=%async_computation.3 | async-start | bytes 1048576 | tf_op jit(solution)/shard_map/all_to_all | solution.py:129
  345.0 3.8 %copy.39 = f32[16,3,1,12288]{3,2,1,0:T(1,128)} copy(f32[16,3,1,12288]{3,0,1,2:T(8,128)S(1)} %copy-done.1) | data formatting | bytes 4718592
  348.8 3.8 %copy.40 = f32[16,3,1,12288]{3,2,1,0:T(1,128)} copy(f32[16,3,1,12288]{3,0,1,2:T(8,128)S(1)} %copy-done.4) | data formatting | bytes 4718592
  352.7 3.8 %copy.41 = f32[16,3,1,12288]{3,2,1,0:T(1,128)} copy(f32[16,3,1,12288]{3,0,1,2:T(8,128)S(1)} %copy-done.3) | data formatting | bytes 4718592
  (50 shorter events, 8.9 us)
Async XLA Ops:
  7.2 4.1 %copy-start.11 = (bf16[1,1024,2048]{2,1,0:T(8,128)(2,1)S(1)}, bf16[1,1024,2048]{2,1,0:T(8,128)(2,1)}, u32[]{:S(2)}) copy-start(bf16[1,1024,2048]{2,1,0:T(8,128)(2,1)} %param.16) | copy-start | bytes 12582916
  7.2 4.4 %copy-start.13 = (bf16[1,3,192,2048]{3,2,1,0:T(8,128)(2,1)S(1)}, bf16[1,3,192,2048]{3,2,1,0:T(8,128)(2,1)}, u32[]{:S(2)}) copy-start(bf16[1,3,192,2048]{3,2,1,0:T(8,128)(2,1)} %param.15) | copy-start | bytes 7077892
  11.6 2.5 copy-start.9
  14.1 10.7 %copy-start.6 = (f32[1,1024]{1,0:T(1,128)S(1)}, f32[1,1024]{1,0:T(1,128)}, u32[]{:S(2)}) copy-start(f32[1,1024]{1,0:T(1,128)} %param.18) | copy-start | bytes 12292
  14.1 78.2 %copy-start.7 = (s32[1,1024]{1,0:T(1,128)S(1)}, s32[1,1024]{1,0:T(1,128)}, u32[]{:S(2)}) copy-start(s32[1,1024]{1,0:T(1,128)} %param.19) | copy-start | bytes 12292
  93.0 4.0 %copy-start.10 = (bf16[1,1024,2048]{2,1,0:T(8,128)(2,1)S(1)}, bf16[1,1024,2048]{2,1,0:T(8,128)(2,1)}, u32[]{:S(2)}) copy-start(bf16[1,1024,2048]{2,1,0:T(8,128)(2,1)} %param.17) | copy-start | bytes 12582916
  96.9 2.2 copy-start.12
  99.1 1.1 copy-start.15
  150.6 4.5 %copy-start.14 = (s32[32]{0:T(128)S(1)}, s32[32]{0:T(128)}, u32[]{:S(2)}) copy-start(s32[32]{0:T(128)} %param.20) | copy-start | bytes 388
  155.2 12.8 %copy-start.8 = (s32[32]{0:T(128)S(1)}, s32[32]{0:T(128)}, u32[]{:S(2)}) copy-start(s32[32]{0:T(128)} %param.21) | copy-start | bytes 388
  166.5 1.4 copy-start
  177.0 4.8 %copy-start.5 = (s32[256,1]{0,1:T(1,128)S(1)}, s32[256,1]{0,1:T(1,128)}, u32[]{:S(2)}) copy-start(s32[256,1]{0,1:T(1,128)} %param.23) | copy-start | bytes 3076
  177.0 43.8 %all-to-all-start.2 = ((bf16[32,3,6,2048]{3,2,1,0:T(8,128)(2,1)}), bf16[32,3,6,2048]{3,2,1,0:T(8,128)(2,1)S(1)}, u32[]{:S(2)}, u32[]{:S(2)}) async-start(bf16[32,3,6,2048]{3,2,1,0:T(8,128)(2,1)} %copy.38), calls=%async_computation.2 | async-start | bytes 6291456 | tf_op jit(solution)/shard_map/all_to_all | solution.py:104
  181.1 23.5 %all-gather.2.cloned.1.call-start = ((), (), s32[]{:S(2)}) async-start(), calls=%async_computation.4 | async-start | bytes 1310720 | tf_op jit(solution)/shard_map/all_gather | solution.py:117
  220.8 33.7 %all-to-all-start = ((bf16[32,16,2048]{2,1,0:T(8,128)(2,1)}), bf16[32,16,2048]{2,1,0:T(8,128)(2,1)}, u32[]{:S(2)}, u32[]{:S(2)}) async-start(bf16[32,16,2048]{2,1,0:T(8,128)(2,1)} %bitcast.132), calls=%async_computation | async-start | bytes 4194304 | tf_op jit(solution)/shard_map/all_to_all | solution.py:122
  227.9 2.9 copy-start.2
  262.1 82.8 %copy-start.1 = (f32[16,3,1,12288]{3,0,1,2:T(8,128)S(1)}, f32[16,3,1,12288]{3,0,1,2:T(8,128)}, u32[]{:S(2)}) copy-start(f32[16,3,1,12288]{3,0,1,2:T(8,128)} %copy-done) | copy-start | bytes 7077892
  339.4 17.2 %all-to-all-start.3 = ((bf16[32,16,512]{2,1,0:T(8,128)(2,1)}), bf16[32,16,512]{2,1,0:T(8,128)(2,1)S(1)}, u32[]{:S(2)}, u32[]{:S(2)}) async-start(bf16[32,16,512]{2,1,0:T(8,128)(2,1)} %bitcast.26), calls=%async_computation.3 | async-start | bytes 1048576 | tf_op jit(solution)/shard_map/all_to_all | solution.py:129
  345.0 3.8 %copy-start.4 = (f32[16,3,1,12288]{3,0,1,2:T(8,128)S(1)}, f32[16,3,1,12288]{3,0,1,2:T(8,128)}, u32[]{:S(2)}) copy-start(f32[16,3,1,12288]{3,0,1,2:T(8,128)} %get-tuple-element.17) | copy-start | bytes 7077892
  348.8 3.8 %copy-start.3 = (f32[16,3,1,12288]{3,0,1,2:T(8,128)S(1)}, f32[16,3,1,12288]{3,0,1,2:T(8,128)}, u32[]{:S(2)}) copy-start(f32[16,3,1,12288]{3,0,1,2:T(8,128)} %get-tuple-element.18) | copy-start | bytes 7077892
Sparse Core Ops, SparseCore 0:
  183.5 21.0 all-gather.1
where the time goes:
time: 365 us
  blocking collectives  197 us (54%)
  waiting for transfers between devices  59.2 us (16%)
  matrix products  40.8 us (11%)
  local copies, waits for them, and re-layouts  36.4 us (10%)
  starting transfers between devices  14.9 us (4%)
  between operations  14.9 us (4%)
    psum x1, blocking collectives, shards(): totals = lax.psum(fwd_partial, 'hid')  75.4 us
    psum x1, blocking collectives, shards(): center = lax.psum(jnp.sum(scores), 'slot') / row_total  66.9 us
    all_to_all x1, blocking collectives, shards(): lax.all_to_all(grads[None].astype(jnp.bfloat16), 'slot', split_axis=2, co...  45.2 us
    all_to_all x1, waiting for transfers between devices, shards(): lax.all_to_all(buffer_rows, 'slot', split_axis=0, concat_axis=0, tiled=True)  23.5 us
    all_gather x1, waiting for transfers between devices, shards(): widened = lax.all_gather(fwd_rows, 'hid', axis=1, tiled=True)  21.8 us
    unnamed x35, local copies, waits for them, and re-layouts  14.4 us
    all_to_all x1, waiting for transfers between devices, shards(): lax.all_to_all(picked, 'slot', split_axis=0, concat_axis=2, tiled=True)[0]  13 us
    dot_general x1, matrix products, shards(): jnp.einsum('es,sabc->eabc', owner_map, arrived, precision=lax.Precision.H...  11.4 us
  transfers between devices with their start and end apart: 4, of which 4 were waited for; matrix products, arithmetic and copies ran while one was open for 6% of the time, Pallas kernels for 0%

commit v1 on v0

v1 whole, which is shorter than its diff:
```python
import functools

import jax
import jax.numpy as jnp
from jax import lax
from jax.experimental import pallas as pl
from jax.experimental.pallas import tpu as pltpu
from jax.sharding import PartitionSpec as P

desired_weight = 1.0
undesired_weight = 1.33
learn_rate = 0.004
decay_first = 0.9
decay_second = 0.999
correct_first = 0.9999734386011124
correct_second = 0.09520785288629043
adam_eps = 1e-08
weight_decay = 0.1

BF = jnp.bfloat16
F32 = jnp.float32
NT = (((1,), (1,)), ((), ()))
LANES = 128


def dot(a, b, dims=(((1,), (0,)), ((), ()))):
    return lax.dot_general(a, b, dims, preferred_element_type=F32)


def swap_map(n):
    size = n * n
    row = lax.broadcasted_iota(jnp.int32, (size, size), 0)
    col = lax.broadcasted_iota(jnp.int32, (size, size), 1)
    hit = ((row % n) == (col // n)) & ((row // n) == (col % n))
    return jnp.where(hit, 1.0, 0.0).astype(BF)


def scores_kernel(x_ref, r_ref, w_ref, ref_ref, a_ref, b_ref, h_ref, part_ref):
    gate = dot(w_ref[0], x_ref[...], NT)
    up = dot(w_ref[1], x_ref[...], NT)
    dh = dot(w_ref[2], r_ref[...], NT)
    sigma = jax.nn.sigmoid(gate)
    hidden = (gate * sigma * up).astype(BF)
    h_ref[...] = hidden
    part_ref[...] = jnp.sum(hidden.astype(F32) * dh, axis=0, keepdims=True) - 0.25 * ref_ref[...]
    a_ref[...] = dh * up * sigma * (1.0 + gate * (1.0 - sigma))
    b_ref[...] = dh * gate * sigma


def scores_call(inputs, direction, weights, ref_logratio):
    rows, width = inputs.shape
    units = weights.shape[1]
    block = 256
    return pl.pallas_call(
        scores_kernel,
        grid=(rows // block,),
        in_specs=[
            pl.BlockSpec((block, width), lambda i: (i, 0)),
            pl.BlockSpec((block, width), lambda i: (i, 0)),
            pl.BlockSpec((3, units, width), lambda i: (0, 0, 0)),
            pl.BlockSpec((1, block), lambda i: (0, i)),
        ],
        out_specs=[
            pl.BlockSpec((units, block), lambda i: (0, i)),
            pl.BlockSpec((units, block), lambda i: (0, i)),
            pl.BlockSpec((units, block), lambda i: (0, i)),
            pl.BlockSpec((1, block), lambda i: (0, i)),
        ],
        out_shape=[
            jax.ShapeDtypeStruct((units, rows), F32),
            jax.ShapeDtypeStruct((units, rows), F32),
            jax.ShapeDtypeStruct((units, rows), BF),
            jax.ShapeDtypeStruct((1, rows), F32),
        ],
        cost_estimate=pl.CostEstimate(
            flops=6 * rows * width * units, bytes_accessed=14 << 20, transcendentals=rows * units
        ),
        name="scores",
    )(inputs, direction, weights, ref_logratio)


def grads_kernel(count, own_ref, parts_ref, lab_ref, *refs):
    terms = refs[:count]
    m_ref = refs[count]
    outs = refs[count + 1 : 2 * count + 1]
    lhs, held = refs[2 * count + 1 :]
    step = pl.program_id(0)
    units, rows = terms[0].shape
    wide = m_ref.shape[1]
    row_total = parts_ref.shape[0] // 4 * rows

    @pl.when(step == 0)
    def _():
        center = jnp.sum(parts_ref[...]) / row_total
        scores = jnp.sum(parts_ref[pl.ds(own_ref[0] * 4, 4)], axis=0)
        q = jax.nn.sigmoid(scores - center)
        slope = q * (1.0 - q) * jnp.where(lab_ref[...] == 1, -desired_weight, undesired_weight)
        for k in range(count):
            for i in range(rows // LANES):
                cols = slice(i * LANES, (i + 1) * LANES)
                lhs[k * units : (k + 1) * units, cols] = (
                    terms[k][:, cols].astype(F32) * slope[i : i + 1]
                ).astype(BF)

    held[:, pl.ds(pl.multiple_of(step * wide, wide), wide)] = dot(lhs[...], m_ref[...]).astype(BF)

    @pl.when(step == pl.num_programs(0) - 1)
    def _():
        swap = swap_map(16)
        for k in range(count):
            for pair in range(units // 32):
                halves = []
                for half in range(2):
                    base = k * units + (2 * pair + half) * 16
                    halves.append(
                        jnp.concatenate(
                            [
                                held[base : base + 16, j * LANES : (j + 1) * LANES]
                                for j in range(16)
                            ],
                            axis=0,
                        )
                    )
                both = dot(swap, jnp.concatenate(halves, axis=1)).astype(BF)
                outs[k][pair * 512 : pair * 512 + 256] = both[:, :LANES]
                outs[k][pair * 512 + 256 : pair * 512 + 512] = both[:, LANES:]


def grads_call(own, parts, labels, terms, right):
    count = len(terms)
    units, rows = terms[0].shape
    width = right.shape[1]
    wide = 512
    whole = lambda shape: pl.BlockSpec(shape, lambda i: (0,) * len(shape))
    return pl.pallas_call(
        functools.partial(grads_kernel, count),
        grid=(width // wide,),
        in_specs=[
            pl.BlockSpec(memory_space=pltpu.SMEM),
            whole(parts.shape),
            whole(labels.shape),
            *[whole(t.shape) for t in terms],
            pl.BlockSpec((rows, wide), lambda i: (0, i)),
        ],
        out_specs=[whole((units * 16, LANES))] * count,
        out_shape=[jax.ShapeDtypeStruct((units * 16, LANES), BF)] * count,
        scratch_shapes=[
            pltpu.VMEM((count * units, rows), BF),
            pltpu.VMEM((count * units, width), BF),
        ],
        cost_estimate=pl.CostEstimate(
            flops=2 * count * rows * width * units, bytes_accessed=6 << 20, transcendentals=rows
        ),
        name="grads%d" % count,
    )(own, parts, labels, *terms, right)


def adam_kernel(pc_ref, pn_ref, arr_ref, ms_ref, m1_ref, m2_ref, *refs):
    om_ref, o1_ref, o2_ref, pick_ref, total, fresh = refs[-6:]
    total[...] = jnp.zeros_like(total)
    for s in range(arr_ref.shape[0]):
        total[pc_ref[s]] += arr_ref[s].astype(F32)
    for e in range(total.shape[0]):
        grad = total[e]
        master = ms_ref[e, 0]
        new_first = decay_first * m1_ref[e, 0] + (1.0 - decay_first) * grad
        new_second = decay_second * m2_ref[e, 0] + (1.0 - decay_second) * grad * grad
        update = new_first / correct_first / (jnp.sqrt(new_second / correct_second) + adam_eps)
        new_master = master - learn_rate * (update + weight_decay * master)
        om_ref[e, 0] = new_master
        o1_ref[e, 0] = new_first
        o2_ref[e, 0] = new_second
        fresh[e] = new_master.astype(BF)
    for t in range(pick_ref.shape[0]):
        pick_ref[t] = fresh[pn_ref[t]]


def adam_call(which, place_cur, place_next, arrived, states, held):
    slots, lines, _ = arrived.shape
    experts = states[0].shape[0]
    block = 32
    state = pl.BlockSpec((experts, 1, block, LANES), lambda i: (0, which, i, 0))
    piece = pl.BlockSpec((slots, block, LANES), lambda i: (0, i, 0))
    smem = pl.BlockSpec(memory_space=pltpu.SMEM)
    extra = [] if held is None else list(held)
    return pl.pallas_call(
        adam_kernel,
        grid=(lines // block,),
        in_specs=[smem, smem, piece, state, state, state]
        + [pl.BlockSpec(memory_space=pl.ANY)] * len(extra),
        out_specs=[state, state, state, piece],
        out_shape=[jax.ShapeDtypeStruct(s.shape, F32) for s in states]
        + [jax.ShapeDtypeStruct(arrived.shape, BF)],
        scratch_shapes=[
            pltpu.VMEM((experts, block, LANES), F32),
            pltpu.VMEM((experts, block, LANES), BF),
        ],
        input_output_aliases={6 + i: i for i in range(len(extra))},
        cost_estimate=pl.CostEstimate(
            flops=20 * experts * lines * LANES, bytes_accessed=6 << 20, transcendentals=0
        ),
        name="adam%d" % which,
    )(place_cur, place_next, arrived, *states, *extra)


def to_matrix(src_ref, dst_ref):
    swap = swap_map(16)
    for pair in range(dst_ref.shape[0] // 32):
        base = pair * 512
        both = jnp.concatenate(
            [src_ref[base : base + 256], src_ref[base + 256 : base + 512]], axis=1
        )
        turned = dot(swap, both).astype(BF)
        for half in range(2):
            top = pair * 32 + half * 16
            for j in range(16):
                dst_ref[top : top + 16, j * LANES : (j + 1) * LANES] = turned[
                    j * 16 : (j + 1) * 16, half * LANES : (half + 1) * LANES
                ]


def project(q_ref, rows, mat):
    quarter = rows[0].shape[1]
    total = None
    for k in range(4):
        start = pl.multiple_of(q_ref[k] * quarter, quarter)
        term = dot(rows[k][...], mat[:, pl.ds(start, quarter)], NT)
        total = term if total is None else total + term
    return total


def gate_kernel(q_ref, w_ref, r0, r1, r2, r3, out_ref, mat):
    to_matrix(w_ref, mat)
    out_ref[...] = project(q_ref, (r0, r1, r2, r3), mat)


def up_kernel(q_ref, w_ref, r0, r1, r2, r3, gate_ref, out_ref, mat):
    to_matrix(w_ref, mat)
    up = project(q_ref, (r0, r1, r2, r3), mat)
    gate = gate_ref[...]
    out_ref[...] = (gate * jax.nn.sigmoid(gate) * up).astype(BF)


def project_call(quarters, packed, rows, gate):
    units = packed.shape[0] // 16
    count = rows[0].shape[0]
    width = rows[0].shape[1] * 4
    vmem = pl.BlockSpec(memory_space=pltpu.VMEM)
    extra = [] if gate is None else [gate]
    return pl.pallas_call(
        gate_kernel if gate is None else up_kernel,
        in_specs=[pl.BlockSpec(memory_space=pltpu.SMEM)] + [vmem] * (5 + len(extra)),
        out_specs=vmem,
        out_shape=jax.ShapeDtypeStruct((count, units), F32 if gate is None else BF),
        scratch_shapes=[pltpu.VMEM((units, width), BF)],
        cost_estimate=pl.CostEstimate(
            flops=2 * count * width * units, bytes_accessed=4 << 20, transcendentals=0
        ),
        name="gate" if gate is None else "up",
    )(quarters, packed, *rows, *extra)


def down_kernel(w_ref, hidden_ref, out_ref, mat):
    to_matrix(w_ref, mat)
    quarter = out_ref.shape[2]
    for k in range(4):
        out_ref[k] = dot(hidden_ref[...], mat[:, k * quarter : (k + 1) * quarter]).astype(BF)


def down_call(packed, hidden):
    count, units = hidden.shape
    width = 16 * LANES
    vmem = pl.BlockSpec(memory_space=pltpu.VMEM)
    return pl.pallas_call(
        down_kernel,
        in_specs=[vmem, vmem],
        out_specs=vmem,
        out_shape=jax.ShapeDtypeStruct((4, count, width // 4), BF),
        scratch_shapes=[pltpu.VMEM((units, width), BF)],
        cost_estimate=pl.CostEstimate(
            flops=2 * count * width * units, bytes_accessed=4 << 20, transcendentals=0
        ),
        name="down",
    )(packed, hidden)


def shards(
    master,
    first_moment,
    second_moment,
    slot_weights,
    back_rows,
    readout,
    ref_logratio,
    labels,
    place_cur,
    place_next,
    fwd_rows,
    routes,
):
    slot_count = lax.axis_size("slot")
    hid_count = lax.axis_size("hid")
    everyone = slot_count * hid_count
    slot_index = lax.axis_index("slot").astype(jnp.int32)
    hid_index = lax.axis_index("hid").astype(jnp.int32)
    rows = back_rows.shape[1]
    term_gate, term_up, hidden, part = scores_call(
        back_rows[0], readout[0], slot_weights[0], ref_logratio
    )
    part = jnp.broadcast_to(part.reshape(1, rows // LANES, LANES), (everyone, rows // LANES, LANES))
    parts = lax.all_to_all(part, ("slot", "hid"), split_axis=0, concat_axis=0, tiled=True)

    capacity = 2 * fwd_rows.shape[0] // slot_count
    quarter = fwd_rows.shape[1]
    target = routes[:, 0]
    target_map = (target[:, None] == jnp.arange(slot_count, dtype=jnp.int32)[None, :]).astype(BF)
    order = jnp.arange(fwd_rows.shape[0], dtype=jnp.int32)
    below = (order[:, None] > order[None, :]).astype(BF)
    earlier = jnp.dot(below, target_map, preferred_element_type=F32)
    position = jnp.sum(earlier * target_map.astype(F32), axis=1).astype(jnp.int32)
    slot_place = target * capacity + position
    place_map = (
        slot_place[None, :] == jnp.arange(slot_count * capacity, dtype=jnp.int32)[:, None]
    ).astype(BF)
    sent_rows = jnp.dot(place_map, fwd_rows, preferred_element_type=F32).astype(BF)
    sent_rows = sent_rows.reshape(slot_count, capacity, quarter)
    own_rows = lax.all_to_all(
        sent_rows, "slot", split_axis=0, concat_axis=0, tiled=True
    ).reshape(slot_count * capacity, quarter)
    pieces = [own_rows] + [
        lax.ppermute(own_rows, "hid", [(i, (i + k) % hid_count) for i in range(hid_count)])
        for k in range(1, hid_count)
    ]
    quarters = (hid_index - jnp.arange(hid_count, dtype=jnp.int32)) % hid_count

    own = slot_index.reshape(1)
    marks = labels.reshape(rows // LANES, LANES)
    (grad_down,) = grads_call(own, parts, marks, [hidden], readout[0])
    grad_gate, grad_up = grads_call(own, parts, marks, [term_gate, term_up], back_rows[0])
    lines = grad_down.shape[0] // slot_count

    def exchange(values):
        return lax.all_to_all(
            values.reshape(slot_count, lines, LANES), "slot", split_axis=0, concat_axis=0, tiled=True
        )

    got = {2: exchange(grad_down), 0: exchange(grad_gate), 1: exchange(grad_up)}
    shape = (master.shape[0], 3, lines, LANES)
    states = [v.reshape(shape) for v in (master, first_moment, second_moment)]
    held, picked = None, {}
    for which in (2, 0, 1):
        *held, picked[which] = adam_call(
            which, place_cur, place_next, got[which], states, held
        )
    weights = {k: exchange(picked[k]).reshape(slot_count * lines, LANES) for k in (0, 1, 2)}

    gate = project_call(quarters, weights[0], pieces, None)
    fwd_hidden = project_call(quarters, weights[1], pieces, gate)
    partial = down_call(weights[2], fwd_hidden)
    shares = lax.all_to_all(partial, "hid", split_axis=0, concat_axis=0, tiled=True)
    total = jnp.sum(shares.astype(F32), axis=0).astype(BF)
    returned = lax.all_to_all(
        total.reshape(slot_count, capacity, quarter), "slot", split_axis=0, concat_axis=0, tiled=True
    ).reshape(slot_count * capacity, quarter)
    out_rows = lax.dot_general(
        place_map, returned, (((0,), (0,)), ((), ())), preferred_element_type=F32
    ).astype(BF)
    return (out_rows, *[v.reshape(master.shape) for v in held])


def solution(mesh):
    shard = P(None, None, "hid", "slot")
    return jax.shard_map(
        shards,
        mesh=mesh,
        in_specs=(
            shard,
            shard,
            shard,
            P("slot", None, "hid", None),
            P("slot", None, None),
            P("slot", None, None),
            P("slot", None),
            P("slot", None),
            P(),
            P(),
            P("slot", "hid"),
            P("slot", None),
        ),
        out_specs=(P("slot", "hid"), shard, shard, shard),
        check_vma=False,
    )
```

time: 365 us -> 252 us (0.69)
  blocking collectives: 197 us -> 108 us
  Pallas kernels: 0 us -> 47.9 us
  matrix products: 40.8 us -> 2.39 us
  local copies, waits for them, and re-layouts: 36.4 us -> 4.02 us
  starting transfers between devices: 14.9 us -> 29.7 us
  between operations: 14.9 us -> 0.76 us
    psum x3 -> x0, blocking collectives: 152 us -> none  [the longest x1 75.4 us: shards(): totals = lax.psum(fwd_partial, 'hid')]
    all_to_all x1 -> x5, blocking collectives: 45.2 us -> 108 us  [the longest x3 58.2 us: exchange(): lax.all_to_all(values.reshape(slot_count, lines, LANES), 'slot', split_ax...]
    pallas_call x0 -> x9, Pallas kernels: none -> 47.9 us  [the longest x3 14.9 us: adam_call(): pl.pallas_call(adam_kernel, grid=(lines // block,), in_specs=[smem, smem,...]
    dot_general x12 -> x2, matrix products: 39.7 us -> 1.33 us  [the longest x1 1.13 us: shards(): jnp.dot(place_map, fwd_rows, preferred_element_type=F32).astype(BF)]
    ppermute x0 -> x3, waiting for transfers between devices: none -> 22.7 us  [shards(): lax.ppermute(own_rows, 'hid', [(i, (i + k) % hid_count) for i in range(hi...]
    all_gather x1 -> x0, waiting for transfers between devices: 21.8 us -> none  [shards(): widened = lax.all_gather(fwd_rows, 'hid', axis=1, tiled=True)]
    all_to_all x3 -> x5, starting transfers between devices: 14.8 us -> 26.8 us  [the longest x3 11.5 us: exchange(): lax.all_to_all(values.reshape(slot_count, lines, LANES), 'slot', split_ax...]
    unnamed x35 -> x22, local copies, waits for them, and re-layouts: 14.4 us -> 2.51 us
  transfers between devices with their start and end apart: 4 -> 8, of which waited for: 4 -> 6; matrix products, arithmetic and copies ran while one was open for 6% -> 1% of each run, Pallas kernels for 0% -> 12%
where the time goes in v1:
time: 252 us; the launch traced here: 251 us
  blocking collectives  108 us (43%)
  waiting for transfers between devices  56.7 us (22%)
  Pallas kernels  47.9 us (19%)
  starting transfers between devices  29.7 us (12%)
  local copies, waits for them, and re-layouts  4.02 us (2%)
    all_to_all x3, blocking collectives, exchange(): lax.all_to_all(values.reshape(slot_count, lines, LANES), 'slot', split_ax...  58.2 us
    all_to_all x1, blocking collectives, shards(): lax.all_to_all(partial, 'hid', split_axis=0, concat_axis=0, tiled=True)  29.7 us
    ppermute x3, waiting for transfers between devices, shards(): lax.ppermute(own_rows, 'hid', [(i, (i + k) % hid_count) for i in range(hi...  22.7 us
    all_to_all x1, blocking collectives, shards(): lax.all_to_all(total.reshape(slot_count, capacity, quarter), 'slot', spli...  20.3 us
    all_to_all x3, waiting for transfers between devices, exchange(): lax.all_to_all(values.reshape(slot_count, lines, LANES), 'slot', split_ax...  20 us
    pallas_call x3, Pallas kernels, adam_call(): pl.pallas_call(adam_kernel, grid=(lines // block,), in_specs=[smem, smem,...  14.9 us
    all_to_all x1, waiting for transfers between devices, shards(): lax.all_to_all(part, ('slot', 'hid'), split_axis=0, concat_axis=0, tiled=...  14.1 us
    pallas_call x2, Pallas kernels, grads_call(): pl.pallas_call(functools.partial(grads_kernel, count), grid=(width // wid...  12.8 us
  transfers between devices with their start and end apart: 8, of which 6 were waited for; matrix products, arithmetic and copies ran while one was open for 1% of the time, Pallas kernels for 12%

profile of v1, /device:TPU:1, one launch (start us, length us, event | category | flops | bytes accessed | tf_op | source)
XLA Modules:
  0.0 250.8 jit_solution(3446709577824971261)
XLA Ops:
  0.6 9.3 %scores.1 = (f32[192,1024]{1,0:T(8,128)}, f32[192,1024]{1,0:T(8,128)}, bf16[192,1024]{1,0:T(8,128)(2,1)}, f32[1,1024]{1,0:T(1,128)}) custom-call(bf16[1024,2048]{1,0:T(8,128)(2,1)} %bitcast.36, bf16[1024,2048]{1,0:T(8,128)(2,1)} %bitcast.34, bf16[3,192,2048]{2,1,0:T(8,128)(2,1)} %bitcast.50, f32[1,1024]{1,0:T(1,128)} %ref_ref.1), custom_call_target="tpu_custom_call" | custom-call | flops 2415919104 | bytes 14680064 | tf_op jit(solution)/shard_map/scores/pallas_call | solution.py:54
  10.0 1.5 broadcast_in_dim.5
  11.5 11.5 %all-to-all-start = ((f32[128,8,128]{2,1,0:T(8,128)}), f32[128,8,128]{2,1,0:T(8,128)S(1)}, u32[]{:S(2)}, u32[]{:S(2)}) async-start(f32[128,8,128]{2,1,0:T(8,128)} %broadcast_in_dim.5), calls=%async_computation | async-start | bytes 1048576 | tf_op jit(solution)/shard_map/all_to_all | solution.py:311
  23.0 14.1 %all-to-all-done.parts_ref = f32[128,8,128]{2,1,0:T(8,128)S(1)} async-done(((f32[128,8,128]{2,1,0:T(8,128)}), f32[128,8,128]{2,1,0:T(8,128)S(1)}, u32[]{:S(2)}, u32[]{:S(2)}) %all-to-all-start) | async-done | bytes 524320 | tf_op jit(solution)/shard_map/all_to_all | solution.py:311
  37.1 0.8 copy-done.2
  37.9 5.6 %grads1.1 = bf16[3072,128]{1,0:T(8,128)(2,1)} custom-call(s32[1]{0:T(128)} %bitcast.1.own_ref, f32[128,8,128]{2,1,0:T(8,128)} %copy-done.2, s32[8,128]{1,0:T(8,128)} %bitcast.55, bf16[192,1024]{1,0:T(8,128)(2,1)} %get-tuple-element.23.refs_0_, bf16[1024,2048]{1,0:T(8,128)(2,1)} %bitcast.35), custom_call_target="tpu_custom_call" | custom-call | flops 805306368 | bytes 6291456 | tf_op jit(solution)/shard_map/grads1/pallas_call | solution.py:135
  43.5 3.9 %all-to-all-start.1 = ((bf16[32,96,128]{2,1,0:T(8,128)(2,1)}), bf16[32,96,128]{2,1,0:T(8,128)(2,1)S(1)}, u32[]{:S(2)}, u32[]{:S(2)}) async-start(bf16[32,96,128]{2,1,0:T(8,128)(2,1)} %bitcast.49), calls=%async_computation.1 | async-start | bytes 1572864 | tf_op jit(solution)/shard_map/all_to_all | solution.py:343
  47.5 7.1 %grads2.1 = (bf16[3072,128]{1,0:T(8,128)(2,1)}, bf16[3072,128]{1,0:T(8,128)(2,1)}) custom-call(s32[1]{0:T(128)} %bitcast.1.own_ref, f32[128,8,128]{2,1,0:T(8,128)} %copy-done.2, s32[8,128]{1,0:T(8,128)} %bitcast.56, f32[192,1024]{1,0:T(8,128)} %get-tuple-element.25.refs_0_, f32[192,1024]{1,0:T(8,128)} %get-tuple-element.26.refs_1_, bf16[1024,2048]{1,0:T(8,128)(2,1)} %bitcast.37), custom_call_target="tpu_custom_call" | custom-call | flops 1610612736 | bytes 6291456 | tf_op jit(solution)/shard_map/grads2/pallas_call | solution.py:135
  54.6 7.1 %all-to-all-done.1.arr_ref = bf16[32,96,128]{2,1,0:T(8,128)(2,1)S(1)} async-done(((bf16[32,96,128]{2,1,0:T(8,128)(2,1)}), bf16[32,96,128]{2,1,0:T(8,128)(2,1)S(1)}, u32[]{:S(2)}, u32[]{:S(2)}) %all-to-all-start.1) | async-done | bytes 786464 | tf_op jit(solution)/shard_map/all_to_all | solution.py:343
  61.7 18.5 %all_to_all.50.arr_ref = bf16[32,96,128]{2,1,0:T(8,128)(2,1)} all-to-all(bf16[32,96,128]{2,1,0:T(8,128)(2,1)} %bitcast.53), channel_id=1, replica_groups=mesh['slot'=32,'hid'=4] {'slot'}, dimensions={0} | all-to-all | bytes 1572864 | tf_op jit(solution)/shard_map/all_to_all | solution.py:343
  80.2 3.8 %all-to-all-start.4 = ((bf16[32,96,128]{2,1,0:T(8,128)(2,1)}), bf16[32,96,128]{2,1,0:T(8,128)(2,1)S(1)}, u32[]{:S(2)}, u32[]{:S(2)}) async-start(bf16[32,96,128]{2,1,0:T(8,128)(2,1)} %bitcast.52), calls=%async_computation.4 | async-start | bytes 1572864 | tf_op jit(solution)/shard_map/all_to_all | solution.py:343
  84.2 1.1 convolution_convert_fusion
  85.3 12.9 %all-to-all-done.4.arr_ref = bf16[32,96,128]{2,1,0:T(8,128)(2,1)S(1)} async-done(((bf16[32,96,128]{2,1,0:T(8,128)(2,1)}), bf16[32,96,128]{2,1,0:T(8,128)(2,1)S(1)}, u32[]{:S(2)}, u32[]{:S(2)}) %all-to-all-start.4) | async-done | bytes 786464 | tf_op jit(solution)/shard_map/all_to_all | solution.py:343
  98.2 3.8 %all-to-all-start.6 = ((bf16[32,16,512]{2,1,0:T(8,128)(2,1)}), bf16[32,16,512]{2,1,0:T(8,128)(2,1)S(1)}, u32[]{:S(2)}, u32[]{:S(2)}) async-start(bf16[32,16,512]{2,1,0:T(8,128)(2,1)} %bitcast.15), calls=%async_computation.6 | async-start | bytes 1048576 | tf_op jit(solution)/shard_map/all_to_all | solution.py:327
  102.0 5.0 %adam2.1 = (f32[16,3,96,128]{3,2,1,0:T(8,128)}, f32[16,3,96,128]{3,2,1,0:T(8,128)}, f32[16,3,96,128]{3,2,1,0:T(8,128)}, bf16[32,96,128]{2,1,0:T(8,128)(2,1)}) custom-call(s32[32]{0:T(128)} %pc_ref.5, s32[32]{0:T(128)} %pn_ref.5, bf16[32,96,128]{2,1,0:T(8,128)(2,1)} %copy-done.3, f32[16,3,96,128]{3,2,1,0:T(8,128)} %bitcast.25, f32[16,3,96,128]{3,2,1,0:T(8,128)} %bitcast.28, ...), custom_call_target="tpu_custom_call" | custom-call | flops 3932160 | bytes 6291456 | tf_op jit(solution)/shard_map/adam2/pallas_call | solution.py:186
  107.0 5.0 %adam0.1 = (f32[16,3,96,128]{3,2,1,0:T(8,128)}, f32[16,3,96,128]{3,2,1,0:T(8,128)}, f32[16,3,96,128]{3,2,1,0:T(8,128)}, bf16[32,96,128]{2,1,0:T(8,128)(2,1)}) custom-call(s32[32]{0:T(128)} %pc_ref.5, s32[32]{0:T(128)} %pn_ref.5, bf16[32,96,128]{2,1,0:T(8,128)(2,1)} %copy-done.5, ...), custom_call_target="tpu_custom_call", output_to_operand_aliasing={{0}: (6, {}), {1}: (7, {}), {2}: (8, {})} | custom-call | flops 3932160 | bytes 6291456 | tf_op jit(solution)/shard_map/adam0/pallas_call | solution.py:186
  111.9 5.0 %adam1.1 = (f32[16,3,96,128]{3,2,1,0:T(8,128)}, f32[16,3,96,128]{3,2,1,0:T(8,128)}, f32[16,3,96,128]{3,2,1,0:T(8,128)}, bf16[32,96,128]{2,1,0:T(8,128)(2,1)}) custom-call(s32[32]{0:T(128)} %pc_ref.5, s32[32]{0:T(128)} %pn_ref.5, bf16[32,96,128]{2,1,0:T(8,128)(2,1)} %all_to_all.50.arr_ref, ...), custom_call_target="tpu_custom_call", output_to_operand_aliasing={{0}: (6, {}), {1}: (7, {}), {2}: (8, {})} | custom-call | flops 3932160 | bytes 6291456 | tf_op jit(solution)/shard_map/adam1/pallas_call | solution.py:186
  117.0 21.7 %all_to_all.51 = bf16[32,96,128]{2,1,0:T(8,128)(2,1)} all-to-all(bf16[32,96,128]{2,1,0:T(8,128)(2,1)} %get-tuple-element.35), channel_id=1, replica_groups=mesh['slot'=32,'hid'=4] {'slot'}, dimensions={0} | all-to-all | bytes 1572864 | tf_op jit(solution)/shard_map/all_to_all | solution.py:343
  138.7 17.9 %all_to_all.52 = bf16[32,96,128]{2,1,0:T(8,128)(2,1)} all-to-all(bf16[32,96,128]{2,1,0:T(8,128)(2,1)S(1)} %copy-done.9), channel_id=1, replica_groups=mesh['slot'=32,'hid'=4] {'slot'}, dimensions={0} | all-to-all | bytes 1572864 | tf_op jit(solution)/shard_map/all_to_all | solution.py:343
  156.6 3.8 %all-to-all-start.2 = ((bf16[32,96,128]{2,1,0:T(8,128)(2,1)}), bf16[32,96,128]{2,1,0:T(8,128)(2,1)S(1)}, u32[]{:S(2)}, u32[]{:S(2)}) async-start(bf16[32,96,128]{2,1,0:T(8,128)(2,1)} %get-tuple-element.24), calls=%async_computation.2 | async-start | bytes 1572864 | tf_op jit(solution)/shard_map/all_to_all | solution.py:343
  160.8 2.1 collective-permute-start.1
  163.9 11.3 %collective-permute-done.r1 = bf16[512,512]{1,0:T(8,128)(2,1)S(1)} collective-permute-done((bf16[512,512]{1,0:T(8,128)(2,1)S(1)}, bf16[512,512]{1,0:T(8,128)(2,1)S(1)}, u32[]{:S(2)}, u32[]{:S(2)}) %collective-permute-start) | collective-permute-done | bytes 524320 | tf_op jit(solution)/shard_map/ppermute | solution.py:331
  175.2 10.8 %collective-permute-done.1.r2 = bf16[512,512]{1,0:T(8,128)(2,1)S(1)} collective-permute-done((bf16[512,512]{1,0:T(8,128)(2,1)S(1)}, bf16[512,512]{1,0:T(8,128)(2,1)S(1)}, u32[]{:S(2)}, u32[]{:S(2)}) %collective-permute-start.1) | collective-permute-done | bytes 524320 | tf_op jit(solution)/shard_map/ppermute | solution.py:331
  186.0 0.5 collective-permute-done.2.r3
  187.3 3.7 %gate.1.gate_ref = f32[512,192]{1,0:T(8,128)} custom-call(s32[4]{0:T(128)} %and_select_fusion.q_ref, bf16[3072,128]{1,0:T(8,128)(2,1)} %bitcast.47, bf16[512,512]{1,0:T(8,128)(2,1)} %bitcast.44, bf16[512,512]{1,0:T(8,128)(2,1)} %copy-done.6, bf16[512,512]{1,0:T(8,128)(2,1)} %copy-done.7, bf16[512,512]{1,0:T(8,128)(2,1)} %copy-done.8), custom_call_target="tpu_custom_call" | custom-call | flops 402653184 | bytes 4194304 | tf_op jit(solution)/shard_map/gate/pallas_call | solution.py:250
  191.0 3.7 %up.1.hidden_ref = bf16[512,192]{1,0:T(8,128)(2,1)} custom-call(s32[4]{0:T(128)} %and_select_fusion.q_ref, bf16[3072,128]{1,0:T(8,128)(2,1)} %bitcast.48, bf16[512,512]{1,0:T(8,128)(2,1)} %bitcast.45, bf16[512,512]{1,0:T(8,128)(2,1)} %copy-done.6, bf16[512,512]{1,0:T(8,128)(2,1)} %copy-done.7, bf16[512,512]{1,0:T(8,128)(2,1)} %copy-done.8, ...), custom_call_target="tpu_custom_call" | custom-call | flops 402653184 | bytes 4194304 | tf_op jit(solution)/shard_map/up/pallas_call | solution.py:250
  194.7 0.9 copy-done.4
  195.6 3.5 %down.1 = bf16[4,512,512]{2,1,0:T(8,128)(2,1)} custom-call(bf16[3072,128]{1,0:T(8,128)(2,1)} %bitcast.46, bf16[512,192]{1,0:T(8,128)(2,1)} %up.1.hidden_ref), custom_call_target="tpu_custom_call" | custom-call | flops 402653184 | bytes 4194304 | tf_op jit(solution)/shard_map/down/pallas_call | solution.py:274
  199.1 29.7 %all_to_all.53 = bf16[4,512,512]{2,1,0:T(8,128)(2,1)S(1)} all-to-all(bf16[4,512,512]{2,1,0:T(8,128)(2,1)} %down.1), channel_id=1, replica_groups=mesh['slot'=32,'hid'=4] {'hid'}, dimensions={0} | all-to-all | bytes 4194304 | tf_op jit(solution)/shard_map/all_to_all | solution.py:360
  228.8 0.6 reduce_sum.22
  229.5 20.3 %all_to_all.54 = bf16[32,16,512]{2,1,0:T(8,128)(2,1)S(1)} all-to-all(bf16[32,16,512]{2,1,0:T(8,128)(2,1)S(1)} %bitcast.51), channel_id=1, replica_groups=mesh['slot'=32,'hid'=4] {'slot'}, dimensions={0} | all-to-all | bytes 1048576 | tf_op jit(solution)/shard_map/all_to_all | solution.py:362
  249.7 1.1 convolution_convert_fusion.1
  (27 shorter events, 2.4 us)
Async XLA Ops:
  0.6 83.6 %copy-start = (bf16[256,512]{1,0:T(8,128)(2,1)S(1)}, bf16[256,512]{1,0:T(8,128)(2,1)}, u32[]{:S(2)}) copy-start(bf16[256,512]{1,0:T(8,128)(2,1)} %param.22) | copy-start | bytes 786436
  11.5 25.6 %all-to-all-start = ((f32[128,8,128]{2,1,0:T(8,128)}), f32[128,8,128]{2,1,0:T(8,128)S(1)}, u32[]{:S(2)}, u32[]{:S(2)}) async-start(f32[128,8,128]{2,1,0:T(8,128)} %broadcast_in_dim.5), calls=%async_computation | async-start | bytes 1048576 | tf_op jit(solution)/shard_map/all_to_all | solution.py:311
  37.1 0.8 copy-start.2
  43.5 18.2 %all-to-all-start.1 = ((bf16[32,96,128]{2,1,0:T(8,128)(2,1)}), bf16[32,96,128]{2,1,0:T(8,128)(2,1)S(1)}, u32[]{:S(2)}, u32[]{:S(2)}) async-start(bf16[32,96,128]{2,1,0:T(8,128)(2,1)} %bitcast.49), calls=%async_computation.1 | async-start | bytes 1572864 | tf_op jit(solution)/shard_map/all_to_all | solution.py:343
  54.6 29.4 %copy-start.10 = (s32[256,1]{0,1:T(1,128)S(1)}, s32[256,1]{0,1:T(1,128)}, u32[]{:S(2)}) copy-start(s32[256,1]{0,1:T(1,128)} %param.23) | copy-start | bytes 3076
  61.7 36.5 %copy-start.3 = (bf16[32,96,128]{2,1,0:T(8,128)(2,1)}, bf16[32,96,128]{2,1,0:T(8,128)(2,1)S(1)}, u32[]{:S(2)}) copy-start(bf16[32,96,128]{2,1,0:T(8,128)(2,1)S(1)} %all-to-all-done.1.arr_ref) | copy-start | bytes 2359300
  80.2 18.0 %all-to-all-start.4 = ((bf16[32,96,128]{2,1,0:T(8,128)(2,1)}), bf16[32,96,128]{2,1,0:T(8,128)(2,1)S(1)}, u32[]{:S(2)}, u32[]{:S(2)}) async-start(bf16[32,96,128]{2,1,0:T(8,128)(2,1)} %bitcast.52), calls=%async_computation.4 | async-start | bytes 1572864 | tf_op jit(solution)/shard_map/all_to_all | solution.py:343
  98.2 8.8 %copy-start.5 = (bf16[32,96,128]{2,1,0:T(8,128)(2,1)}, bf16[32,96,128]{2,1,0:T(8,128)(2,1)S(1)}, u32[]{:S(2)}) copy-start(bf16[32,96,128]{2,1,0:T(8,128)(2,1)S(1)} %all-to-all-done.4.arr_ref) | copy-start | bytes 2359300
  98.2 18.8 %all-to-all-start.6 = ((bf16[32,16,512]{2,1,0:T(8,128)(2,1)}), bf16[32,16,512]{2,1,0:T(8,128)(2,1)S(1)}, u32[]{:S(2)}, u32[]{:S(2)}) async-start(bf16[32,16,512]{2,1,0:T(8,128)(2,1)} %bitcast.15), calls=%async_computation.6 | async-start | bytes 1048576 | tf_op jit(solution)/shard_map/all_to_all | solution.py:327
  111.9 26.8 %copy-start.9 = (bf16[32,96,128]{2,1,0:T(8,128)(2,1)S(1)}, bf16[32,96,128]{2,1,0:T(8,128)(2,1)}, u32[]{:S(2)}) copy-start(bf16[32,96,128]{2,1,0:T(8,128)(2,1)} %get-tuple-element.36) | copy-start | bytes 2359300
  117.0 46.0 %copy-start.1 = (bf16[32,16,512]{2,1,0:T(8,128)(2,1)}, bf16[32,16,512]{2,1,0:T(8,128)(2,1)S(1)}, u32[]{:S(2)}) copy-start(bf16[32,16,512]{2,1,0:T(8,128)(2,1)S(1)} %all-to-all-done.6) | copy-start | bytes 1572868
  156.6 38.1 %all-to-all-start.2 = ((bf16[32,96,128]{2,1,0:T(8,128)(2,1)}), bf16[32,96,128]{2,1,0:T(8,128)(2,1)S(1)}, u32[]{:S(2)}, u32[]{:S(2)}) async-start(bf16[32,96,128]{2,1,0:T(8,128)(2,1)} %get-tuple-element.24), calls=%async_computation.2 | async-start | bytes 1572864 | tf_op jit(solution)/shard_map/all_to_all | solution.py:343
  160.4 14.8 %collective-permute-start = (bf16[512,512]{1,0:T(8,128)(2,1)S(1)}, bf16[512,512]{1,0:T(8,128)(2,1)S(1)}, u32[]{:S(2)}, u32[]{:S(2)}) collective-permute-start(bf16[512,512]{1,0:T(8,128)(2,1)S(1)} %bitcast.41), channel_id=1, source_target_pairs={{0,1},{1,2},{2,3},{3,0},{4,5},{5,6},{6,7},{7,4},{8,9},{9,10},{10,1... | collective-permute-start | bytes 1572872 | tf_op jit(solution)/shard_map/ppermute | solution.py:331
  160.8 25.2 %collective-permute-start.1 = (bf16[512,512]{1,0:T(8,128)(2,1)S(1)}, bf16[512,512]{1,0:T(8,128)(2,1)S(1)}, u32[]{:S(2)}, u32[]{:S(2)}) collective-permute-start(bf16[512,512]{1,0:T(8,128)(2,1)S(1)} %bitcast.42), channel_id=1, source_target_pairs={{0,2},{1,3},{2,0},{3,1},{4,6},{5,7},{6,4},{7,5},{8,10},{9,11},{10,... | collective-permute-start | bytes 1572872 | tf_op jit(solution)/shard_map/ppermute | solution.py:331
  162.9 23.6 %collective-permute-start.2 = (bf16[512,512]{1,0:T(8,128)(2,1)S(1)}, bf16[512,512]{1,0:T(8,128)(2,1)S(1)}, u32[]{:S(2)}, u32[]{:S(2)}) collective-permute-start(bf16[512,512]{1,0:T(8,128)(2,1)S(1)} %bitcast.43), channel_id=1, source_target_pairs={{0,3},{1,0},{2,1},{3,2},{4,7},{5,4},{6,5},{7,6},{8,11},{9,8},{10,9... | collective-permute-start | bytes 1572872 | tf_op jit(solution)/shard_map/ppermute | solution.py:331
  175.2 11.4 %copy-start.6 = (bf16[512,512]{1,0:T(8,128)(2,1)}, bf16[512,512]{1,0:T(8,128)(2,1)S(1)}, u32[]{:S(2)}) copy-start(bf16[512,512]{1,0:T(8,128)(2,1)S(1)} %collective-permute-done.r1) | copy-start | bytes 1572868
  186.0 0.8 copy-start.7
  186.5 0.8 copy-start.8
  194.7 0.9 copy-start.4

commit v2 on v0

v2 whole, which is shorter than its diff:
```python
import functools

import jax
import jax.numpy as jnp
from jax import lax
from jax.experimental import pallas as pl
from jax.experimental.pallas import tpu as pltpu
from jax.sharding import PartitionSpec as P

desired_weight = 1.0
undesired_weight = 1.33
learn_rate = 0.004
decay_first = 0.9
decay_second = 0.999
correct_first = 0.9999734386011124
correct_second = 0.09520785288629043
adam_eps = 1e-08
weight_decay = 0.1

BF = jnp.bfloat16
F32 = jnp.float32
NT = (((1,), (1,)), ((), ()))
TN = (((0,), (0,)), ((), ()))
LANES = 128


def dot(a, b, dims=(((1,), (0,)), ((), ()))):
    return lax.dot_general(a, b, dims, preferred_element_type=F32)


def swap_map(first, second, tail=1):
    size = first * second * tail
    row = lax.broadcasted_iota(jnp.int32, (size, size), 0)
    col = lax.broadcasted_iota(jnp.int32, (size, size), 1)
    b, a, t = row // (first * tail), row // tail % first, row % tail
    return jnp.where(col == (a * second + b) * tail + t, 1.0, 0.0).astype(BF)


def whole(shape):
    return pl.BlockSpec(shape, lambda *_: (0,) * len(shape))


def limits(mib):
    return pltpu.CompilerParams(vmem_limit_bytes=mib << 20)


def scores_kernel(x_ref, r_ref, w_ref, a_ref, b_ref, h_ref, part_ref):
    units = h_ref.shape[0]
    both = dot(w_ref[0 : 2 * units], x_ref[...], NT)
    dh = dot(w_ref[2 * units :], r_ref[...], NT)
    gate, up = both[:units], both[units:]
    sigma = jax.nn.sigmoid(gate)
    hidden = (gate * sigma * up).astype(BF)
    h_ref[...] = hidden
    part_ref[...] = jnp.sum(hidden.astype(F32) * dh, axis=0, keepdims=True)
    a_ref[...] = dh * up * sigma * (1.0 + gate * (1.0 - sigma))
    b_ref[...] = dh * gate * sigma


def scores_call(inputs, direction, weights):
    rows, width = inputs.shape
    units = weights.shape[0] // 3
    block = 256
    tall = pl.BlockSpec((units, block), lambda i: (0, i))
    return pl.pallas_call(
        scores_kernel,
        grid=(rows // block,),
        in_specs=[
            pl.BlockSpec((block, width), lambda i: (i, 0)),
            pl.BlockSpec((block, width), lambda i: (i, 0)),
            pl.BlockSpec((3 * units, width), lambda i: (0, 0), pipeline_mode=pl.Buffered(1)),
        ],
        out_specs=[tall, tall, tall, pl.BlockSpec((1, block), lambda i: (0, i))],
        out_shape=[
            jax.ShapeDtypeStruct((units, rows), F32),
            jax.ShapeDtypeStruct((units, rows), F32),
            jax.ShapeDtypeStruct((units, rows), BF),
            jax.ShapeDtypeStruct((1, rows), F32),
        ],
        cost_estimate=pl.CostEstimate(
            flops=6 * rows * width * units, bytes_accessed=14 << 20, transcendentals=rows * units
        ),
        compiler_params=limits(32),
        name="scores",
    )(inputs, direction, weights)


def grads_kernel(sums_ref, sco_ref, lab_ref, a_ref, b_ref, h_ref, rows_ref, r_ref, x_ref, out_ref, lhs, held):
    step = pl.program_id(0)
    last = pl.num_programs(0) // 2 - 1
    units, rows = a_ref.shape
    wide = x_ref.shape[1]
    slots = out_ref.shape[0]

    @pl.when(step == 0)
    def _():
        center = jnp.sum(sums_ref[...][:, 0, 0:1]) / (slots * rows)
        q = jax.nn.sigmoid(sco_ref[...] - center)
        slope = q * (1.0 - q) * jnp.where(lab_ref[...] == 1, -desired_weight, undesired_weight)
        for k, term in enumerate((h_ref, a_ref, b_ref)):
            for i in range(rows // LANES):
                cols = slice(i * LANES, (i + 1) * LANES)
                lhs[k * units : (k + 1) * units, cols] = (
                    term[:, cols].astype(F32) * slope[i : i + 1]
                ).astype(BF)
        capacity = rows_ref.shape[0] // slots
        for s in range(slots):
            for j in range(rows_ref.shape[1] // LANES):
                out_ref[s, 288 + j * capacity : 288 + (j + 1) * capacity] = rows_ref[
                    s * capacity : (s + 1) * capacity, j * LANES : (j + 1) * LANES
                ]

    @pl.when(step <= last)
    def _():
        cols = pl.ds(pl.multiple_of(step * wide, wide), wide)
        held[0:units, cols] = dot(lhs[0:units], r_ref[...]).astype(BF)

    @pl.when(step > last)
    def _():
        cols = pl.ds(pl.multiple_of((step - last - 1) * wide, wide), wide)
        held[units:, cols] = dot(lhs[units:], x_ref[...]).astype(BF)

    def spread(k, line):
        swap = swap_map(16, 16)
        for pair in range(units // 32):
            halves = []
            for half in range(2):
                base = k * units + (2 * pair + half) * 16
                tiles = [held[base : base + 16, j * LANES : (j + 1) * LANES] for j in range(16)]
                halves.append(jnp.concatenate(tiles, axis=0))
            both = dot(swap, jnp.concatenate(halves, axis=1)).astype(BF)
            for half in range(2):
                for p in range(8):
                    at = (2 * pair + half) * 256 + p * 32
                    top = line + at % 96
                    out_ref[at // 96, top : top + 32] = both[
                        p * 32 : (p + 1) * 32, half * LANES : (half + 1) * LANES
                    ]

    @pl.when(step == last)
    def _():
        spread(0, 192)

    @pl.when(step == 2 * last + 1)
    def _():
        spread(1, 0)
        spread(2, 96)


def grads_call(sums, scores, labels, a, b, h, sent_rows, direction, inputs):
    units, rows = a.shape
    width = inputs.shape[1]
    slots = sums.shape[0]
    wide = 512
    steps = width // wide
    out = (slots, 288 + 64, LANES)
    return pl.pallas_call(
        grads_kernel,
        grid=(2 * steps,),
        in_specs=[whole(v.shape) for v in (sums, scores, labels, a, b, h, sent_rows)]
        + [
            pl.BlockSpec((rows, wide), lambda i: (0, jnp.minimum(i, steps - 1))),
            pl.BlockSpec((rows, wide), lambda i: (0, jnp.maximum(i - steps, 0))),
        ],
        out_specs=whole(out),
        out_shape=jax.ShapeDtypeStruct(out, BF),
        scratch_shapes=[pltpu.VMEM((3 * units, rows), BF), pltpu.VMEM((3 * units, width), BF)],
        cost_estimate=pl.CostEstimate(
            flops=6 * rows * width * units, bytes_accessed=12 << 20, transcendentals=rows
        ),
        compiler_params=limits(32),
        name="grads",
    )(sums, scores, labels, a, b, h, sent_rows, direction, inputs)


def adam_step(pc_ref, arr_ref, ms_ref, m1_ref, m2_ref, om_ref, o1_ref, o2_ref, total, fresh):
    total[...] = jnp.zeros_like(total)
    for s in range(arr_ref.shape[0]):
        total[pc_ref[s]] += arr_ref[s].astype(F32)
    for e in range(total.shape[0]):
        grad = total[e]
        master = ms_ref[e, 0]
        new_first = decay_first * m1_ref[e, 0] + (1.0 - decay_first) * grad
        new_second = decay_second * m2_ref[e, 0] + (1.0 - decay_second) * grad * grad
        update = new_first / correct_first / (jnp.sqrt(new_second / correct_second) + adam_eps)
        new_master = master - learn_rate * (update + weight_decay * master)
        om_ref[e, 0] = new_master
        o1_ref[e, 0] = new_first
        o2_ref[e, 0] = new_second
        fresh[e] = new_master.astype(BF)


def adam_pick_kernel(pc_ref, pn_ref, arr_ref, ms, m1, m2, om, o1, o2, pick_ref, total, fresh):
    adam_step(pc_ref, arr_ref, ms, m1, m2, om, o1, o2, total, fresh)
    for t in range(pick_ref.shape[0]):
        pick_ref[t] = fresh[pn_ref[t]]


def adam_split_kernel(pc_ref, arr_ref, ms, m1, m2, _a, _b, _c, om, o1, o2, piece_ref, total, fresh):
    adam_step(pc_ref, arr_ref, ms, m1, m2, om, o1, o2, total, fresh)
    experts = fresh.shape[0]
    turned = dot(swap_map(2, 4, 4), jnp.concatenate([fresh[e] for e in range(experts)], axis=1))
    for q in range(4):
        for e in range(experts):
            piece_ref[q, e] = turned[q * 8 : (q + 1) * 8, e * LANES : (e + 1) * LANES].astype(BF)


def adam_call(place_cur, place_next, arrived, states, held):
    slots = arrived.shape[0]
    experts, _, lines, _ = states[0].shape
    block = 32
    steps = lines // block
    first = 0 if held is None else 2
    state = pl.BlockSpec((experts, 1, block, LANES), lambda i: (0, first + i // steps, i % steps, 0))
    got = pl.BlockSpec((slots, block, LANES), lambda i: (0, first * steps + i, 0))
    smem = pl.BlockSpec(memory_space=pltpu.SMEM)
    shapes = [jax.ShapeDtypeStruct(s.shape, F32) for s in states]
    scratch = [pltpu.VMEM((experts, block, LANES), F32), pltpu.VMEM((experts, block, LANES), BF)]
    cost = pl.CostEstimate(flops=20 << 20, bytes_accessed=6 << 20, transcendentals=0)
    if held is None:
        return pl.pallas_call(
            adam_pick_kernel,
            grid=(2 * steps,),
            in_specs=[smem, smem, got, state, state, state],
            out_specs=[state, state, state, pl.BlockSpec((slots, block, LANES), lambda i: (0, i, 0))],
            out_shape=shapes + [jax.ShapeDtypeStruct((slots, 2 * lines, LANES), BF)],
            scratch_shapes=scratch,
            cost_estimate=cost,
            compiler_params=limits(24),
            name="adam_pick",
        )(place_cur, place_next, arrived, *states)
    return pl.pallas_call(
        adam_split_kernel,
        grid=(steps,),
        in_specs=[smem, got, state, state, state] + [pl.BlockSpec(memory_space=pl.ANY)] * 3,
        out_specs=[state, state, state, pl.BlockSpec((4, experts, 8, LANES), lambda i: (0, 0, i, 0))],
        out_shape=shapes + [jax.ShapeDtypeStruct((4, experts, 8 * steps, LANES), BF)],
        scratch_shapes=scratch,
        input_output_aliases={5: 0, 6: 1, 7: 2},
        cost_estimate=cost,
        compiler_params=limits(24),
        name="adam_split",
    )(place_cur, arrived, *states, *held)


def pick_kernel(pn_ref, p0, p1, p2, p3, out_ref):
    for t in range(out_ref.shape[0]):
        expert = pn_ref[t]
        own = [p[expert].astype(F32) for p in (p0, p1, p2, p3)]
        for a in range(3):
            out_ref[t, a * 32 : (a + 1) * 32] = jnp.concatenate(
                [v[a * 8 : (a + 1) * 8] for v in own], axis=0
            ).astype(BF)


def pick_call(place_next, pieces):
    slots = place_next.shape[0]
    shape = (slots, 4 * pieces[0].shape[1], LANES)
    return pl.pallas_call(
        pick_kernel,
        grid=(1,),
        in_specs=[pl.BlockSpec(memory_space=pltpu.SMEM)] + [whole(p.shape) for p in pieces],
        out_specs=whole(shape),
        out_shape=jax.ShapeDtypeStruct(shape, BF),
        cost_estimate=pl.CostEstimate(flops=1 << 20, bytes_accessed=2 << 20, transcendentals=0),
        compiler_params=limits(16),
        name="pick",
    )(place_next, *pieces)


def hidden_kernel(q_ref, w_ref, r0, r1, r2, r3, out_ref, mat):
    units = out_ref.shape[0]
    swap = swap_map(16, 16)
    for group in range(4):
        for a in range(3):
            both = jnp.concatenate(
                [
                    w_ref[group * 8 : group * 8 + 8, m * 96 + a * 32 : m * 96 + a * 32 + 32].reshape(
                        256, LANES
                    )
                    for m in range(2)
                ],
                axis=1,
            )
            turned = dot(swap, both).astype(BF)
            for m in range(2):
                top = m * units + (group * 3 + a) * 16
                for j in range(16):
                    mat[top : top + 16, j * LANES : (j + 1) * LANES] = turned[
                        j * 16 : (j + 1) * 16, m * LANES : (m + 1) * LANES
                    ]
    total = None
    for k, rows in enumerate((r0, r1, r2, r3)):
        quarter = rows.shape[1]
        start = pl.multiple_of(q_ref[k] * quarter, quarter)
        term = dot(mat[:, pl.ds(start, quarter)], rows[...], NT)
        total = term if total is None else total + term
    gate, up = total[:units], total[units:]
    out_ref[...] = (gate * jax.nn.sigmoid(gate) * up).astype(BF)


def hidden_call(quarters, packed, rows):
    units = packed.shape[0] * 6
    count, quarter = rows[0].shape
    return pl.pallas_call(
        hidden_kernel,
        grid=(1,),
        in_specs=[pl.BlockSpec(memory_space=pltpu.SMEM), whole(packed.shape)]
        + [whole(r.shape) for r in rows],
        out_specs=whole((units, count)),
        out_shape=jax.ShapeDtypeStruct((units, count), BF),
        scratch_shapes=[pltpu.VMEM((2 * units, 4 * quarter), BF)],
        cost_estimate=pl.CostEstimate(
            flops=16 * count * quarter * units, bytes_accessed=4 << 20, transcendentals=count * units
        ),
        compiler_params=limits(24),
        name="hidden",
    )(quarters, packed, *rows)


def unpack_kernel(w_ref, out_ref):
    swap = swap_map(16, 16)
    lines = w_ref.shape[1]
    row = lax.broadcasted_iota(jnp.int32, (256, 256), 0)
    col = lax.broadcasted_iota(jnp.int32, (256, 256), 1)
    k, j, s, b = row // 64, row // 16 % 4, row // 2 % 8, row % 2
    turn = jnp.where(col == ((s * 4 + k) * 2 + b) * 4 + j, 1.0, 0.0).astype(BF)
    for group in range(4):
        for a in range(lines // 32):
            turned = dot(
                turn, w_ref[group * 8 : group * 8 + 8, a * 32 : a * 32 + 32].reshape(256, LANES)
            ).astype(BF)
            top = (group * 3 + a) * 16
            for k in range(4):
                for j in range(4):
                    at = (k * 4 + j) * 16
                    out_ref[k, top : top + 16, j * LANES : (j + 1) * LANES] = turned[at : at + 16]


def unpack_call(packed):
    shape = (4, packed.shape[0] * 6, 4 * LANES)
    return pl.pallas_call(
        unpack_kernel,
        grid=(1,),
        in_specs=[whole(packed.shape)],
        out_specs=whole(shape),
        out_shape=jax.ShapeDtypeStruct(shape, BF),
        cost_estimate=pl.CostEstimate(flops=1 << 28, bytes_accessed=2 << 20, transcendentals=0),
        compiler_params=limits(16),
        name="unpack",
    )(packed)


def down_kernel(w_ref, h0, h1, h2, h3, out_ref):
    total = None
    for k, h in enumerate((h0, h1, h2, h3)):
        term = dot(h[...], w_ref[k], TN)
        total = term if total is None else total + term
    out_ref[...] = total.astype(BF)


def down_call(weights, hidden):
    units, count = hidden[0].shape
    quarter = weights.shape[2]
    return pl.pallas_call(
        down_kernel,
        grid=(1,),
        in_specs=[whole(weights.shape)] + [whole(h.shape) for h in hidden],
        out_specs=whole((count, quarter)),
        out_shape=jax.ShapeDtypeStruct((count, quarter), BF),
        cost_estimate=pl.CostEstimate(
            flops=8 * count * quarter * units, bytes_accessed=3 << 20, transcendentals=0
        ),
        compiler_params=limits(16),
        name="down",
    )(weights, *hidden)


def shards(
    master,
    first_moment,
    second_moment,
    slot_weights,
    back_rows,
    readout,
    ref_logratio,
    labels,
    place_cur,
    place_next,
    fwd_rows,
    routes,
):
    slot_count = lax.axis_size("slot")
    hid_count = lax.axis_size("hid")
    hid_index = lax.axis_index("hid").astype(jnp.int32)
    rows, width = back_rows.shape[1:]

    def pass_on(value, k):
        return lax.ppermute(value, "hid", [(i, (i + k) % hid_count) for i in range(hid_count)])

    def exchange(value):
        return lax.all_to_all(value, "slot", split_axis=0, concat_axis=0, tiled=True)

    capacity = 2 * fwd_rows.shape[0] // slot_count
    quarter = fwd_rows.shape[1]
    target = routes[:, 0]
    target_map = (target[:, None] == jnp.arange(slot_count, dtype=jnp.int32)[None, :]).astype(BF)
    order = jnp.arange(fwd_rows.shape[0], dtype=jnp.int32)
    below = (order[:, None] > order[None, :]).astype(BF)
    earlier = jnp.dot(below, target_map, preferred_element_type=F32)
    position = jnp.sum(earlier * target_map.astype(F32), axis=1).astype(jnp.int32)
    slot_place = target * capacity + position
    place_map = (
        slot_place[None, :] == jnp.arange(slot_count * capacity, dtype=jnp.int32)[:, None]
    ).astype(BF)
    sent_rows = jnp.dot(place_map, fwd_rows, preferred_element_type=F32).astype(BF)

    a, b, h, part = scores_call(back_rows[0], readout[0], slot_weights.reshape(-1, width))
    part = part.reshape(rows // LANES, LANES)
    policy = part
    for k in range(1, hid_count):
        policy = policy + pass_on(part, k)
    scores = policy - ref_logratio.reshape(part.shape)
    sums = exchange(jnp.broadcast_to(jnp.sum(scores), (slot_count, 1, LANES)))
    blocks = grads_call(
        sums, scores, labels.reshape(part.shape), a, b, h, sent_rows, readout[0], back_rows[0]
    )
    arrived = exchange(blocks)

    own_rows = arrived[:, 288:].reshape(slot_count, quarter // LANES, capacity, LANES)
    own_rows = own_rows.transpose(0, 2, 1, 3).reshape(slot_count * capacity, quarter)
    all_rows = [own_rows] + [pass_on(own_rows, k) for k in range(1, hid_count)]
    quarters = (hid_index + hid_count - jnp.arange(hid_count, dtype=jnp.int32)) % hid_count

    lines = 96
    shape = (master.shape[0], 3, lines, LANES)
    states = [v.reshape(shape) for v in (master, first_moment, second_moment)]
    *held, picked = adam_call(place_cur, place_next, arrived, states, None)
    gate_up = exchange(picked)
    *held, pieces = adam_call(place_cur, place_next, arrived, states, held)
    pieces = [
        lax.dynamic_index_in_dim(pieces, (hid_index + k) % hid_count, 0, keepdims=False)
        for k in range(hid_count)
    ]
    pieces = [pieces[0]] + [pass_on(pieces[k], k) for k in range(1, hid_count)]
    down = exchange(pick_call(place_next, pieces))

    hidden = hidden_call(quarters, gate_up, all_rows)
    hidden = [hidden] + [pass_on(hidden, k) for k in range(1, hid_count)]
    produced = down_call(unpack_call(down), hidden)
    returned = exchange(produced.reshape(slot_count, capacity, quarter))
    out_rows = lax.dot_general(
        place_map,
        returned.reshape(slot_count * capacity, quarter),
        (((0,), (0,)), ((), ())),
        preferred_element_type=F32,
    ).astype(BF)
    return (out_rows, *[v.reshape(master.shape) for v in held])


def solution(mesh):
    shard = P(None, None, "hid", "slot")
    return jax.shard_map(
        shards,
        mesh=mesh,
        in_specs=(
            shard,
            shard,
            shard,
            P("slot", None, "hid", None),
            P("slot", None, None),
            P("slot", None, None),
            P("slot", None),
            P("slot", None),
            P(),
            P(),
            P("slot", "hid"),
            P("slot", None),
        ),
        out_specs=(P("slot", "hid"), shard, shard, shard),
        check_vma=False,
    )
```

time: 365 us -> 183 us (0.50)
  blocking collectives: 197 us -> 60 us
  matrix products: 40.8 us -> 1.57 us
  waiting for transfers between devices: 59.2 us -> 32 us
  Pallas kernels: 0 us -> 24.8 us
  starting transfers between devices: 14.9 us -> 35.8 us
  between operations: 14.9 us -> 0.94 us
  local copies, waits for them, and re-layouts: 36.4 us -> 26 us
    psum x3 -> x0, blocking collectives: 152 us -> none  [the longest x1 75.4 us: shards(): totals = lax.psum(fwd_partial, 'hid')]
    dot_general x13 -> x3, matrix products: 40.8 us -> 1.57 us  [the longest x1 1.06 us: shards(): lax.dot_general(place_map, returned.reshape(slot_count * capacity, quarte...]
    all_to_all x3, waiting for transfers between devices: 36.7 us -> 10.4 us  [exchange(): lax.all_to_all(value, 'slot', split_axis=0, concat_axis=0, tiled=True)]
    pallas_call x0 -> x8, Pallas kernels: none -> 24.8 us  [the longest x1 6.21 us: grads_call(): pl.pallas_call(grads_kernel, grid=(2 * steps,), in_specs=[whole(v.shape)...]
    all_gather x1 -> x0, waiting for transfers between devices: 21.8 us -> none  [shards(): widened = lax.all_gather(fwd_rows, 'hid', axis=1, tiled=True)]
    ppermute x0 -> x12, waiting for transfers between devices: none -> 21.6 us  [pass_on(): lax.ppermute(value, 'hid', [(i, (i + k) % hid_count) for i in range(hid_c...]
    ppermute x0 -> x12, starting transfers between devices: none -> 16.3 us  [pass_on(): lax.ppermute(value, 'hid', [(i, (i + k) % hid_count) for i in range(hid_c...]
    all_to_all x1 -> x2, blocking collectives: 45.2 us -> 60 us  [exchange(): lax.all_to_all(value, 'slot', split_axis=0, concat_axis=0, tiled=True)]
  transfers between devices with their start and end apart: 4 -> 15, of which waited for: 4 -> 10; matrix products, arithmetic and copies ran while one was open for 6% -> 1% of each run, Pallas kernels for 0% -> 5%
where the time goes in v2:
time: 183 us; the launch traced here: 182 us
  blocking collectives  60 us (33%)
  starting transfers between devices  35.8 us (20%)
  waiting for transfers between devices  32 us (17%)
  local copies, waits for them, and re-layouts  26 us (14%)
  Pallas kernels  24.8 us (14%)
    all_to_all x2, blocking collectives, exchange(): lax.all_to_all(value, 'slot', split_axis=0, concat_axis=0, tiled=True)  60 us
    unnamed x53, local copies, waits for them, and re-layouts  24.4 us
    ppermute x12, waiting for transfers between devices, pass_on(): lax.ppermute(value, 'hid', [(i, (i + k) % hid_count) for i in range(hid_c...  21.6 us
    all_to_all x3, starting transfers between devices, exchange(): lax.all_to_all(value, 'slot', split_axis=0, concat_axis=0, tiled=True)  19.5 us
    ppermute x12, starting transfers between devices, pass_on(): lax.ppermute(value, 'hid', [(i, (i + k) % hid_count) for i in range(hid_c...  16.3 us
    all_to_all x3, waiting for transfers between devices, exchange(): lax.all_to_all(value, 'slot', split_axis=0, concat_axis=0, tiled=True)  10.4 us
    pallas_call x1, Pallas kernels, grads_call(): pl.pallas_call(grads_kernel, grid=(2 * steps,), in_specs=[whole(v.shape)...  6.21 us
    pallas_call x1, Pallas kernels, adam_call(): pl.pallas_call(adam_pick_kernel, grid=(2 * steps,), in_specs=[smem, smem,...  5.09 us
  transfers between devices with their start and end apart: 15, of which 10 were waited for; matrix products, arithmetic and copies ran while one was open for 1% of the time, Pallas kernels for 5%

profile of v2, /device:TPU:1, one launch (start us, length us, event | category | flops | bytes accessed | tf_op | source)
XLA Modules:
  0.0 181.8 jit_solution(17587444095124097759)
XLA Ops:
  0.7 2.2 %copy-done.1 = bf16[1,1024,2048]{2,1,0:T(8,128)(2,1)S(1)} copy-done((bf16[1,1024,2048]{2,1,0:T(8,128)(2,1)S(1)}, bf16[1,1024,2048]{2,1,0:T(8,128)(2,1)}, u32[]{:S(2)}) %copy-start.1) | copy-done | bytes 4194328
  2.9 2.2 %copy-done.3 = bf16[1,1024,2048]{2,1,0:T(8,128)(2,1)S(1)} copy-done((bf16[1,1024,2048]{2,1,0:T(8,128)(2,1)S(1)}, bf16[1,1024,2048]{2,1,0:T(8,128)(2,1)}, u32[]{:S(2)}) %copy-start.3) | copy-done | bytes 4194328
  5.1 1.7 copy-done.11
  6.7 4.1 %scores.1 = (f32[192,1024]{1,0:T(8,128)S(1)}, f32[192,1024]{1,0:T(8,128)S(1)}, bf16[192,1024]{1,0:T(8,128)(2,1)S(1)}, f32[1,1024]{1,0:T(1,128)S(1)}) custom-call(bf16[1024,2048]{1,0:T(8,128)(2,1)S(1)} %bitcast.32, bf16[1024,2048]{1,0:T(8,128)(2,1)S(1)} %bitcast.34, bf16[576,2048]{1,0:T(8,128)(2,1)S(1)} %bitcast.42), custom_call_target="tpu_custom_call" | custom-call | flops 2415919104 | bytes 14680064 | tf_op jit(solution)/shard_map/scores/pallas_call | solution.py:65
  12.6 2.0 %collective-permute-start = (f32[8,128]{1,0:T(8,128)S(1)}, f32[8,128]{1,0:T(8,128)S(1)}, u32[]{:S(2)}, u32[]{:S(2)}) collective-permute-start(f32[8,128]{1,0:T(8,128)S(1)} %bitcast.49), channel_id=1, source_target_pairs={{0,1},{1,2},{2,3},{3,0},{4,5},{5,6},{6,7},{7,4},{8,9},{9,10},{10,1... | collective-permute-start | bytes 12296 | tf_op jit(solution)/shard_map/ppermute | solution.py:399
  14.6 2.4 %collective-permute-start.1 = (f32[8,128]{1,0:T(8,128)S(1)}, f32[8,128]{1,0:T(8,128)S(1)}, u32[]{:S(2)}, u32[]{:S(2)}) collective-permute-start(f32[8,128]{1,0:T(8,128)S(1)} %bitcast.50), channel_id=1, source_target_pairs={{0,2},{1,3},{2,0},{3,1},{4,6},{5,7},{6,4},{7,5},{8,10},{9,11},{10,... | collective-permute-start | bytes 12296 | tf_op jit(solution)/shard_map/ppermute | solution.py:399
  20.4 1.3 broadcast_in_dim.2
  21.7 10.2 %all-to-all-start = ((f32[32,1,128]{2,1,0:T(1,128)}), f32[32,1,128]{2,1,0:T(1,128)S(1)}, u32[]{:S(2)}, u32[]{:S(2)}) async-start(f32[32,1,128]{2,1,0:T(1,128)} %broadcast_in_dim.2), calls=%async_computation | async-start | bytes 32768 | tf_op jit(solution)/shard_map/all_to_all | solution.py:402
  32.2 6.6 %all-to-all-done.sums_ref = f32[32,1,128]{2,1,0:T(1,128)S(1)} async-done(((f32[32,1,128]{2,1,0:T(1,128)}), f32[32,1,128]{2,1,0:T(1,128)S(1)}, u32[]{:S(2)}, u32[]{:S(2)}) %all-to-all-start) | async-done | bytes 16416 | tf_op jit(solution)/shard_map/all_to_all | solution.py:402
  38.8 2.2 %copy-done.2 = bf16[1,1024,2048]{2,1,0:T(8,128)(2,1)S(1)} copy-done((bf16[1,1024,2048]{2,1,0:T(8,128)(2,1)S(1)}, bf16[1,1024,2048]{2,1,0:T(8,128)(2,1)}, u32[]{:S(2)}) %copy-start.2) | copy-done | bytes 4194328
  41.0 2.2 %copy-done.4 = bf16[1,1024,2048]{2,1,0:T(8,128)(2,1)S(1)} copy-done((bf16[1,1024,2048]{2,1,0:T(8,128)(2,1)S(1)}, bf16[1,1024,2048]{2,1,0:T(8,128)(2,1)}, u32[]{:S(2)}) %copy-start.4) | copy-done | bytes 4194328
  45.4 6.2 %grads.1 = bf16[32,352,128]{2,1,0:T(8,128)(2,1)S(1)} custom-call(f32[32,1,128]{2,1,0:T(1,128)S(1)} %all-to-all-done.sums_ref, f32[8,128]{1,0:T(8,128)S(1)} %get-tuple-element.37.sco_ref, s32[8,128]{1,0:T(8,128)S(1)} %bitcast.48, f32[192,1024]{1,0:T(8,128)S(1)} %copy-done.14, f32[192,1024]{1,0:T(8,128)S(1)} %copy-done.16, ...), custom_call_target="tpu_custom_call" | custom-call | flops 2415919104 | bytes 12582912 | tf_op jit(solution)/shard_map/grads/pallas_call | solution.py:157
  51.7 40.7 %all_to_all.25.arr_ref = bf16[32,352,128]{2,1,0:T(8,128)(2,1)S(1)} all-to-all(bf16[32,352,128]{2,1,0:T(8,128)(2,1)S(1)} %grads.1), channel_id=1, replica_groups=mesh['slot'=32,'hid'=4] {'slot'}, dimensions={0} | all-to-all | bytes 5767168 | tf_op jit(solution)/shard_map/all_to_all | solution.py:402
  92.4 5.1 %adam_pick.1 = (f32[16,3,96,128]{3,2,1,0:T(8,128)}, f32[16,3,96,128]{3,2,1,0:T(8,128)}, f32[16,3,96,128]{3,2,1,0:T(8,128)}, bf16[32,192,128]{2,1,0:T(8,128)(2,1)S(1)}) custom-call(s32[32]{0:T(128)S(1)} %copy-done.22, s32[32]{0:T(128)S(1)} %copy-done.23, bf16[32,352,128]{2,1,0:T(8,128)(2,1)S(1)} %all_to_all.25.arr_ref, f32[16,3,96,128]{3,2,1,0:T(8,128)S(1)} %bitcast.36, ...), custom_call_target="tpu_custom_call" | custom-call | flops 20971520 | bytes 6291456 | tf_op jit(solution)/shard_map/adam_pick/pallas_call | solution.py:221
  98.7 4.5 %all-to-all-start.3 = ((bf16[32,192,128]{2,1,0:T(8,128)(2,1)}), bf16[32,192,128]{2,1,0:T(8,128)(2,1)}, u32[]{:S(2)}, u32[]{:S(2)}) async-start(bf16[32,192,128]{2,1,0:T(8,128)(2,1)} %copy-done.12), calls=%async_computation.3 | async-start | bytes 3145728 | tf_op jit(solution)/shard_map/all_to_all | solution.py:402
  103.2 1.7 copy-done.6
  104.9 1.7 copy-done.8
  106.6 1.7 copy-done.10
  108.2 3.5 %adam_split.1 = (f32[16,3,96,128]{3,2,1,0:T(8,128)}, f32[16,3,96,128]{3,2,1,0:T(8,128)}, f32[16,3,96,128]{3,2,1,0:T(8,128)}, bf16[4,16,24,128]{3,2,1,0:T(8,128)(2,1)S(1)}) custom-call(s32[32]{0:T(128)S(1)} %copy-done.22, bf16[32,352,128]{2,1,0:T(8,128)(2,1)S(1)} %all_to_all.25.arr_ref, ...), custom_call_target="tpu_custom_call", output_to_operand_aliasing={{0}: (5, {}), {1}: (6, {}), {2}: (7, {})} | custom-call | flops 20971520 | bytes 6291456 | tf_op jit(solution)/shard_map/adam_split/pallas_call | solution.py:232
  111.8 3.5 %collective-permute-start.4 = (bf16[16,24,128]{2,1,0:T(8,128)(2,1)S(1)}, bf16[16,24,128]{2,1,0:T(8,128)(2,1)S(1)}, u32[]{:S(2)}, u32[]{:S(2)}) collective-permute-start(bf16[16,24,128]{2,1,0:T(8,128)(2,1)S(1)} %get-tuple-element.39), channel_id=1, source_target_pairs={{0,2},{1,3},{2,0},{3,1},{4,6},{5,7},{6,4},{7,5},{8,10},{9,11},{10,... | collective-permute-start | bytes 294920 | tf_op jit(solution)/shard_map/ppermute | solution.py:399
  115.8 1.5 collective-permute-start.6
  117.4 2.4 %collective-permute-start.8 = (bf16[512,512]{1,0:T(8,128)(2,1)S(1)}, bf16[512,512]{1,0:T(8,128)(2,1)}, u32[]{:S(2)}, u32[]{:S(2)}) collective-permute-start(bf16[512,512]{1,0:T(8,128)(2,1)S(1)} %bitcast.45), channel_id=1, source_target_pairs={{0,3},{1,0},{2,1},{3,2},{4,7},{5,4},{6,5},{7,6},{8,11},{9,8},{10,9... | collective-permute-start | bytes 1572872 | tf_op jit(solution)/shard_map/ppermute | solution.py:399
  120.3 1.6 pick.1
  121.9 3.8 %all-to-all-done.3.w_ref = bf16[32,192,128]{2,1,0:T(8,128)(2,1)} async-done(((bf16[32,192,128]{2,1,0:T(8,128)(2,1)}), bf16[32,192,128]{2,1,0:T(8,128)(2,1)}, u32[]{:S(2)}, u32[]{:S(2)}) %all-to-all-start.3) | async-done | bytes 1572896 | tf_op jit(solution)/shard_map/all_to_all | solution.py:402
  125.7 4.8 %all-to-all-start.2 = ((bf16[32,96,128]{2,1,0:T(8,128)(2,1)}), bf16[32,96,128]{2,1,0:T(8,128)(2,1)S(1)}, u32[]{:S(2)}, u32[]{:S(2)}) async-start(bf16[32,96,128]{2,1,0:T(8,128)(2,1)} %pick.1), calls=%async_computation.2 | async-start | bytes 1572864 | tf_op jit(solution)/shard_map/all_to_all | solution.py:402
  130.5 1.4 collective-permute-done.6.r1
  132.7 10.0 %collective-permute-done.7.r2 = bf16[512,512]{1,0:T(8,128)(2,1)S(1)} collective-permute-done((bf16[512,512]{1,0:T(8,128)(2,1)S(1)}, bf16[512,512]{1,0:T(8,128)(2,1)S(1)}, u32[]{:S(2)}, u32[]{:S(2)}) %collective-permute-start.7) | collective-permute-done | bytes 524320 | tf_op jit(solution)/shard_map/ppermute | solution.py:399
  145.6 3.0 %hidden.1.h0 = bf16[192,512]{1,0:T(8,128)(2,1)S(1)} custom-call(s32[4]{0:T(128)S(1)} %and_select_fusion.q_ref, bf16[32,192,128]{2,1,0:T(8,128)(2,1)} %all-to-all-done.3.w_ref, bf16[512,512]{1,0:T(8,128)(2,1)S(1)} %bitcast.46, bf16[512,512]{1,0:T(8,128)(2,1)S(1)} %copy-done.18, bf16[512,512]{1,0:T(8,128)(2,1)S(1)} %copy-done.20, ...), custom_call_target="tpu_custom_call" | custom-call | flops 805306368 | bytes 4194304 | tf_op jit(solution)/shard_map/hidden/pallas_call | solution.py:305
  148.9 2.8 %collective-permute-start.11 = (bf16[192,512]{1,0:T(8,128)(2,1)S(1)}, bf16[192,512]{1,0:T(8,128)(2,1)S(1)}, u32[]{:S(2)}, u32[]{:S(2)}) collective-permute-start(bf16[192,512]{1,0:T(8,128)(2,1)S(1)} %hidden.1.h0), channel_id=1, source_target_pairs={{0,3},{1,0},{2,1},{3,2},{4,7},{5,4},{6,5},{7,6},{8,11},{9,8},{10,9... | collective-permute-start | bytes 589832 | tf_op jit(solution)/shard_map/ppermute | solution.py:399
  152.3 3.4 %collective-permute-done.10.h2 = bf16[192,512]{1,0:T(8,128)(2,1)S(1)} collective-permute-done((bf16[192,512]{1,0:T(8,128)(2,1)S(1)}, bf16[192,512]{1,0:T(8,128)(2,1)S(1)}, u32[]{:S(2)}, u32[]{:S(2)}) %collective-permute-start.10) | collective-permute-done | bytes 196640 | tf_op jit(solution)/shard_map/ppermute | solution.py:399
  155.7 4.3 %collective-permute-done.11.h3 = bf16[192,512]{1,0:T(8,128)(2,1)S(1)} collective-permute-done((bf16[192,512]{1,0:T(8,128)(2,1)S(1)}, bf16[192,512]{1,0:T(8,128)(2,1)S(1)}, u32[]{:S(2)}, u32[]{:S(2)}) %collective-permute-start.11) | collective-permute-done | bytes 196640 | tf_op jit(solution)/shard_map/ppermute | solution.py:399
  161.4 19.3 %all_to_all.26 = bf16[32,16,512]{2,1,0:T(8,128)(2,1)S(1)} all-to-all(bf16[32,16,512]{2,1,0:T(8,128)(2,1)S(1)} %bitcast.47), channel_id=1, replica_groups=mesh['slot'=32,'hid'=4] {'slot'}, dimensions={0} | all-to-all | bytes 1048576 | tf_op jit(solution)/shard_map/all_to_all | solution.py:402
  (71 shorter events, 17.1 us)
Async XLA Ops:
  0.6 31.2 %copy-start = (bf16[256,512]{1,0:T(8,128)(2,1)S(1)}, bf16[256,512]{1,0:T(8,128)(2,1)}, u32[]{:S(2)}) copy-start(bf16[256,512]{1,0:T(8,128)(2,1)} %param.22) | copy-start | bytes 786436
  0.6 2.2 %copy-start.1 = (bf16[1,1024,2048]{2,1,0:T(8,128)(2,1)S(1)}, bf16[1,1024,2048]{2,1,0:T(8,128)(2,1)}, u32[]{:S(2)}) copy-start(bf16[1,1024,2048]{2,1,0:T(8,128)(2,1)} %param.16) | copy-start | bytes 12582916
  2.9 2.2 %copy-start.3 = (bf16[1,1024,2048]{2,1,0:T(8,128)(2,1)S(1)}, bf16[1,1024,2048]{2,1,0:T(8,128)(2,1)}, u32[]{:S(2)}) copy-start(bf16[1,1024,2048]{2,1,0:T(8,128)(2,1)} %param.17) | copy-start | bytes 12582916
  5.1 1.7 copy-start.11
  6.7 11.5 %copy-start.25 = (s32[256,1]{0,1:T(1,128)S(1)}, s32[256,1]{0,1:T(1,128)}, u32[]{:S(2)}) copy-start(s32[256,1]{0,1:T(1,128)} %param.23) | copy-start | bytes 3076
  6.7 13.1 %copy-start.24 = (f32[1,1024]{1,0:T(1,128)S(1)}, f32[1,1024]{1,0:T(1,128)}, u32[]{:S(2)}) copy-start(f32[1,1024]{1,0:T(1,128)} %param.18) | copy-start | bytes 12292
  6.7 32.0 %copy-start.21 = (s32[1,1024]{1,0:T(1,128)S(1)}, s32[1,1024]{1,0:T(1,128)}, u32[]{:S(2)}) copy-start(s32[1,1024]{1,0:T(1,128)} %param.19) | copy-start | bytes 12292
  12.6 5.9 %collective-permute-start = (f32[8,128]{1,0:T(8,128)S(1)}, f32[8,128]{1,0:T(8,128)S(1)}, u32[]{:S(2)}, u32[]{:S(2)}) collective-permute-start(f32[8,128]{1,0:T(8,128)S(1)} %bitcast.49), channel_id=1, source_target_pairs={{0,1},{1,2},{2,3},{3,0},{4,5},{5,6},{6,7},{7,4},{8,9},{9,10},{10,1... | collective-permute-start | bytes 12296 | tf_op jit(solution)/shard_map/ppermute | solution.py:399
  14.6 4.0 %collective-permute-start.1 = (f32[8,128]{1,0:T(8,128)S(1)}, f32[8,128]{1,0:T(8,128)S(1)}, u32[]{:S(2)}, u32[]{:S(2)}) collective-permute-start(f32[8,128]{1,0:T(8,128)S(1)} %bitcast.50), channel_id=1, source_target_pairs={{0,2},{1,3},{2,0},{3,1},{4,6},{5,7},{6,4},{7,5},{8,10},{9,11},{10,... | collective-permute-start | bytes 12296 | tf_op jit(solution)/shard_map/ppermute | solution.py:399
  17.0 2.8 %collective-permute-start.2 = (f32[8,128]{1,0:T(8,128)S(1)}, f32[8,128]{1,0:T(8,128)S(1)}, u32[]{:S(2)}, u32[]{:S(2)}) collective-permute-start(f32[8,128]{1,0:T(8,128)S(1)} %bitcast.51), channel_id=1, source_target_pairs={{0,3},{1,0},{2,1},{3,2},{4,7},{5,4},{6,5},{7,6},{8,11},{9,8},{10,9... | collective-permute-start | bytes 12296 | tf_op jit(solution)/shard_map/ppermute | solution.py:399
  21.7 17.1 %all-to-all-start = ((f32[32,1,128]{2,1,0:T(1,128)}), f32[32,1,128]{2,1,0:T(1,128)S(1)}, u32[]{:S(2)}, u32[]{:S(2)}) async-start(f32[32,1,128]{2,1,0:T(1,128)} %broadcast_in_dim.2), calls=%async_computation | async-start | bytes 32768 | tf_op jit(solution)/shard_map/all_to_all | solution.py:402
  38.8 2.2 %copy-start.2 = (bf16[1,1024,2048]{2,1,0:T(8,128)(2,1)S(1)}, bf16[1,1024,2048]{2,1,0:T(8,128)(2,1)}, u32[]{:S(2)}) copy-start(bf16[1,1024,2048]{2,1,0:T(8,128)(2,1)} %param.16) | copy-start | bytes 12582916
  41.0 2.2 %copy-start.4 = (bf16[1,1024,2048]{2,1,0:T(8,128)(2,1)S(1)}, bf16[1,1024,2048]{2,1,0:T(8,128)(2,1)}, u32[]{:S(2)}) copy-start(bf16[1,1024,2048]{2,1,0:T(8,128)(2,1)} %param.17) | copy-start | bytes 12582916
  45.4 47.0 %copy-start.9 = (f32[16,3,1,12288]{3,2,1,0:T(1,128)S(1)}, f32[16,3,1,12288]{3,2,1,0:T(1,128)}, u32[]{:S(2)}) copy-start(f32[16,3,1,12288]{3,2,1,0:T(1,128)} %param.14) | copy-start | bytes 7077892
  51.6 40.7 %copy-start.5 = (f32[16,3,1,12288]{3,2,1,0:T(1,128)S(1)}, f32[16,3,1,12288]{3,2,1,0:T(1,128)}, u32[]{:S(2)}) copy-start(f32[16,3,1,12288]{3,2,1,0:T(1,128)} %param.12) | copy-start | bytes 7077892
  51.6 40.7 %copy-start.7 = (f32[16,3,1,12288]{3,2,1,0:T(1,128)S(1)}, f32[16,3,1,12288]{3,2,1,0:T(1,128)}, u32[]{:S(2)}) copy-start(f32[16,3,1,12288]{3,2,1,0:T(1,128)} %param.13) | copy-start | bytes 7077892
  51.7 40.7 %copy-start.22 = (s32[32]{0:T(128)S(1)}, s32[32]{0:T(128)}, u32[]{:S(2)}) copy-start(s32[32]{0:T(128)} %pc_ref.3) | copy-start | bytes 388
  51.7 40.7 %copy-start.23 = (s32[32]{0:T(128)S(1)}, s32[32]{0:T(128)}, u32[]{:S(2)}) copy-start(s32[32]{0:T(128)} %pn_ref.3) | copy-start | bytes 388
  98.7 27.0 %all-to-all-start.3 = ((bf16[32,192,128]{2,1,0:T(8,128)(2,1)}), bf16[32,192,128]{2,1,0:T(8,128)(2,1)}, u32[]{:S(2)}, u32[]{:S(2)}) async-start(bf16[32,192,128]{2,1,0:T(8,128)(2,1)} %copy-done.12), calls=%async_computation.3 | async-start | bytes 3145728 | tf_op jit(solution)/shard_map/all_to_all | solution.py:402
  103.2 1.7 copy-start.6
  104.9 1.7 copy-start.8
  106.5 1.7 copy-start.10
  111.8 5.7 %collective-permute-start.3 = (bf16[16,24,128]{2,1,0:T(8,128)(2,1)S(1)}, bf16[16,24,128]{2,1,0:T(8,128)(2,1)S(1)}, u32[]{:S(2)}, u32[]{:S(2)}) collective-permute-start(bf16[16,24,128]{2,1,0:T(8,128)(2,1)S(1)} %get-tuple-element.40), channel_id=1, source_target_pairs={{0,1},{1,2},{2,3},{3,0},{4,5},{5,6},{6,7},{7,4},{8,9},{9,10},{10,1... | collective-permute-start | bytes 294920 | tf_op jit(solution)/shard_map/ppermute | solution.py:399
  111.8 8.5 %collective-permute-start.4 = (bf16[16,24,128]{2,1,0:T(8,128)(2,1)S(1)}, bf16[16,24,128]{2,1,0:T(8,128)(2,1)S(1)}, u32[]{:S(2)}, u32[]{:S(2)}) collective-permute-start(bf16[16,24,128]{2,1,0:T(8,128)(2,1)S(1)} %get-tuple-element.39), channel_id=1, source_target_pairs={{0,2},{1,3},{2,0},{3,1},{4,6},{5,7},{6,4},{7,5},{8,10},{9,11},{10,... | collective-permute-start | bytes 294920 | tf_op jit(solution)/shard_map/ppermute | solution.py:399
  115.4 5.0 %collective-permute-start.5 = (bf16[16,24,128]{2,1,0:T(8,128)(2,1)S(1)}, bf16[16,24,128]{2,1,0:T(8,128)(2,1)S(1)}, u32[]{:S(2)}, u32[]{:S(2)}) collective-permute-start(bf16[16,24,128]{2,1,0:T(8,128)(2,1)S(1)} %get-tuple-element.38), channel_id=1, source_target_pairs={{0,3},{1,0},{2,1},{3,2},{4,7},{5,4},{6,5},{7,6},{8,11},{9,8},{10,9... | collective-permute-start | bytes 294920 | tf_op jit(solution)/shard_map/ppermute | solution.py:399
  115.8 16.1 %collective-permute-start.6 = (bf16[512,512]{1,0:T(8,128)(2,1)S(1)}, bf16[512,512]{1,0:T(8,128)(2,1)S(1)}, u32[]{:S(2)}, u32[]{:S(2)}) collective-permute-start(bf16[512,512]{1,0:T(8,128)(2,1)S(1)} %bitcast.43), channel_id=1, source_target_pairs={{0,1},{1,2},{2,3},{3,0},{4,5},{5,6},{6,7},{7,4},{8,9},{9,10},{10,1... | collective-permute-start | bytes 1572872 | tf_op jit(solution)/shard_map/ppermute | solution.py:399
  117.3 25.4 %collective-permute-start.7 = (bf16[512,512]{1,0:T(8,128)(2,1)S(1)}, bf16[512,512]{1,0:T(8,128)(2,1)S(1)}, u32[]{:S(2)}, u32[]{:S(2)}) collective-permute-start(bf16[512,512]{1,0:T(8,128)(2,1)S(1)} %bitcast.44), channel_id=1, source_target_pairs={{0,2},{1,3},{2,0},{3,1},{4,6},{5,7},{6,4},{7,5},{8,10},{9,11},{10,... | collective-permute-start | bytes 1572872 | tf_op jit(solution)/shard_map/ppermute | solution.py:399
  117.4 26.1 %collective-permute-start.8 = (bf16[512,512]{1,0:T(8,128)(2,1)S(1)}, bf16[512,512]{1,0:T(8,128)(2,1)}, u32[]{:S(2)}, u32[]{:S(2)}) collective-permute-start(bf16[512,512]{1,0:T(8,128)(2,1)S(1)} %bitcast.45), channel_id=1, source_target_pairs={{0,3},{1,0},{2,1},{3,2},{4,7},{5,4},{6,5},{7,6},{8,11},{9,8},{10,9... | collective-permute-start | bytes 1572872 | tf_op jit(solution)/shard_map/ppermute | solution.py:399
  125.7 26.0 %all-to-all-start.2 = ((bf16[32,96,128]{2,1,0:T(8,128)(2,1)}), bf16[32,96,128]{2,1,0:T(8,128)(2,1)S(1)}, u32[]{:S(2)}, u32[]{:S(2)}) async-start(bf16[32,96,128]{2,1,0:T(8,128)(2,1)} %pick.1), calls=%async_computation.2 | async-start | bytes 1572864 | tf_op jit(solution)/shard_map/all_to_all | solution.py:402
  148.6 7.1 %collective-permute-start.10 = (bf16[192,512]{1,0:T(8,128)(2,1)S(1)}, bf16[192,512]{1,0:T(8,128)(2,1)S(1)}, u32[]{:S(2)}, u32[]{:S(2)}) collective-permute-start(bf16[192,512]{1,0:T(8,128)(2,1)S(1)} %hidden.1.h0), channel_id=1, source_target_pairs={{0,2},{1,3},{2,0},{3,1},{4,6},{5,7},{6,4},{7,5},{8,10},{9,11},{10,... | collective-permute-start | bytes 589832 | tf_op jit(solution)/shard_map/ppermute | solution.py:399
  148.9 11.0 %collective-permute-start.11 = (bf16[192,512]{1,0:T(8,128)(2,1)S(1)}, bf16[192,512]{1,0:T(8,128)(2,1)S(1)}, u32[]{:S(2)}, u32[]{:S(2)}) collective-permute-start(bf16[192,512]{1,0:T(8,128)(2,1)S(1)} %hidden.1.h0), channel_id=1, source_target_pairs={{0,3},{1,0},{2,1},{3,2},{4,7},{5,4},{6,5},{7,6},{8,11},{9,8},{10,9... | collective-permute-start | bytes 589832 | tf_op jit(solution)/shard_map/ppermute | solution.py:399
  151.7 8.9 %collective-permute-start.9 = (bf16[192,512]{1,0:T(8,128)(2,1)S(1)}, bf16[192,512]{1,0:T(8,128)(2,1)S(1)}, u32[]{:S(2)}, u32[]{:S(2)}) collective-permute-start(bf16[192,512]{1,0:T(8,128)(2,1)S(1)} %hidden.1.h0), channel_id=1, source_target_pairs={{0,1},{1,2},{2,3},{3,0},{4,5},{5,6},{6,7},{7,4},{8,9},{9,10},{10,1... | collective-permute-start | bytes 589832 | tf_op jit(solution)/shard_map/ppermute | solution.py:399
  (9 other events, 8.9 us)

commit v3 on v2

v3 whole, which is shorter than its diff:
```python
import functools

import jax
import jax.numpy as jnp
from jax import lax
from jax.experimental import pallas as pl
from jax.experimental.pallas import tpu as pltpu
from jax.sharding import PartitionSpec as P

desired_weight = 1.0
undesired_weight = 1.33
learn_rate = 0.004
decay_first = 0.9
decay_second = 0.999
correct_first = 0.9999734386011124
correct_second = 0.09520785288629043
adam_eps = 1e-08
weight_decay = 0.1

BF = jnp.bfloat16
F32 = jnp.float32
NT = (((1,), (1,)), ((), ()))
TN = (((0,), (0,)), ((), ()))
LANES = 128
CAPACITY = 16
CHUNKS = 2
AHEAD = 3


def dot(a, b, dims=(((1,), (0,)), ((), ()))):
    return lax.dot_general(a, b, dims, preferred_element_type=F32)


def swap_map(first, second, tail=1):
    size = first * second * tail
    row = lax.broadcasted_iota(jnp.int32, (size, size), 0)
    col = lax.broadcasted_iota(jnp.int32, (size, size), 1)
    b, a, t = row // (first * tail), row // tail % first, row % tail
    return jnp.where(col == (a * second + b) * tail + t, 1.0, 0.0).astype(BF)


def piece_map():
    row = lax.broadcasted_iota(jnp.int32, (96, 96), 0)
    col = lax.broadcasted_iota(jnp.int32, (96, 96), 1)
    q, unit, j = row // 24, row // 4 % 6, row % 4
    return jnp.where(col == (unit * 4 + q) * 4 + j, 1.0, 0.0).astype(BF)


def whole(shape):
    return pl.BlockSpec(shape, lambda *_: (0,) * len(shape))


def single(shape):
    return pl.BlockSpec(shape, lambda *_: (0,) * len(shape), pipeline_mode=pl.Buffered(1))


def limits(mib):
    return pltpu.CompilerParams(vmem_limit_bytes=mib << 20)


def scores_kernel(
    own_ref, x_hbm, r_hbm, w_hbm, log_ref, route_ref, fwd_ref,
    x_ref, r_ref, a_ref, b_ref, h_ref, parts_ref, sent_ref, place_ref, w_ref, sems,
):
    rows = x_ref.shape[0]
    units = h_ref.shape[0]
    block = rows // CHUNKS
    pairs = [(w_hbm.at[pl.ds(0, 2 * units)], w_ref.at[pl.ds(0, 2 * units)])]
    for c in range(CHUNKS):
        part = pl.ds(c * block, block)
        pairs.append((x_hbm.at[part], x_ref.at[part]))
        if c == 0:
            down = pl.ds(2 * units, units)
            pairs.append((w_hbm.at[down], w_ref.at[down]))
        pairs.append((r_hbm.at[part], r_ref.at[part]))
    copies = [pltpu.make_async_copy(*pair, sems.at[k]) for k, pair in enumerate(pairs)]

    def arrive(k):
        copies[k].wait()
        if k + AHEAD < len(copies):
            copies[k + AHEAD].start()

    for copy in copies[:AHEAD]:
        copy.start()

    count = fwd_ref.shape[0]
    span = sent_ref.shape[0]
    slots = 2 * count // CAPACITY
    route = route_ref[...]
    named = route == lax.broadcasted_iota(jnp.int32, (slots, count), 0)
    before = lax.broadcasted_iota(jnp.int32, (count, count), 0) < lax.broadcasted_iota(
        jnp.int32, (count, count), 1
    )
    earlier = dot(jnp.where(named, 1.0, 0.0).astype(BF), jnp.where(before, 1.0, 0.0).astype(BF))
    position = jnp.sum(jnp.where(named, earlier, 0.0), axis=0, keepdims=True)
    place = route * CAPACITY + position.astype(jnp.int32)
    place_ref[...] = place
    hit = place == lax.broadcasted_iota(jnp.int32, (span, count), 0)
    sent_ref[...] = dot(jnp.where(hit, 1.0, 0.0).astype(BF), fwd_ref[...]).astype(BF)

    arrive(0)
    terms = []
    for c in range(CHUNKS):
        cols = slice(c * block, (c + 1) * block)
        arrive(2 * c + 1 + (c > 0))
        both = dot(w_ref[0 : 2 * units], x_ref[cols], NT)
        if c == 0:
            arrive(2)
        arrive(2 * c + 3)
        dh = dot(w_ref[2 * units :], r_ref[cols], NT)
        gate, up = both[:units], both[units:]
        sigma = jax.nn.sigmoid(gate)
        hidden = (gate * sigma * up).astype(BF)
        h_ref[:, cols] = hidden
        term = jnp.sum(hidden.astype(F32) * dh, axis=0, keepdims=True) - 0.25 * log_ref[:, cols]
        terms += [term[:, k * LANES : (k + 1) * LANES] for k in range(block // LANES)]
        a_ref[:, cols] = dh * up * sigma * (1.0 + gate * (1.0 - sigma))
        b_ref[:, cols] = dh * gate * sigma
    term = jnp.concatenate(terms, axis=0)
    for k in range(parts_ref.shape[0]):
        parts_ref[k] = term


def scores_call(own, inputs, direction, weights, ref_logratio, route, fwd_rows, everyone):
    rows, width = inputs.shape
    units = weights.shape[0] // 3
    span = 2 * fwd_rows.shape[0]
    hbm = pl.BlockSpec(memory_space=pltpu.HBM)
    vmem = pl.BlockSpec(memory_space=pltpu.VMEM)
    return pl.pallas_call(
        scores_kernel,
        in_specs=[pl.BlockSpec(memory_space=pltpu.SMEM), hbm, hbm, hbm, vmem, vmem, vmem],
        out_specs=[vmem] * 8,
        out_shape=[
            pltpu.VMEM((rows, width), BF),
            pltpu.VMEM((rows, width), BF),
            pltpu.VMEM((units, rows), F32),
            pltpu.VMEM((units, rows), F32),
            pltpu.VMEM((units, rows), BF),
            jax.ShapeDtypeStruct((everyone, rows // LANES, LANES), F32),
            pltpu.VMEM((span, fwd_rows.shape[1]), BF),
            jax.ShapeDtypeStruct((1, fwd_rows.shape[0]), jnp.int32),
        ],
        scratch_shapes=[
            pltpu.VMEM(weights.shape, BF),
            pltpu.SemaphoreType.DMA((2 * CHUNKS + 2,)),
        ],
        cost_estimate=pl.CostEstimate(
            flops=6 * rows * width * units, bytes_accessed=14 << 20, transcendentals=rows * units
        ),
        compiler_params=limits(48),
        name="scores",
    )(own, inputs, direction, weights, ref_logratio, route, fwd_rows)


def grads_kernel(own_ref, parts_ref, lab_ref, a_ref, b_ref, h_ref, sent_ref, r_ref, x_ref, out_ref, lhs, held):
    units, rows = a_ref.shape
    wide = 512
    slots = out_ref.shape[0]
    center = jnp.sum(parts_ref[...]) / (slots * rows)
    hids = parts_ref.shape[0] // slots
    q = jax.nn.sigmoid(jnp.sum(parts_ref[pl.ds(own_ref[0] * hids, hids)], axis=0) - center)
    slope = q * (1.0 - q) * jnp.where(lab_ref[...] == 1, -desired_weight, undesired_weight)
    for k, term in enumerate((a_ref, b_ref, h_ref)):
        for i in range(rows // LANES):
            cols = slice(i * LANES, (i + 1) * LANES)
            lhs[k * units : (k + 1) * units, cols] = (
                term[:, cols].astype(F32) * slope[i : i + 1]
            ).astype(BF)

    @pl.loop(0, x_ref.shape[1] // wide)
    def _(step):
        cols = pl.ds(pl.multiple_of(step * wide, wide), wide)
        held[0 : 2 * units, cols] = dot(lhs[0 : 2 * units], x_ref[:, cols]).astype(BF)
        held[2 * units :, cols] = dot(lhs[2 * units :], r_ref[:, cols]).astype(BF)

    swap = swap_map(16, 16)
    for k in range(3):
        for pair in range(units // 32):
            halves = []
            for half in range(2):
                base = k * units + (2 * pair + half) * 16
                tiles = [held[base : base + 16, j * LANES : (j + 1) * LANES] for j in range(16)]
                halves.append(jnp.concatenate(tiles, axis=0))
            both = dot(swap, jnp.concatenate(halves, axis=1)).astype(BF)
            for half in range(2):
                for p in range(8):
                    at = (2 * pair + half) * 256 + p * 32
                    top = k * 96 + at % 96
                    out_ref[at // 96, top : top + 32] = both[
                        p * 32 : (p + 1) * 32, half * LANES : (half + 1) * LANES
                    ]
    for s in range(slots):
        for j in range(sent_ref.shape[1] // LANES):
            top = 288 + j * CAPACITY
            out_ref[s, top : top + CAPACITY] = sent_ref[
                s * CAPACITY : (s + 1) * CAPACITY, j * LANES : (j + 1) * LANES
            ]


def grads_call(own, parts, labels, a, b, h, sent, direction, inputs, slots):
    units, rows = a.shape
    width = inputs.shape[1]
    vmem = pl.BlockSpec(memory_space=pltpu.VMEM)
    return pl.pallas_call(
        grads_kernel,
        in_specs=[pl.BlockSpec(memory_space=pltpu.SMEM)] + [vmem] * 8,
        out_specs=vmem,
        out_shape=jax.ShapeDtypeStruct((slots, 288 + 4 * CAPACITY, LANES), BF),
        scratch_shapes=[pltpu.VMEM((3 * units, rows), BF), pltpu.VMEM((3 * units, width), BF)],
        cost_estimate=pl.CostEstimate(
            flops=6 * rows * width * units, bytes_accessed=12 << 20, transcendentals=rows
        ),
        compiler_params=limits(24),
        name="grads",
    )(own, parts, labels, a, b, h, sent, direction, inputs)


def adam_step(pc_ref, arr_ref, ms_ref, m1_ref, m2_ref, total, fresh, outs=None):
    for sums in total:
        sums[...] = jnp.zeros_like(sums)
    for s in range(arr_ref.shape[0]):
        total[s % len(total)][pc_ref[s]] += arr_ref[s].astype(F32)
    for e in range(fresh.shape[0]):
        grad = functools.reduce(jnp.add, [sums[e] for sums in total])
        master = ms_ref[e, 0]
        new_first = decay_first * m1_ref[e, 0] + (1.0 - decay_first) * grad
        new_second = decay_second * m2_ref[e, 0] + (1.0 - decay_second) * grad * grad
        size = jnp.sqrt(new_second * (1.0 / correct_second)) + adam_eps
        update = new_first * (1.0 / correct_first) / size
        new_master = master - learn_rate * (update + weight_decay * master)
        if outs is not None:
            outs[0][e, 0] = new_master
            outs[1][e, 0] = new_first
            outs[2][e, 0] = new_second
        fresh[e] = new_master.astype(BF)


def adam_pick_kernel(info_ref, pc_ref, pn_ref, arr_ref, ms, m1, m2, pick_ref, p0, p1, p2, p3, t0, t1, fresh, turned):
    adam_step(pc_ref, arr_ref, ms, m1, m2, (t0, t1), fresh)
    step = pl.program_id(0)

    @pl.when(step < 2)
    def _():
        for t in range(pick_ref.shape[0]):
            pick_ref[t] = fresh[pn_ref[t]]

    @pl.when(step >= 2)
    def _():
        experts = fresh.shape[0]
        side = jnp.concatenate([fresh[e] for e in range(experts)], axis=1)
        turned[...] = dot(piece_map(), side).reshape(turned.shape)
        for k, piece_ref in enumerate((p0, p1, p2, p3)):
            mine = turned[info_ref[5 + k]]
            for e in range(experts):
                piece_ref[e] = mine[:, e * LANES : (e + 1) * LANES].astype(BF)


def adam_full_kernel(pc_ref, arr_ref, ms, m1, m2, om, o1, o2, t0, t1, fresh):
    adam_step(pc_ref, arr_ref, ms, m1, m2, (t0, t1), fresh, (om, o1, o2))


def adam_call(info, place_cur, place_next, arrived, states, full):
    slots = arrived.shape[0]
    experts, _, lines, _ = states[0].shape
    block = lines
    steps = lines // block
    smem = pl.BlockSpec(memory_space=pltpu.SMEM)
    state = pl.BlockSpec((experts, 1, block, LANES), lambda i: (0, i // steps, i % steps, 0))
    piece = pl.BlockSpec((slots, block, LANES), lambda i: (0, i, 0))
    scratch = [pltpu.VMEM((experts, block, LANES), t) for t in (F32, F32, BF)]
    cost = pl.CostEstimate(flops=20 << 20, bytes_accessed=6 << 20, transcendentals=0)
    if not full:
        return pl.pallas_call(
            adam_pick_kernel,
            grid=(3 * steps,),
            in_specs=[smem, smem, smem, piece, state, state, state],
            out_specs=[pl.BlockSpec((slots, block, LANES), lambda i: (0, jnp.minimum(i, 1), 0))]
            + [single((experts, lines // 4, LANES))] * 4,
            out_shape=[pltpu.HBM((slots, 2 * lines, LANES), BF)]
            + [jax.ShapeDtypeStruct((experts, lines // 4, LANES), BF)] * 4,
            scratch_shapes=scratch + [pltpu.VMEM((4, lines // 4, experts * LANES), F32)],
            cost_estimate=cost,
            compiler_params=limits(18),
            name="adam_pick",
        )(info, place_cur, place_next, arrived, *states)
    return pl.pallas_call(
        adam_full_kernel,
        grid=(3 * steps,),
        in_specs=[smem, piece, state, state, state],
        out_specs=[state, state, state],
        out_shape=[jax.ShapeDtypeStruct(s.shape, F32) for s in states],
        scratch_shapes=scratch,
        cost_estimate=cost,
        compiler_params=limits(60),
        name="adam_full",
    )(place_cur, arrived, *states)


def pick_kernel(pn_ref, p0, p1, p2, p3, out_ref):
    for t in range(out_ref.shape[0]):
        expert = pn_ref[t]
        own = [p[expert].astype(F32) for p in (p0, p1, p2, p3)]
        for a in range(3):
            out_ref[t, a * 32 : (a + 1) * 32] = jnp.concatenate(
                [v[a * 8 : (a + 1) * 8] for v in own], axis=0
            ).astype(BF)


def pick_call(place_next, pieces):
    slots = place_next.shape[0]
    shape = (slots, 4 * pieces[0].shape[1], LANES)
    return pl.pallas_call(
        pick_kernel,
        grid=(1,),
        in_specs=[pl.BlockSpec(memory_space=pltpu.SMEM)] + [whole(p.shape) for p in pieces],
        out_specs=whole(shape),
        out_shape=jax.ShapeDtypeStruct(shape, BF),
        cost_estimate=pl.CostEstimate(flops=1 << 20, bytes_accessed=2 << 20, transcendentals=0),
        compiler_params=limits(16),
        name="pick",
    )(place_next, *pieces)


def hidden_kernel(q_ref, w_ref, r0, r1, r2, r3, out_ref, mat):
    units = out_ref.shape[0]
    swap = swap_map(16, 16)
    for group in range(4):
        for a in range(3):
            both = jnp.concatenate(
                [
                    w_ref[group * 8 : group * 8 + 8, m * 96 + a * 32 : m * 96 + a * 32 + 32].reshape(
                        256, LANES
                    )
                    for m in range(2)
                ],
                axis=1,
            )
            turned = dot(swap, both).astype(BF)
            for m in range(2):
                top = m * units + (group * 3 + a) * 16
                for j in range(16):
                    mat[top : top + 16, j * LANES : (j + 1) * LANES] = turned[
                        j * 16 : (j + 1) * 16, m * LANES : (m + 1) * LANES
                    ]
    total = None
    for k, rows in enumerate((r0, r1, r2, r3)):
        quarter = rows.shape[1]
        start = pl.multiple_of(q_ref[1 + k] * quarter, quarter)
        term = dot(mat[:, pl.ds(start, quarter)], rows[...], NT)
        total = term if total is None else total + term
    gate, up = total[:units], total[units:]
    out_ref[...] = (gate * jax.nn.sigmoid(gate) * up).astype(BF)


def hidden_call(quarters, packed, rows):
    units = packed.shape[0] * 6
    count, quarter = rows[0].shape
    return pl.pallas_call(
        hidden_kernel,
        grid=(1,),
        in_specs=[pl.BlockSpec(memory_space=pltpu.SMEM), whole(packed.shape)]
        + [whole(r.shape) for r in rows],
        out_specs=whole((units, count)),
        out_shape=jax.ShapeDtypeStruct((units, count), BF),
        scratch_shapes=[pltpu.VMEM((2 * units, 4 * quarter), BF)],
        cost_estimate=pl.CostEstimate(
            flops=16 * count * quarter * units, bytes_accessed=4 << 20, transcendentals=count * units
        ),
        compiler_params=limits(24),
        name="hidden",
    )(quarters, packed, *rows)


def unpack_kernel(w_ref, out_ref):
    swap = swap_map(16, 16)
    lines = w_ref.shape[1]
    row = lax.broadcasted_iota(jnp.int32, (256, 256), 0)
    col = lax.broadcasted_iota(jnp.int32, (256, 256), 1)
    k, j, s, b = row // 64, row // 16 % 4, row // 2 % 8, row % 2
    turn = jnp.where(col == ((s * 4 + k) * 2 + b) * 4 + j, 1.0, 0.0).astype(BF)
    for group in range(4):
        for a in range(lines // 32):
            turned = dot(
                turn, w_ref[group * 8 : group * 8 + 8, a * 32 : a * 32 + 32].reshape(256, LANES)
            ).astype(BF)
            top = (group * 3 + a) * 16
            for k in range(4):
                for j in range(4):
                    at = (k * 4 + j) * 16
                    out_ref[k, top : top + 16, j * LANES : (j + 1) * LANES] = turned[at : at + 16]


def unpack_call(packed):
    shape = (4, packed.shape[0] * 6, 4 * LANES)
    return pl.pallas_call(
        unpack_kernel,
        grid=(1,),
        in_specs=[whole(packed.shape)],
        out_specs=whole(shape),
        out_shape=jax.ShapeDtypeStruct(shape, BF),
        cost_estimate=pl.CostEstimate(flops=1 << 28, bytes_accessed=2 << 20, transcendentals=0),
        compiler_params=limits(16),
        name="unpack",
    )(packed)


def down_kernel(w_ref, h0, h1, h2, h3, out_ref):
    total = None
    for k, h in enumerate((h0, h1, h2, h3)):
        term = dot(h[...], w_ref[k], TN)
        total = term if total is None else total + term
    out_ref[...] = total.astype(BF)


def down_call(weights, hidden):
    units, count = hidden[0].shape
    quarter = weights.shape[2]
    return pl.pallas_call(
        down_kernel,
        grid=(1,),
        in_specs=[whole(weights.shape)] + [whole(h.shape) for h in hidden],
        out_specs=whole((count, quarter)),
        out_shape=jax.ShapeDtypeStruct((count, quarter), BF),
        cost_estimate=pl.CostEstimate(
            flops=8 * count * quarter * units, bytes_accessed=3 << 20, transcendentals=0
        ),
        compiler_params=limits(16),
        name="down",
    )(weights, *hidden)


def shards(
    master,
    first_moment,
    second_moment,
    slot_weights,
    back_rows,
    readout,
    ref_logratio,
    labels,
    place_cur,
    place_next,
    fwd_rows,
    routes,
):
    slot_count = lax.axis_size("slot")
    hid_count = lax.axis_size("hid")
    hid_index = lax.axis_index("hid").astype(jnp.int32)
    _, width = back_rows.shape[1:]

    def pass_on(value, k):
        return lax.ppermute(value, "hid", [(i, (i + k) % hid_count) for i in range(hid_count)])

    def exchange(value):
        return lax.all_to_all(value, "slot", split_axis=0, concat_axis=0, tiled=True)

    capacity = CAPACITY
    quarter = fwd_rows.shape[1]
    everyone = slot_count * hid_count
    turns = jnp.arange(hid_count, dtype=jnp.int32)
    info = jnp.concatenate(
        [
            lax.axis_index("slot").astype(jnp.int32).reshape(1),
            (hid_index + hid_count - turns) % hid_count,
            (hid_index + turns) % hid_count,
        ]
    )
    inputs, direction, a, b, h, part, sent, slot_place = scores_call(
        info, back_rows[0], readout[0], slot_weights.reshape(-1, width), ref_logratio,
        routes.reshape(1, -1), fwd_rows, everyone,
    )
    parts = lax.all_to_all(part, ("slot", "hid"), split_axis=0, concat_axis=0, tiled=True)
    blocks = grads_call(
        info, parts, labels.reshape(part.shape[1:]), a, b, h, sent, direction, inputs, slot_count
    )
    arrived = exchange(blocks)

    lines = 96
    shape = (master.shape[0], 3, lines, LANES)
    states = [v.reshape(shape) for v in (master, first_moment, second_moment)]
    picked, *pieces = adam_call(info, place_cur, place_next, arrived, states, False)
    gate_up = exchange(picked)
    pieces = [pieces[0]] + [pass_on(pieces[k], k) for k in range(1, hid_count)]
    down = pick_call(place_next, pieces)
    down = exchange(down)

    own_rows = arrived[:, 3 * lines :].reshape(slot_count, quarter // LANES, capacity, LANES)
    own_rows = own_rows.transpose(0, 2, 1, 3).reshape(slot_count * capacity, quarter)
    all_rows = [own_rows] + [pass_on(own_rows, k) for k in range(1, hid_count)]
    held = adam_call(info, place_cur, place_next, arrived, states, True)

    hidden = hidden_call(info, gate_up, all_rows)
    hidden = [hidden] + [pass_on(hidden, k) for k in range(1, hid_count)]
    produced = down_call(unpack_call(down), hidden)
    returned = exchange(produced.reshape(slot_count, capacity, quarter))
    place_map = (
        slot_place == jnp.arange(slot_count * capacity, dtype=jnp.int32)[:, None]
    ).astype(BF)
    out_rows = lax.dot_general(
        place_map,
        returned.reshape(slot_count * capacity, quarter),
        (((0,), (0,)), ((), ())),
        preferred_element_type=F32,
    ).astype(BF)
    return (out_rows, *[v.reshape(master.shape) for v in held])


def solution(mesh):
    shard = P(None, None, "hid", "slot")
    return jax.shard_map(
        shards,
        mesh=mesh,
        in_specs=(
            shard,
            shard,
            shard,
            P("slot", None, "hid", None),
            P("slot", None, None),
            P("slot", None, None),
            P("slot", None),
            P("slot", None),
            P(),
            P(),
            P("slot", "hid"),
            P("slot", None),
        ),
        out_specs=(P("slot", "hid"), shard, shard, shard),
        check_vma=False,
    )
```

time: 183 us -> 161 us (0.88)
  local copies, waits for them, and re-layouts: 26 us -> 0.43 us
  starting transfers between devices: 35.8 us -> 24 us
  Pallas kernels: 24.8 us -> 34.3 us
  blocking collectives: 60 us -> 66.3 us
    all_to_all x0 -> x1, blocking collectives: none -> 25.6 us  [shards(): lax.all_to_all(part, ('slot', 'hid'), split_axis=0, concat_axis=0, tiled=...]
    unnamed x53 -> x19, local copies, waits for them, and re-layouts: 24.4 us -> 0.13 us
    all_to_all x2 -> x1, blocking collectives: 60 us -> 40.7 us  [exchange(): lax.all_to_all(value, 'slot', split_axis=0, concat_axis=0, tiled=True)]
    all_to_all x3, waiting for transfers between devices: 10.4 us -> 20 us  [exchange(): lax.all_to_all(value, 'slot', split_axis=0, concat_axis=0, tiled=True)]
    ppermute x12 -> x9, waiting for transfers between devices: 21.6 us -> 12.8 us  [pass_on(): lax.ppermute(value, 'hid', [(i, (i + k) % hid_count) for i in range(hid_c...]
    pallas_call x4, Pallas kernels: 18.8 us -> 27.7 us  [the longest x1 8.91 us: adam_call(): pl.pallas_call(adam_full_kernel, grid=(3 * steps,), in_specs=[smem, piece...]
    ppermute x12 -> x9, starting transfers between devices: 16.3 us -> 8 us  [pass_on(): lax.ppermute(value, 'hid', [(i, (i + k) % hid_count) for i in range(hid_c...]
    all_to_all x3, starting transfers between devices: 19.5 us -> 16 us  [exchange(): lax.all_to_all(value, 'slot', split_axis=0, concat_axis=0, tiled=True)]
  transfers between devices with their start and end apart: 15 -> 12, of which waited for: 10 -> 8; matrix products, arithmetic and copies ran while one was open for 1% -> 0% of each run, Pallas kernels for 5% -> 9%
where the time goes in v3:
time: 161 us; the launch traced here: 160 us
  blocking collectives  66.3 us (41%)
  Pallas kernels  34.3 us (21%)
  waiting for transfers between devices  32.8 us (20%)
  starting transfers between devices  24 us (15%)
    all_to_all x1, blocking collectives, exchange(): lax.all_to_all(value, 'slot', split_axis=0, concat_axis=0, tiled=True)  40.7 us
    all_to_all x1, blocking collectives, shards(): lax.all_to_all(part, ('slot', 'hid'), split_axis=0, concat_axis=0, tiled=...  25.6 us
    all_to_all x3, waiting for transfers between devices, exchange(): lax.all_to_all(value, 'slot', split_axis=0, concat_axis=0, tiled=True)  20 us
    all_to_all x3, starting transfers between devices, exchange(): lax.all_to_all(value, 'slot', split_axis=0, concat_axis=0, tiled=True)  16 us
    ppermute x9, waiting for transfers between devices, pass_on(): lax.ppermute(value, 'hid', [(i, (i + k) % hid_count) for i in range(hid_c...  12.8 us
    pallas_call x1, Pallas kernels, adam_call(): pl.pallas_call(adam_full_kernel, grid=(3 * steps,), in_specs=[smem, piece...  8.91 us
    pallas_call x1, Pallas kernels, scores_call(): pl.pallas_call(scores_kernel, in_specs=[pl.BlockSpec(memory_space=pltpu.S...  8.11 us
    ppermute x9, starting transfers between devices, pass_on(): lax.ppermute(value, 'hid', [(i, (i + k) % hid_count) for i in range(hid_c...  8 us
  transfers between devices with their start and end apart: 12, of which 8 were waited for; matrix products, arithmetic and copies ran while one was open for 0% of the time, Pallas kernels for 9%

profile of v3, /device:TPU:1, one launch (start us, length us, event | category | flops | bytes accessed | tf_op | source)
XLA Modules:
  0.0 160.3 jit_solution(3296546618392860874)
XLA Ops:
  0.7 0.6 pad_add_fusion.own_ref.info_ref.q_ref
  1.2 8.1 %scores.1 = (bf16[1024,2048]{1,0:T(8,128)(2,1)S(1)}, bf16[1024,2048]{1,0:T(8,128)(2,1)S(1)}, f32[192,1024]{1,0:T(8,128)S(1)}, f32[192,1024]{1,0:T(8,128)S(1)}, b...) custom-call(s32[9]{0:T(128)} %pad_add_fusion.own_ref.info_ref.q_ref, ...), custom_call_target="tpu_custom_call" | custom-call | flops 2415919104 | bytes 14680064 | tf_op jit(solution)/shard_map/scores/pallas_call | solution.py:130
  9.4 25.6 %all_to_all.25.parts_ref = f32[128,8,128]{2,1,0:T(8,128)S(1)} all-to-all(f32[128,8,128]{2,1,0:T(8,128)} %get-tuple-element.21), channel_id=1, replica_groups=mesh['slot'=32,'hid'=4] {'slot','hid'}, dimensions={0} | all-to-all | bytes 1048576 | tf_op jit(solution)/shard_map/all_to_all | solution.py:473
  35.0 5.1 %grads.1 = bf16[32,352,128]{2,1,0:T(8,128)(2,1)S(1)} custom-call(s32[9]{0:T(128)S(1)} %copy-done.4, f32[128,8,128]{2,1,0:T(8,128)S(1)} %all_to_all.25.parts_ref, s32[8,128]{1,0:T(8,128)S(1)} %bitcast.34, f32[192,1024]{1,0:T(8,128)S(1)} %get-tuple-element.22.a_ref, f32[192,1024]{1,0:T(8,128)S(1)} %get-tuple-element.23.b_ref, ...), custom_call_target="tpu_custom_call" | custom-call | flops 2415919104 | bytes 12582912 | tf_op jit(solution)/shard_map/grads/pallas_call | solution.py:205
  40.2 40.7 %all_to_all.26.arr_ref = bf16[32,352,128]{2,1,0:T(8,128)(2,1)S(1)} all-to-all(bf16[32,352,128]{2,1,0:T(8,128)(2,1)S(1)} %grads.1), channel_id=1, replica_groups=mesh['slot'=32,'hid'=4] {'slot'}, dimensions={0} | all-to-all | bytes 5767168 | tf_op jit(solution)/shard_map/all_to_all | solution.py:456
  80.9 5.5 %adam_pick.1 = (bf16[32,192,128]{2,1,0:T(8,128)(2,1)}, bf16[16,24,128]{2,1,0:T(8,128)(2,1)S(1)}, bf16[16,24,128]{2,1,0:T(8,128)(2,1)S(1)}, bf16[16,24,128]{2,1,0:T(8,128)(2,1)S(1)}, bf16[16,24,128]{2,1,0:T(8,128)(2,1)S(1)}) custom-call(s32[9]{0:T(128)S(1)} %copy-done.4, s32[32]{0:T(128)S(1)} %copy-done.7, s32[32]{0:T(128)S(1)} %copy-done.6, ...), custom_call_target="tpu_custom_call" | custom-call | flops 20971520 | bytes 6291456 | tf_op jit(solution)/shard_map/adam_pick/pallas_call | solution.py:274
  86.4 4.5 %all-to-all-start.3 = ((bf16[32,192,128]{2,1,0:T(8,128)(2,1)}), bf16[32,192,128]{2,1,0:T(8,128)(2,1)}, u32[]{:S(2)}, u32[]{:S(2)}) async-start(bf16[32,192,128]{2,1,0:T(8,128)(2,1)} %get-tuple-element.32), calls=%async_computation.3 | async-start | bytes 3145728 | tf_op jit(solution)/shard_map/all_to_all | solution.py:456
  90.9 0.4 collective-permute-start
  91.3 1.4 collective-permute-start.1
  92.8 1.0 collective-permute-start.2
  93.9 0.3 copy.20
  94.1 0.1 copy.35
  94.2 0.8 collective-permute-start.5
  95.1 1.5 collective-permute-start.4
  96.6 2.0 %collective-permute-done.p1 = bf16[16,24,128]{2,1,0:T(8,128)(2,1)S(1)} collective-permute-done((bf16[16,24,128]{2,1,0:T(8,128)(2,1)S(1)}, bf16[16,24,128]{2,1,0:T(8,128)(2,1)S(1)}, u32[]{:S(2)}, u32[]{:S(2)}) %collective-permute-start) | collective-permute-done | bytes 98336 | tf_op jit(solution)/shard_map/ppermute | solution.py:453
  98.6 0.3 collective-permute-done.2.p3
  99.0 1.6 pick.1
  100.6 12.9 %all-to-all-done.3.w_ref = bf16[32,192,128]{2,1,0:T(8,128)(2,1)} async-done(((bf16[32,192,128]{2,1,0:T(8,128)(2,1)}), bf16[32,192,128]{2,1,0:T(8,128)(2,1)}, u32[]{:S(2)}, u32[]{:S(2)}) %all-to-all-start.3) | async-done | bytes 1572896 | tf_op jit(solution)/shard_map/all_to_all | solution.py:456
  113.4 4.1 %all-to-all-start.2 = ((bf16[32,96,128]{2,1,0:T(8,128)(2,1)}), bf16[32,96,128]{2,1,0:T(8,128)(2,1)S(1)}, u32[]{:S(2)}, u32[]{:S(2)}) async-start(bf16[32,96,128]{2,1,0:T(8,128)(2,1)} %pick.1), calls=%async_computation.2 | async-start | bytes 1572864 | tf_op jit(solution)/shard_map/all_to_all | solution.py:456
  117.6 4.2 %collective-permute-done.3.r1 = bf16[512,512]{1,0:T(8,128)(2,1)S(1)} collective-permute-done((bf16[512,512]{1,0:T(8,128)(2,1)S(1)}, bf16[512,512]{1,0:T(8,128)(2,1)S(1)}, u32[]{:S(2)}, u32[]{:S(2)}) %collective-permute-start.3) | collective-permute-done | bytes 524320 | tf_op jit(solution)/shard_map/ppermute | solution.py:453
  121.8 2.9 %hidden.1.h0 = bf16[192,512]{1,0:T(8,128)(2,1)S(1)} custom-call(s32[9]{0:T(128)S(1)} %copy-done.4, bf16[32,192,128]{2,1,0:T(8,128)(2,1)} %all-to-all-done.3.w_ref, bf16[512,512]{1,0:T(8,128)(2,1)S(1)} %bitcast.33, bf16[512,512]{1,0:T(8,128)(2,1)S(1)} %collective-permute-done.3.r1, bf16[512,512]{1,0:T(8,128)(2,1)S(1)} %collective-permute-done.4.r2, ...), custom_call_target="tpu_custom_call" | custom-call | flops 805306368 | bytes 4194304 | tf_op jit(solution)/shard_map/hidden/pallas_call | solution.py:359
  124.7 2.1 %collective-permute-start.8 = (bf16[192,512]{1,0:T(8,128)(2,1)S(1)}, bf16[192,512]{1,0:T(8,128)(2,1)S(1)}, u32[]{:S(2)}, u32[]{:S(2)}) collective-permute-start(bf16[192,512]{1,0:T(8,128)(2,1)S(1)} %hidden.1.h0), channel_id=1, source_target_pairs={{0,3},{1,0},{2,1},{3,2},{4,7},{5,4},{6,5},{7,6},{8,11},{9,8},{10,9... | collective-permute-start | bytes 589832 | tf_op jit(solution)/shard_map/ppermute | solution.py:453
  126.8 0.7 collective-permute-start.6
  127.4 4.5 %all-to-all-done.2.w_ref = bf16[32,96,128]{2,1,0:T(8,128)(2,1)S(1)} async-done(((bf16[32,96,128]{2,1,0:T(8,128)(2,1)}), bf16[32,96,128]{2,1,0:T(8,128)(2,1)S(1)}, u32[]{:S(2)}, u32[]{:S(2)}) %all-to-all-start.2) | async-done | bytes 786464 | tf_op jit(solution)/shard_map/all_to_all | solution.py:456
  131.9 0.6 unpack.1.w_ref
  132.5 0.8 collective-permute-done.7.h2
  133.3 5.5 %collective-permute-done.6.h1 = bf16[192,512]{1,0:T(8,128)(2,1)S(1)} collective-permute-done((bf16[192,512]{1,0:T(8,128)(2,1)S(1)}, bf16[192,512]{1,0:T(8,128)(2,1)S(1)}, u32[]{:S(2)}, u32[]{:S(2)}) %collective-permute-start.6) | collective-permute-done | bytes 196640 | tf_op jit(solution)/shard_map/ppermute | solution.py:453
  138.7 1.6 down.1
  140.3 7.4 %all-to-all-start.4 = ((bf16[32,16,512]{2,1,0:T(8,128)(2,1)}), bf16[32,16,512]{2,1,0:T(8,128)(2,1)S(1)}, u32[]{:S(2)}, u32[]{:S(2)}) async-start(bf16[32,16,512]{2,1,0:T(8,128)(2,1)} %bitcast.12), calls=%async_computation.4 | async-start | bytes 1048576 | tf_op jit(solution)/shard_map/all_to_all | solution.py:456
  147.7 8.9 %adam_full.1 = (f32[16,3,96,128]{3,2,1,0:T(8,128)}, f32[16,3,96,128]{3,2,1,0:T(8,128)}, f32[16,3,96,128]{3,2,1,0:T(8,128)}) custom-call(s32[32]{0:T(128)} %pc_ref.3, bf16[32,352,128]{2,1,0:T(8,128)(2,1)} %copy-done, f32[16,3,96,128]{3,2,1,0:T(8,128)} %bitcast.24, f32[16,3,96,128]{3,2,1,0:T(8,128)} %bitcast.26, f32[16,3,96,128]{3,2,1,0:T(8,128)} %bitcast.28), custom_call_target="tpu_custom_call" | custom-call | flops 20971520 | bytes 6291456 | tf_op jit(solution)/shard_map/adam_full/pallas_call | solution.py:287
  156.6 2.7 %all-to-all-done.4 = bf16[32,16,512]{2,1,0:T(8,128)(2,1)S(1)} async-done(((bf16[32,16,512]{2,1,0:T(8,128)(2,1)}), bf16[32,16,512]{2,1,0:T(8,128)(2,1)S(1)}, u32[]{:S(2)}, u32[]{:S(2)}) %all-to-all-start.4) | async-done | bytes 524320 | tf_op jit(solution)/shard_map/all_to_all | solution.py:456
  159.3 1.1 convolution_convert_fusion
  (26 shorter events, 0.1 us)
Async XLA Ops:
  1.2 33.7 %copy-start.4 = (s32[9]{0:T(128)S(1)}, s32[9]{0:T(128)}, u32[]{:S(2)}) copy-start(s32[9]{0:T(128)} %pad_add_fusion.own_ref.info_ref.q_ref) | copy-start | bytes 112
  1.2 33.7 %copy-start.5 = (s32[1,1024]{1,0:T(1,128)S(1)}, s32[1,1024]{1,0:T(1,128)}, u32[]{:S(2)}) copy-start(s32[1,1024]{1,0:T(1,128)} %param.19) | copy-start | bytes 12292
  35.0 45.9 %copy-start.3 = (f32[16,3,1,12288]{3,2,1,0:T(1,128)S(1)}, f32[16,3,1,12288]{3,2,1,0:T(1,128)}, u32[]{:S(2)}) copy-start(f32[16,3,1,12288]{3,2,1,0:T(1,128)} %param.14) | copy-start | bytes 7077892
  40.1 40.8 %copy-start.1 = (f32[16,3,1,12288]{3,2,1,0:T(1,128)S(1)}, f32[16,3,1,12288]{3,2,1,0:T(1,128)}, u32[]{:S(2)}) copy-start(f32[16,3,1,12288]{3,2,1,0:T(1,128)} %param.12) | copy-start | bytes 7077892
  40.1 40.8 %copy-start.2 = (f32[16,3,1,12288]{3,2,1,0:T(1,128)S(1)}, f32[16,3,1,12288]{3,2,1,0:T(1,128)}, u32[]{:S(2)}) copy-start(f32[16,3,1,12288]{3,2,1,0:T(1,128)} %param.13) | copy-start | bytes 7077892
  40.1 40.8 %copy-start.6 = (s32[32]{0:T(128)S(1)}, s32[32]{0:T(128)}, u32[]{:S(2)}) copy-start(s32[32]{0:T(128)} %pn_ref.3) | copy-start | bytes 388
  40.2 40.7 %copy-start.7 = (s32[32]{0:T(128)S(1)}, s32[32]{0:T(128)}, u32[]{:S(2)}) copy-start(s32[32]{0:T(128)} %pc_ref.3) | copy-start | bytes 388
  80.9 12.9 %copy-start = (bf16[32,352,128]{2,1,0:T(8,128)(2,1)}, bf16[32,352,128]{2,1,0:T(8,128)(2,1)S(1)}, u32[]{:S(2)}) copy-start(bf16[32,352,128]{2,1,0:T(8,128)(2,1)S(1)} %all_to_all.26.arr_ref) | copy-start | bytes 8650756
  86.4 27.0 %all-to-all-start.3 = ((bf16[32,192,128]{2,1,0:T(8,128)(2,1)}), bf16[32,192,128]{2,1,0:T(8,128)(2,1)}, u32[]{:S(2)}, u32[]{:S(2)}) async-start(bf16[32,192,128]{2,1,0:T(8,128)(2,1)} %get-tuple-element.32), calls=%async_computation.3 | async-start | bytes 3145728 | tf_op jit(solution)/shard_map/all_to_all | solution.py:456
  90.9 7.7 %collective-permute-start = (bf16[16,24,128]{2,1,0:T(8,128)(2,1)S(1)}, bf16[16,24,128]{2,1,0:T(8,128)(2,1)S(1)}, u32[]{:S(2)}, u32[]{:S(2)}) collective-permute-start(bf16[16,24,128]{2,1,0:T(8,128)(2,1)S(1)} %get-tuple-element.29), channel_id=1, source_target_pairs={{0,1},{1,2},{2,3},{3,0},{4,5},{5,6},{6,7},{7,4},{8,9},{9,10},{10,1... | collective-permute-start | bytes 294920 | tf_op jit(solution)/shard_map/ppermute | solution.py:453
  91.3 7.3 %collective-permute-start.1 = (bf16[16,24,128]{2,1,0:T(8,128)(2,1)S(1)}, bf16[16,24,128]{2,1,0:T(8,128)(2,1)S(1)}, u32[]{:S(2)}, u32[]{:S(2)}) collective-permute-start(bf16[16,24,128]{2,1,0:T(8,128)(2,1)S(1)} %get-tuple-element.30), channel_id=1, source_target_pairs={{0,2},{1,3},{2,0},{3,1},{4,6},{5,7},{6,4},{7,5},{8,10},{9,11},{10,... | collective-permute-start | bytes 294920 | tf_op jit(solution)/shard_map/ppermute | solution.py:453
  92.8 6.2 %collective-permute-start.2 = (bf16[16,24,128]{2,1,0:T(8,128)(2,1)S(1)}, bf16[16,24,128]{2,1,0:T(8,128)(2,1)S(1)}, u32[]{:S(2)}, u32[]{:S(2)}) collective-permute-start(bf16[16,24,128]{2,1,0:T(8,128)(2,1)S(1)} %get-tuple-element.31), channel_id=1, source_target_pairs={{0,3},{1,0},{2,1},{3,2},{4,7},{5,4},{6,5},{7,6},{8,11},{9,8},{10,9... | collective-permute-start | bytes 294920 | tf_op jit(solution)/shard_map/ppermute | solution.py:453
  94.2 23.3 %collective-permute-start.5 = (bf16[512,512]{1,0:T(8,128)(2,1)S(1)}, bf16[512,512]{1,0:T(8,128)(2,1)S(1)}, u32[]{:S(2)}, u32[]{:S(2)}) collective-permute-start(bf16[512,512]{1,0:T(8,128)(2,1)S(1)} %bitcast.30), channel_id=1, source_target_pairs={{0,3},{1,0},{2,1},{3,2},{4,7},{5,4},{6,5},{7,6},{8,11},{9,8},{10,9... | collective-permute-start | bytes 1572872 | tf_op jit(solution)/shard_map/ppermute | solution.py:453
  95.1 22.5 %collective-permute-start.4 = (bf16[512,512]{1,0:T(8,128)(2,1)S(1)}, bf16[512,512]{1,0:T(8,128)(2,1)S(1)}, u32[]{:S(2)}, u32[]{:S(2)}) collective-permute-start(bf16[512,512]{1,0:T(8,128)(2,1)S(1)} %bitcast.31), channel_id=1, source_target_pairs={{0,2},{1,3},{2,0},{3,1},{4,6},{5,7},{6,4},{7,5},{8,10},{9,11},{10,... | collective-permute-start | bytes 1572872 | tf_op jit(solution)/shard_map/ppermute | solution.py:453
  98.6 23.1 %collective-permute-start.3 = (bf16[512,512]{1,0:T(8,128)(2,1)S(1)}, bf16[512,512]{1,0:T(8,128)(2,1)S(1)}, u32[]{:S(2)}, u32[]{:S(2)}) collective-permute-start(bf16[512,512]{1,0:T(8,128)(2,1)S(1)} %bitcast.32), channel_id=1, source_target_pairs={{0,1},{1,2},{2,3},{3,0},{4,5},{5,6},{6,7},{7,4},{8,9},{9,10},{10,1... | collective-permute-start | bytes 1572872 | tf_op jit(solution)/shard_map/ppermute | solution.py:453
  113.4 18.4 %all-to-all-start.2 = ((bf16[32,96,128]{2,1,0:T(8,128)(2,1)}), bf16[32,96,128]{2,1,0:T(8,128)(2,1)S(1)}, u32[]{:S(2)}, u32[]{:S(2)}) async-start(bf16[32,96,128]{2,1,0:T(8,128)(2,1)} %pick.1), calls=%async_computation.2 | async-start | bytes 1572864 | tf_op jit(solution)/shard_map/all_to_all | solution.py:456
  124.7 7.8 %collective-permute-start.8 = (bf16[192,512]{1,0:T(8,128)(2,1)S(1)}, bf16[192,512]{1,0:T(8,128)(2,1)S(1)}, u32[]{:S(2)}, u32[]{:S(2)}) collective-permute-start(bf16[192,512]{1,0:T(8,128)(2,1)S(1)} %hidden.1.h0), channel_id=1, source_target_pairs={{0,3},{1,0},{2,1},{3,2},{4,7},{5,4},{6,5},{7,6},{8,11},{9,8},{10,9... | collective-permute-start | bytes 589832 | tf_op jit(solution)/shard_map/ppermute | solution.py:453
  126.8 6.5 %collective-permute-start.7 = (bf16[192,512]{1,0:T(8,128)(2,1)S(1)}, bf16[192,512]{1,0:T(8,128)(2,1)S(1)}, u32[]{:S(2)}, u32[]{:S(2)}) collective-permute-start(bf16[192,512]{1,0:T(8,128)(2,1)S(1)} %hidden.1.h0), channel_id=1, source_target_pairs={{0,2},{1,3},{2,0},{3,1},{4,6},{5,7},{6,4},{7,5},{8,10},{9,11},{10,... | collective-permute-start | bytes 589832 | tf_op jit(solution)/shard_map/ppermute | solution.py:453
  126.8 12.0 %collective-permute-start.6 = (bf16[192,512]{1,0:T(8,128)(2,1)S(1)}, bf16[192,512]{1,0:T(8,128)(2,1)S(1)}, u32[]{:S(2)}, u32[]{:S(2)}) collective-permute-start(bf16[192,512]{1,0:T(8,128)(2,1)S(1)} %hidden.1.h0), channel_id=1, source_target_pairs={{0,1},{1,2},{2,3},{3,0},{4,5},{5,6},{6,7},{7,4},{8,9},{9,10},{10,1... | collective-permute-start | bytes 589832 | tf_op jit(solution)/shard_map/ppermute | solution.py:453
  140.3 19.0 %all-to-all-start.4 = ((bf16[32,16,512]{2,1,0:T(8,128)(2,1)}), bf16[32,16,512]{2,1,0:T(8,128)(2,1)S(1)}, u32[]{:S(2)}, u32[]{:S(2)}) async-start(bf16[32,16,512]{2,1,0:T(8,128)(2,1)} %bitcast.12), calls=%async_computation.4 | async-start | bytes 1048576 | tf_op jit(solution)/shard_map/all_to_all | solution.py:456
  147.7 11.6 %copy-start.8 = (s32[1,256]{1,0:T(1,128)S(1)}, s32[1,256]{1,0:T(1,128)}, u32[]{:S(2)}) copy-start(s32[1,256]{1,0:T(1,128)} %get-tuple-element.20) | copy-start | bytes 3076

commit v4 on v3

--- a/solution.py
+++ b/solution.py
@@ -1,5 +1,3 @@
-import functools
-
 import jax
 import jax.numpy as jnp
 from jax import lax
@@ -46,12 +44,11 @@
     return jnp.where(col == (unit * 4 + q) * 4 + j, 1.0, 0.0).astype(BF)
 
 
-def whole(shape):
-    return pl.BlockSpec(shape, lambda *_: (0,) * len(shape))
-
-
-def single(shape):
-    return pl.BlockSpec(shape, lambda *_: (0,) * len(shape), pipeline_mode=pl.Buffered(1))
+VM = pl.BlockSpec(memory_space=pltpu.VMEM)
+
+
+def in_hbm(value):
+    return pltpu.with_memory_space_constraint(value, pltpu.HBM)
 
 
 def limits(mib):
@@ -59,7 +56,7 @@
 
 
 def scores_kernel(
-    own_ref, x_hbm, r_hbm, w_hbm, log_ref, route_ref, fwd_ref,
+    x_hbm, r_hbm, w_hbm, log_ref, route_ref, fwd_ref,
     x_ref, r_ref, a_ref, b_ref, h_ref, parts_ref, sent_ref, place_ref, w_ref, sems,
 ):
     rows = x_ref.shape[0]
@@ -121,7 +118,7 @@
         parts_ref[k] = term
 
 
-def scores_call(own, inputs, direction, weights, ref_logratio, route, fwd_rows, everyone):
+def scores_call(inputs, direction, weights, ref_logratio, route, fwd_rows, everyone):
     rows, width = inputs.shape
     units = weights.shape[0] // 3
     span = 2 * fwd_rows.shape[0]
@@ -129,7 +126,7 @@
     vmem = pl.BlockSpec(memory_space=pltpu.VMEM)
     return pl.pallas_call(
         scores_kernel,
-        in_specs=[pl.BlockSpec(memory_space=pltpu.SMEM), hbm, hbm, hbm, vmem, vmem, vmem],
+        in_specs=[hbm, hbm, hbm, vmem, vmem, vmem],
         out_specs=[vmem] * 8,
         out_shape=[
             pltpu.VMEM((rows, width), BF),
@@ -150,16 +147,16 @@
         ),
         compiler_params=limits(48),
         name="scores",
-    )(own, inputs, direction, weights, ref_logratio, route, fwd_rows)
-
-
-def grads_kernel(own_ref, parts_ref, lab_ref, a_ref, b_ref, h_ref, sent_ref, r_ref, x_ref, out_ref, lhs, held):
+    )(inputs, direction, weights, ref_logratio, route, fwd_rows)
+
+
+def grads_kernel(parts_ref, lab_ref, a_ref, b_ref, h_ref, sent_ref, r_ref, x_ref, out_ref, lhs, held):
     units, rows = a_ref.shape
     wide = 512
     slots = out_ref.shape[0]
     center = jnp.sum(parts_ref[...]) / (slots * rows)
     hids = parts_ref.shape[0] // slots
-    q = jax.nn.sigmoid(jnp.sum(parts_ref[pl.ds(own_ref[0] * hids, hids)], axis=0) - center)
+    q = jax.nn.sigmoid(jnp.sum(parts_ref[pl.ds(lax.axis_index("slot") * hids, hids)], axis=0) - center)
     slope = q * (1.0 - q) * jnp.where(lab_ref[...] == 1, -desired_weight, undesired_weight)
     for k, term in enumerate((a_ref, b_ref, h_ref)):
         for i in range(rows // LANES):
@@ -198,100 +195,141 @@
             ]
 
 
-def grads_call(own, parts, labels, a, b, h, sent, direction, inputs, slots):
+def grads_call(parts, labels, a, b, h, sent, direction, inputs, slots):
     units, rows = a.shape
     width = inputs.shape[1]
     vmem = pl.BlockSpec(memory_space=pltpu.VMEM)
     return pl.pallas_call(
         grads_kernel,
-        in_specs=[pl.BlockSpec(memory_space=pltpu.SMEM)] + [vmem] * 8,
+        in_specs=[vmem] * 8,
         out_specs=vmem,
         out_shape=jax.ShapeDtypeStruct((slots, 288 + 4 * CAPACITY, LANES), BF),
         scratch_shapes=[pltpu.VMEM((3 * units, rows), BF), pltpu.VMEM((3 * units, width), BF)],
         cost_estimate=pl.CostEstimate(
             flops=6 * rows * width * units, bytes_accessed=12 << 20, transcendentals=rows
         ),
-        compiler_params=limits(24),
+        compiler_params=limits(6),
         name="grads",
-    )(own, parts, labels, a, b, h, sent, direction, inputs)
-
-
-def adam_step(pc_ref, arr_ref, ms_ref, m1_ref, m2_ref, total, fresh, outs=None):
-    for sums in total:
-        sums[...] = jnp.zeros_like(sums)
+    )(parts, labels, a, b, h, sent, direction, inputs)
+
+
+def adam_update(master, first, second, grad):
+    new_first = decay_first * first + (1.0 - decay_first) * grad
+    new_second = decay_second * second + (1.0 - decay_second) * grad * grad
+    size = jnp.sqrt(new_second * (1.0 / correct_second)) + adam_eps
+    update = new_first * (1.0 / correct_first) / size
+    return master - learn_rate * (update + weight_decay * master), new_first, new_second
+
+
+def updated_master(master, first, second, grad):
+    step = (learn_rate * decay_first / correct_first) * first + (
+        learn_rate * (1.0 - decay_first) / correct_first
+    ) * grad
+    second = (decay_second / correct_second) * second + (
+        (1.0 - decay_second) / correct_second
+    ) * (grad * grad)
+    size = second * lax.rsqrt(second) + adam_eps
+    return (1.0 - learn_rate * weight_decay) * master - step / size
+
+
+def sum_experts(pc_ref, arr_ref, sums):
+    lines = sums[0].shape[1]
+    for part in sums:
+        part[...] = jnp.zeros_like(part)
     for s in range(arr_ref.shape[0]):
-        total[s % len(total)][pc_ref[s]] += arr_ref[s].astype(F32)
-    for e in range(fresh.shape[0]):
-        grad = functools.reduce(jnp.add, [sums[e] for sums in total])
-        master = ms_ref[e, 0]
-        new_first = decay_first * m1_ref[e, 0] + (1.0 - decay_first) * grad
-        new_second = decay_second * m2_ref[e, 0] + (1.0 - decay_second) * grad * grad
-        size = jnp.sqrt(new_second * (1.0 / correct_second)) + adam_eps
-        update = new_first * (1.0 / correct_first) / size
-        new_master = master - learn_rate * (update + weight_decay * master)
-        if outs is not None:
-            outs[0][e, 0] = new_master
-            outs[1][e, 0] = new_first
-            outs[2][e, 0] = new_second
-        fresh[e] = new_master.astype(BF)
-
-
-def adam_pick_kernel(info_ref, pc_ref, pn_ref, arr_ref, ms, m1, m2, pick_ref, p0, p1, p2, p3, t0, t1, fresh, turned):
-    adam_step(pc_ref, arr_ref, ms, m1, m2, (t0, t1), fresh)
-    step = pl.program_id(0)
-
-    @pl.when(step < 2)
-    def _():
-        for t in range(pick_ref.shape[0]):
-            pick_ref[t] = fresh[pn_ref[t]]
-
-    @pl.when(step >= 2)
-    def _():
-        experts = fresh.shape[0]
-        side = jnp.concatenate([fresh[e] for e in range(experts)], axis=1)
-        turned[...] = dot(piece_map(), side).reshape(turned.shape)
-        for k, piece_ref in enumerate((p0, p1, p2, p3)):
-            mine = turned[info_ref[5 + k]]
-            for e in range(experts):
-                piece_ref[e] = mine[:, e * LANES : (e + 1) * LANES].astype(BF)
-
-
-def adam_full_kernel(pc_ref, arr_ref, ms, m1, m2, om, o1, o2, t0, t1, fresh):
-    adam_step(pc_ref, arr_ref, ms, m1, m2, (t0, t1), fresh, (om, o1, o2))
-
-
-def adam_call(info, place_cur, place_next, arrived, states, full):
+        sums[s % len(sums)][pc_ref[s]] += arr_ref[s, 0:lines].astype(F32)
+
+
+def adam_pick_kernel(
+    pc_ref, pn_ref, arr_ref, ms, m1, m2,
+    pick_hbm, p0, p1, p2, p3, rows_hbm, s0, s1, fresh, turned, picks, split, rows, sems,
+):
+    slots = arr_ref.shape[0]
+    experts, _, lines, _ = ms.shape
+    for s in range(slots):
+        for j in range(rows.shape[1] // LANES):
+            top = 3 * lines + j * CAPACITY
+            rows[s * CAPACITY : (s + 1) * CAPACITY, j * LANES : (j + 1) * LANES] = arr_ref[
+                s, top : top + CAPACITY
+            ]
+    writes = [pltpu.make_async_copy(rows, rows_hbm, sems.at[6])]
+    writes[0].start()
+    sum_experts(pc_ref, arr_ref, (s0, s1))
+    for which in range(3):
+        part = slice(which * lines, (which + 1) * lines)
+        for e in range(experts):
+            at = (e, which)
+            grad = s0[e, part] + s1[e, part]
+            fresh[e] = updated_master(ms[at], m1[at], m2[at], grad).astype(BF)
+        if which < 2:
+            for t in range(slots):
+                picks[which, t] = fresh[pn_ref[t]]
+            part = pick_hbm.at[:, pl.ds(which * lines, lines)]
+            writes.append(pltpu.make_async_copy(picks.at[which], part, sems.at[which]))
+            writes[-1].start()
+    side = jnp.concatenate([fresh[e] for e in range(experts)], axis=1)
+    turned[...] = dot(piece_map(), side).reshape(turned.shape)
+    hid = lax.axis_index("hid")
+    for k, piece_ref in enumerate((p0, p1, p2, p3)):
+        mine = turned[lax.rem(hid + k, 4)]
+        for e in range(experts):
+            split[k, e] = mine[:, e * LANES : (e + 1) * LANES].astype(BF)
+        writes.append(pltpu.make_async_copy(split.at[k], piece_ref, sems.at[2 + k]))
+        writes[-1].start()
+    for write in writes:
+        write.wait()
+
+
+def adam_pick_call(place_cur, place_next, arrived, states):
     slots = arrived.shape[0]
     experts, _, lines, _ = states[0].shape
-    block = lines
-    steps = lines // block
     smem = pl.BlockSpec(memory_space=pltpu.SMEM)
-    state = pl.BlockSpec((experts, 1, block, LANES), lambda i: (0, i // steps, i % steps, 0))
-    piece = pl.BlockSpec((slots, block, LANES), lambda i: (0, i, 0))
-    scratch = [pltpu.VMEM((experts, block, LANES), t) for t in (F32, F32, BF)]
-    cost = pl.CostEstimate(flops=20 << 20, bytes_accessed=6 << 20, transcendentals=0)
-    if not full:
-        return pl.pallas_call(
-            adam_pick_kernel,
-            grid=(3 * steps,),
-            in_specs=[smem, smem, smem, piece, state, state, state],
-            out_specs=[pl.BlockSpec((slots, block, LANES), lambda i: (0, jnp.minimum(i, 1), 0))]
-            + [single((experts, lines // 4, LANES))] * 4,
-            out_shape=[pltpu.HBM((slots, 2 * lines, LANES), BF)]
-            + [jax.ShapeDtypeStruct((experts, lines // 4, LANES), BF)] * 4,
-            scratch_shapes=scratch + [pltpu.VMEM((4, lines // 4, experts * LANES), F32)],
-            cost_estimate=cost,
-            compiler_params=limits(18),
-            name="adam_pick",
-        )(info, place_cur, place_next, arrived, *states)
+    vmem = pl.BlockSpec(memory_space=pltpu.VMEM)
+    rows_shape = (slots * CAPACITY, (arrived.shape[1] - 3 * lines) // CAPACITY * LANES)
+    return pl.pallas_call(
+        adam_pick_kernel,
+        in_specs=[smem, smem] + [vmem] * 4,
+        out_specs=[pl.BlockSpec(memory_space=pltpu.HBM)] * 6,
+        out_shape=[pltpu.HBM((slots, 2 * lines, LANES), BF)]
+        + [pltpu.HBM((experts, lines // 4, LANES), BF)] * 4
+        + [pltpu.HBM(rows_shape, BF)],
+        scratch_shapes=[pltpu.VMEM((experts, 3 * lines, LANES), F32)] * 2
+        + [
+            pltpu.VMEM((experts, lines, LANES), BF),
+            pltpu.VMEM((4, lines // 4, experts * LANES), F32),
+            pltpu.VMEM((2, slots, lines, LANES), BF),
+            pltpu.VMEM((4, experts, lines // 4, LANES), BF),
+            pltpu.VMEM(rows_shape, BF),
+            pltpu.SemaphoreType.DMA((7,)),
+        ],
+        cost_estimate=pl.CostEstimate(flops=20 << 20, bytes_accessed=6 << 20, transcendentals=0),
+        compiler_params=limits(10),
+        name="adam_pick",
+    )(place_cur, place_next, arrived, *states)
+
+
+def adam_full_kernel(pc_ref, arr_ref, ms, m1, m2, om, o1, o2, s0, s1):
+    sum_experts(pc_ref, arr_ref, (s0, s1))
+    for e in range(ms.shape[0]):
+        om[e, 0], o1[e, 0], o2[e, 0] = adam_update(ms[e, 0], m1[e, 0], m2[e, 0], s0[e] + s1[e])
+
+
+def adam_full_call(place_cur, arrived, states):
+    slots = arrived.shape[0]
+    experts, count, lines, _ = states[0].shape
+    state = pl.BlockSpec((experts, 1, lines, LANES), lambda i: (0, i, 0, 0))
     return pl.pallas_call(
         adam_full_kernel,
-        grid=(3 * steps,),
-        in_specs=[smem, piece, state, state, state],
+        grid=(count,),
+        in_specs=[
+            pl.BlockSpec(memory_space=pltpu.SMEM),
+            pl.BlockSpec((slots, lines, LANES), lambda i: (0, i, 0)),
+            state, state, state,
+        ],
         out_specs=[state, state, state],
         out_shape=[jax.ShapeDtypeStruct(s.shape, F32) for s in states],
-        scratch_shapes=scratch,
-        cost_estimate=cost,
+        scratch_shapes=[pltpu.VMEM((experts, lines, LANES), F32)] * 2,
+        cost_estimate=pl.CostEstimate(flops=20 << 20, bytes_accessed=6 << 20, transcendentals=0),
         compiler_params=limits(60),
         name="adam_full",
     )(place_cur, arrived, *states)
@@ -312,17 +350,16 @@
     shape = (slots, 4 * pieces[0].shape[1], LANES)
     return pl.pallas_call(
         pick_kernel,
-        grid=(1,),
-        in_specs=[pl.BlockSpec(memory_space=pltpu.SMEM)] + [whole(p.shape) for p in pieces],
-        out_specs=whole(shape),
+        in_specs=[pl.BlockSpec(memory_space=pltpu.SMEM)] + [VM] * len(pieces),
+        out_specs=VM,
         out_shape=jax.ShapeDtypeStruct(shape, BF),
         cost_estimate=pl.CostEstimate(flops=1 << 20, bytes_accessed=2 << 20, transcendentals=0),
-        compiler_params=limits(16),
+        compiler_params=limits(4),
         name="pick",
     )(place_next, *pieces)
 
 
-def hidden_kernel(q_ref, w_ref, r0, r1, r2, r3, out_ref, mat):
+def hidden_kernel(w_ref, r0, r1, r2, r3, out_ref, mat):
     units = out_ref.shape[0]
     swap = swap_map(16, 16)
     for group in range(4):
@@ -346,30 +383,29 @@
     total = None
     for k, rows in enumerate((r0, r1, r2, r3)):
         quarter = rows.shape[1]
-        start = pl.multiple_of(q_ref[1 + k] * quarter, quarter)
+        turn = lax.rem(lax.axis_index("hid") + 4 - k, 4)
+        start = pl.multiple_of(turn * quarter, quarter)
         term = dot(mat[:, pl.ds(start, quarter)], rows[...], NT)
         total = term if total is None else total + term
     gate, up = total[:units], total[units:]
     out_ref[...] = (gate * jax.nn.sigmoid(gate) * up).astype(BF)
 
 
-def hidden_call(quarters, packed, rows):
+def hidden_call(packed, rows):
     units = packed.shape[0] * 6
     count, quarter = rows[0].shape
     return pl.pallas_call(
         hidden_kernel,
-        grid=(1,),
-        in_specs=[pl.BlockSpec(memory_space=pltpu.SMEM), whole(packed.shape)]
-        + [whole(r.shape) for r in rows],
-        out_specs=whole((units, count)),
+        in_specs=[VM] * (1 + len(rows)),
+        out_specs=VM,
         out_shape=jax.ShapeDtypeStruct((units, count), BF),
         scratch_shapes=[pltpu.VMEM((2 * units, 4 * quarter), BF)],
         cost_estimate=pl.CostEstimate(
             flops=16 * count * quarter * units, bytes_accessed=4 << 20, transcendentals=count * units
         ),
-        compiler_params=limits(24),
+        compiler_params=limits(6),
         name="hidden",
-    )(quarters, packed, *rows)
+    )(packed, *rows)
 
 
 def unpack_kernel(w_ref, out_ref):
@@ -395,12 +431,11 @@
     shape = (4, packed.shape[0] * 6, 4 * LANES)
     return pl.pallas_call(
         unpack_kernel,
-        grid=(1,),
-        in_specs=[whole(packed.shape)],
-        out_specs=whole(shape),
+        in_specs=[VM],
+        out_specs=VM,
         out_shape=jax.ShapeDtypeStruct(shape, BF),
         cost_estimate=pl.CostEstimate(flops=1 << 28, bytes_accessed=2 << 20, transcendentals=0),
-        compiler_params=limits(16),
+        compiler_params=limits(4),
         name="unpack",
     )(packed)
 
@@ -418,14 +453,13 @@
     quarter = weights.shape[2]
     return pl.pallas_call(
         down_kernel,
-        grid=(1,),
-        in_specs=[whole(weights.shape)] + [whole(h.shape) for h in hidden],
-        out_specs=whole((count, quarter)),
+        in_specs=[VM] * (1 + len(hidden)),
+        out_specs=VM,
         out_shape=jax.ShapeDtypeStruct((count, quarter), BF),
         cost_estimate=pl.CostEstimate(
             flops=8 * count * quarter * units, bytes_accessed=3 << 20, transcendentals=0
         ),
-        compiler_params=limits(16),
+        compiler_params=limits(4),
         name="down",
     )(weights, *hidden)
 
@@ -446,7 +480,6 @@
 ):
     slot_count = lax.axis_size("slot")
     hid_count = lax.axis_size("hid")
-    hid_index = lax.axis_index("hid").astype(jnp.int32)
     _, width = back_rows.shape[1:]
 
     def pass_on(value, k):
@@ -458,39 +491,31 @@
     capacity = CAPACITY
     quarter = fwd_rows.shape[1]
     everyone = slot_count * hid_count
-    turns = jnp.arange(hid_count, dtype=jnp.int32)
-    info = jnp.concatenate(
-        [
-            lax.axis_index("slot").astype(jnp.int32).reshape(1),
-            (hid_index + hid_count - turns) % hid_count,
-            (hid_index + turns) % hid_count,
-        ]
-    )
     inputs, direction, a, b, h, part, sent, slot_place = scores_call(
-        info, back_rows[0], readout[0], slot_weights.reshape(-1, width), ref_logratio,
+        back_rows[0], readout[0], slot_weights.reshape(-1, width), ref_logratio,
         routes.reshape(1, -1), fwd_rows, everyone,
     )
     parts = lax.all_to_all(part, ("slot", "hid"), split_axis=0, concat_axis=0, tiled=True)
     blocks = grads_call(
-        info, parts, labels.reshape(part.shape[1:]), a, b, h, sent, direction, inputs, slot_count
+        parts, labels.reshape(part.shape[1:]), a, b, h, sent, direction, inputs, slot_count
     )
     arrived = exchange(blocks)
 
     lines = 96
     shape = (master.shape[0], 3, lines, LANES)
     states = [v.reshape(shape) for v in (master, first_moment, second_moment)]
-    picked, *pieces = adam_call(info, place_cur, place_next, arrived, states, False)
-    gate_up = exchange(picked)
+    picked, *pieces, own_rows = adam_pick_call(place_cur, place_next, arrived, states)
+    far_rows = pass_on(own_rows, 2)
+    all_rows = [own_rows, pass_on(own_rows, 1), far_rows, pass_on(own_rows, 3)]
+
+    gate_up = in_hbm(exchange(picked))
     pieces = [pieces[0]] + [pass_on(pieces[k], k) for k in range(1, hid_count)]
     down = pick_call(place_next, pieces)
     down = exchange(down)
 
-    own_rows = arrived[:, 3 * lines :].reshape(slot_count, quarter // LANES, capacity, LANES)
-    own_rows = own_rows.transpose(0, 2, 1, 3).reshape(slot_count * capacity, quarter)
-    all_rows = [own_rows] + [pass_on(own_rows, k) for k in range(1, hid_count)]
-    held = adam_call(info, place_cur, place_next, arrived, states, True)
-
-    hidden = hidden_call(info, gate_up, all_rows)
+    held = adam_full_call(place_cur, arrived, states)
+
+    hidden = hidden_call(gate_up, all_rows)
     hidden = [hidden] + [pass_on(hidden, k) for k in range(1, hid_count)]
     produced = down_call(unpack_call(down), hidden)
     returned = exchange(produced.reshape(slot_count, capacity, quarter))

time: 161 us -> 159 us (0.988)
  starting transfers between devices: 24 us -> 28.2 us
  waiting for transfers between devices: 32.8 us -> 29.2 us
    ppermute x9, waiting for transfers between devices: 12.8 us -> 8.63 us  [pass_on(): lax.ppermute(value, 'hid', [(i, (i + k) % hid_count) for i in range(hid_c...]
    ppermute x9, starting transfers between devices: 8 us -> 11.5 us  [pass_on(): lax.ppermute(value, 'hid', [(i, (i + k) % hid_count) for i in range(hid_c...]
    pallas_call x8, Pallas kernels: 34.3 us -> 32.7 us  [the longest x1 8.89 us: adam_full_call(): pl.pallas_call(adam_full_kernel, grid=(count,), in_specs=[pl.BlockSpec(me...]
  transfers between devices with their start and end apart: 12 -> 12, of which waited for: 8 -> 7; matrix products, arithmetic and copies ran while one was open for 0% -> 0% of each run, Pallas kernels for 9% -> 9%
where the time goes in v4:
time: 159 us; the launch traced here: 158 us
  blocking collectives  66.3 us (42%)
  Pallas kernels  32.7 us (21%)
  waiting for transfers between devices  29.2 us (18%)
  starting transfers between devices  28.2 us (18%)
    all_to_all x1, blocking collectives, exchange(): lax.all_to_all(value, 'slot', split_axis=0, concat_axis=0, tiled=True)  40.7 us
    all_to_all x1, blocking collectives, shards(): lax.all_to_all(part, ('slot', 'hid'), split_axis=0, concat_axis=0, tiled=...  25.6 us
    all_to_all x3, waiting for transfers between devices, exchange(): lax.all_to_all(value, 'slot', split_axis=0, concat_axis=0, tiled=True)  20.5 us
    all_to_all x3, starting transfers between devices, exchange(): lax.all_to_all(value, 'slot', split_axis=0, concat_axis=0, tiled=True)  16.7 us
    ppermute x9, starting transfers between devices, pass_on(): lax.ppermute(value, 'hid', [(i, (i + k) % hid_count) for i in range(hid_c...  11.5 us
    pallas_call x1, Pallas kernels, adam_full_call(): pl.pallas_call(adam_full_kernel, grid=(count,), in_specs=[pl.BlockSpec(me...  8.89 us
    ppermute x9, waiting for transfers between devices, pass_on(): lax.ppermute(value, 'hid', [(i, (i + k) % hid_count) for i in range(hid_c...  8.63 us
    pallas_call x1, Pallas kernels, scores_call(): pl.pallas_call(scores_kernel, in_specs=[hbm, hbm, hbm, vmem, vmem, vmem],...  8.08 us
  transfers between devices with their start and end apart: 12, of which 7 were waited for; matrix products, arithmetic and copies ran while one was open for 0% of the time, Pallas kernels for 9%

profile of v4, /device:TPU:1, one launch (start us, length us, event | category | flops | bytes accessed | tf_op | source)
XLA Modules:
  0.0 158.4 jit_solution(14912560249204394723)
XLA Ops:
  0.6 8.1 %scores.1 = (bf16[1024,2048]{1,0:T(8,128)(2,1)S(1)}, bf16[1024,2048]{1,0:T(8,128)(2,1)S(1)}, f32[192,1024]{1,0:T(8,128)S(1)}, f32[192,1024]{1,0:T(8,128)S(1)}, b...) custom-call(bf16[1024,2048]{1,0:T(8,128)(2,1)} %bitcast.22, ...), custom_call_target="tpu_custom_call" | custom-call | flops 2415919104 | bytes 14680064 | tf_op jit(solution)/shard_map/scores/pallas_call | solution.py:127
  8.7 25.6 %all_to_all.25.parts_ref = f32[128,8,128]{2,1,0:T(8,128)S(1)} all-to-all(f32[128,8,128]{2,1,0:T(8,128)} %get-tuple-element.22), channel_id=1, replica_groups=mesh['slot'=32,'hid'=4] {'slot','hid'}, dimensions={0} | all-to-all | bytes 1048576 | tf_op jit(solution)/shard_map/all_to_all | solution.py:498
  34.3 4.6 %grads.1 = bf16[32,352,128]{2,1,0:T(8,128)(2,1)S(1)} custom-call(f32[128,8,128]{2,1,0:T(8,128)S(1)} %all_to_all.25.parts_ref, s32[8,128]{1,0:T(8,128)S(1)} %bitcast.21, f32[192,1024]{1,0:T(8,128)S(1)} %get-tuple-element.23.a_ref, f32[192,1024]{1,0:T(8,128)S(1)} %get-tuple-element.24.b_ref, bf16[192,1024]{1,0:T(8,128)(2,1)S(1)} %get-tuple-element.25.h_ref, ...), custom_call_target="tpu_custom_call" | custom-call | flops 2415919104 | bytes 12582912 | tf_op jit(solution)/shard_map/grads/pallas_call | solution.py:202
  38.9 0.0 copy-start.1
  39.0 0.0 copy-start.8
  39.0 40.7 %all_to_all.26.arr_ref = bf16[32,352,128]{2,1,0:T(8,128)(2,1)S(1)} all-to-all(bf16[32,352,128]{2,1,0:T(8,128)(2,1)S(1)} %grads.1), channel_id=1, replica_groups=mesh['slot'=32,'hid'=4] {'slot'}, dimensions={0} | all-to-all | bytes 5767168 | tf_op jit(solution)/shard_map/all_to_all | solution.py:489
  79.7 4.6 %adam_pick.1 = (bf16[32,192,128]{2,1,0:T(8,128)(2,1)}, bf16[16,24,128]{2,1,0:T(8,128)(2,1)}, bf16[16,24,128]{2,1,0:T(8,128)(2,1)}, bf16[16,24,128]{2,1,0:T(8,128...) custom-call(s32[32]{0:T(128)S(1)} %copy-done.8, s32[32]{0:T(128)S(1)} %copy-done.7, ...), custom_call_target="tpu_custom_call" | custom-call | flops 20971520 | bytes 6291456 | tf_op jit(solution)/shard_map/adam_pick/pallas_call | solution.py:289
  84.3 0.0 copy-start.4
  84.4 0.0 copy-start.5
  84.4 4.6 %all-to-all-start.3 = ((bf16[32,192,128]{2,1,0:T(8,128)(2,1)}), bf16[32,192,128]{2,1,0:T(8,128)(2,1)}, u32[]{:S(2)}, u32[]{:S(2)}) async-start(bf16[32,192,128]{2,1,0:T(8,128)(2,1)} %get-tuple-element.33), calls=%async_computation.3 | async-start | bytes 3145728 | tf_op jit(solution)/shard_map/all_to_all | solution.py:489
  89.0 0.4 collective-permute-start
  89.4 1.4 collective-permute-start.1
  90.9 1.1 collective-permute-start.2
  91.9 0.8 collective-permute-start.5
  92.7 1.5 collective-permute-start.4
  94.2 2.5 %collective-permute-done.p1 = bf16[16,24,128]{2,1,0:T(8,128)(2,1)S(1)} collective-permute-done((bf16[16,24,128]{2,1,0:T(8,128)(2,1)S(1)}, bf16[16,24,128]{2,1,0:T(8,128)(2,1)S(1)}, u32[]{:S(2)}, u32[]{:S(2)}) %collective-permute-start) | collective-permute-done | bytes 98336 | tf_op jit(solution)/shard_map/ppermute | solution.py:486
  96.7 0.3 collective-permute-done.2.p3
  97.1 1.6 pick.1
  98.7 12.9 %all-to-all-done.3.w_ref = bf16[32,192,128]{2,1,0:T(8,128)(2,1)} async-done(((bf16[32,192,128]{2,1,0:T(8,128)(2,1)}), bf16[32,192,128]{2,1,0:T(8,128)(2,1)}, u32[]{:S(2)}, u32[]{:S(2)}) %all-to-all-start.3) | async-done | bytes 1572896 | tf_op jit(solution)/shard_map/all_to_all | solution.py:489
  111.5 4.7 %all-to-all-start.2 = ((bf16[32,96,128]{2,1,0:T(8,128)(2,1)}), bf16[32,96,128]{2,1,0:T(8,128)(2,1)S(1)}, u32[]{:S(2)}, u32[]{:S(2)}) async-start(bf16[32,96,128]{2,1,0:T(8,128)(2,1)} %pick.1), calls=%async_computation.2 | async-start | bytes 1572864 | tf_op jit(solution)/shard_map/all_to_all | solution.py:489
  116.2 2.9 %hidden.1.h0 = bf16[192,512]{1,0:T(8,128)(2,1)S(1)} custom-call(bf16[32,192,128]{2,1,0:T(8,128)(2,1)} %all-to-all-done.3.w_ref, bf16[512,512]{1,0:T(8,128)(2,1)S(1)} %copy-done.4, bf16[512,512]{1,0:T(8,128)(2,1)S(1)} %collective-permute-done.3.r1, bf16[512,512]{1,0:T(8,128)(2,1)S(1)} %collective-permute-done.4.r2, bf16[512,512]{1,0:T(8,128)(2,1)S(1)} %collective-permute-done.5.r3), custom_call_target="tpu_custom_call" | custom-call | flops 805306368 | bytes 4194304 | tf_op jit(solution)/shard_map/hidden/pallas_call | solution.py:397
  119.1 5.7 %collective-permute-start.8 = (bf16[192,512]{1,0:T(8,128)(2,1)S(1)}, bf16[192,512]{1,0:T(8,128)(2,1)S(1)}, u32[]{:S(2)}, u32[]{:S(2)}) collective-permute-start(bf16[192,512]{1,0:T(8,128)(2,1)S(1)} %hidden.1.h0), channel_id=1, source_target_pairs={{0,3},{1,0},{2,1},{3,2},{4,7},{5,4},{6,5},{7,6},{8,11},{9,8},{10,9... | collective-permute-start | bytes 589832 | tf_op jit(solution)/shard_map/ppermute | solution.py:486
  124.8 0.7 collective-permute-start.6
  125.5 5.0 %all-to-all-done.2.w_ref = bf16[32,96,128]{2,1,0:T(8,128)(2,1)S(1)} async-done(((bf16[32,96,128]{2,1,0:T(8,128)(2,1)}), bf16[32,96,128]{2,1,0:T(8,128)(2,1)S(1)}, u32[]{:S(2)}, u32[]{:S(2)}) %all-to-all-start.2) | async-done | bytes 786464 | tf_op jit(solution)/shard_map/all_to_all | solution.py:489
  130.4 0.6 unpack.1.w_ref
  131.0 1.5 collective-permute-done.8.h3
  132.5 4.2 %collective-permute-done.6.h1 = bf16[192,512]{1,0:T(8,128)(2,1)S(1)} collective-permute-done((bf16[192,512]{1,0:T(8,128)(2,1)S(1)}, bf16[192,512]{1,0:T(8,128)(2,1)S(1)}, u32[]{:S(2)}, u32[]{:S(2)}) %collective-permute-start.6) | collective-permute-done | bytes 196640 | tf_op jit(solution)/shard_map/ppermute | solution.py:486
  136.8 1.6 down.1
  138.3 7.4 %all-to-all-start.4 = ((bf16[32,16,512]{2,1,0:T(8,128)(2,1)}), bf16[32,16,512]{2,1,0:T(8,128)(2,1)S(1)}, u32[]{:S(2)}, u32[]{:S(2)}) async-start(bf16[32,16,512]{2,1,0:T(8,128)(2,1)} %bitcast.9), calls=%async_computation.4 | async-start | bytes 1048576 | tf_op jit(solution)/shard_map/all_to_all | solution.py:489
  145.7 8.9 %adam_full.1 = (f32[16,3,96,128]{3,2,1,0:T(8,128)}, f32[16,3,96,128]{3,2,1,0:T(8,128)}, f32[16,3,96,128]{3,2,1,0:T(8,128)}) custom-call(s32[32]{0:T(128)} %pc_ref.3, bf16[32,352,128]{2,1,0:T(8,128)(2,1)} %copy-done, f32[16,3,96,128]{3,2,1,0:T(8,128)} %bitcast.15, f32[16,3,96,128]{3,2,1,0:T(8,128)} %bitcast.17, f32[16,3,96,128]{3,2,1,0:T(8,128)} %bitcast.19), custom_call_target="tpu_custom_call" | custom-call | flops 20971520 | bytes 6291456 | tf_op jit(solution)/shard_map/adam_full/pallas_call | solution.py:321
  154.6 2.7 %all-to-all-done.4 = bf16[32,16,512]{2,1,0:T(8,128)(2,1)S(1)} async-done(((bf16[32,16,512]{2,1,0:T(8,128)(2,1)}), bf16[32,16,512]{2,1,0:T(8,128)(2,1)S(1)}, u32[]{:S(2)}, u32[]{:S(2)}) %all-to-all-start.4) | async-done | bytes 524320 | tf_op jit(solution)/shard_map/all_to_all | solution.py:489
  157.3 1.1 convolution_convert_fusion
  (29 shorter events, 0.1 us)
Async XLA Ops:
  0.6 33.7 %copy-start.6 = (s32[1,1024]{1,0:T(1,128)S(1)}, s32[1,1024]{1,0:T(1,128)}, u32[]{:S(2)}) copy-start(s32[1,1024]{1,0:T(1,128)} %param.19) | copy-start | bytes 12292
  34.3 45.4 %copy-start.3 = (f32[16,3,1,12288]{3,2,1,0:T(1,128)S(1)}, f32[16,3,1,12288]{3,2,1,0:T(1,128)}, u32[]{:S(2)}) copy-start(f32[16,3,1,12288]{3,2,1,0:T(1,128)} %param.14) | copy-start | bytes 7077892
  38.9 40.8 %copy-start.1 = (f32[16,3,1,12288]{3,2,1,0:T(1,128)S(1)}, f32[16,3,1,12288]{3,2,1,0:T(1,128)}, u32[]{:S(2)}) copy-start(f32[16,3,1,12288]{3,2,1,0:T(1,128)} %param.12) | copy-start | bytes 7077892
  39.0 40.8 %copy-start.2 = (f32[16,3,1,12288]{3,2,1,0:T(1,128)S(1)}, f32[16,3,1,12288]{3,2,1,0:T(1,128)}, u32[]{:S(2)}) copy-start(f32[16,3,1,12288]{3,2,1,0:T(1,128)} %param.13) | copy-start | bytes 7077892
  39.0 40.8 %copy-start.7 = (s32[32]{0:T(128)S(1)}, s32[32]{0:T(128)}, u32[]{:S(2)}) copy-start(s32[32]{0:T(128)} %pn_ref.3) | copy-start | bytes 388
  39.0 40.7 %copy-start.8 = (s32[32]{0:T(128)S(1)}, s32[32]{0:T(128)}, u32[]{:S(2)}) copy-start(s32[32]{0:T(128)} %pc_ref.3) | copy-start | bytes 388
  79.7 4.6 %copy-start = (bf16[32,352,128]{2,1,0:T(8,128)(2,1)}, bf16[32,352,128]{2,1,0:T(8,128)(2,1)S(1)}, u32[]{:S(2)}) copy-start(bf16[32,352,128]{2,1,0:T(8,128)(2,1)S(1)} %all_to_all.26.arr_ref) | copy-start | bytes 8650756
  84.3 4.7 %copy-start.11 = (bf16[16,24,128]{2,1,0:T(8,128)(2,1)S(1)}, bf16[16,24,128]{2,1,0:T(8,128)(2,1)}, u32[]{:S(2)}) copy-start(bf16[16,24,128]{2,1,0:T(8,128)(2,1)} %get-tuple-element.30) | copy-start | bytes 294916
  84.3 5.1 %copy-start.10 = (bf16[16,24,128]{2,1,0:T(8,128)(2,1)S(1)}, bf16[16,24,128]{2,1,0:T(8,128)(2,1)}, u32[]{:S(2)}) copy-start(bf16[16,24,128]{2,1,0:T(8,128)(2,1)} %get-tuple-element.31) | copy-start | bytes 294916
  84.3 6.5 %copy-start.9 = (bf16[16,24,128]{2,1,0:T(8,128)(2,1)S(1)}, bf16[16,24,128]{2,1,0:T(8,128)(2,1)}, u32[]{:S(2)}) copy-start(bf16[16,24,128]{2,1,0:T(8,128)(2,1)} %get-tuple-element.32) | copy-start | bytes 294916
  84.3 7.6 %copy-start.4 = (bf16[512,512]{1,0:T(8,128)(2,1)S(1)}, bf16[512,512]{1,0:T(8,128)(2,1)}, u32[]{:S(2)}) copy-start(bf16[512,512]{1,0:T(8,128)(2,1)} %get-tuple-element.34.r0) | copy-start | bytes 1572868
  84.4 12.7 %copy-start.5 = (bf16[16,24,128]{2,1,0:T(8,128)(2,1)S(1)}, bf16[16,24,128]{2,1,0:T(8,128)(2,1)}, u32[]{:S(2)}) copy-start(bf16[16,24,128]{2,1,0:T(8,128)(2,1)} %get-tuple-element.29.p0) | copy-start | bytes 294916
  84.4 27.2 %all-to-all-start.3 = ((bf16[32,192,128]{2,1,0:T(8,128)(2,1)}), bf16[32,192,128]{2,1,0:T(8,128)(2,1)}, u32[]{:S(2)}, u32[]{:S(2)}) async-start(bf16[32,192,128]{2,1,0:T(8,128)(2,1)} %get-tuple-element.33), calls=%async_computation.3 | async-start | bytes 3145728 | tf_op jit(solution)/shard_map/all_to_all | solution.py:489
  89.0 7.7 %collective-permute-start = (bf16[16,24,128]{2,1,0:T(8,128)(2,1)S(1)}, bf16[16,24,128]{2,1,0:T(8,128)(2,1)S(1)}, u32[]{:S(2)}, u32[]{:S(2)}) collective-permute-start(bf16[16,24,128]{2,1,0:T(8,128)(2,1)S(1)} %copy-done.11), channel_id=1, source_target_pairs={{0,1},{1,2},{2,3},{3,0},{4,5},{5,6},{6,7},{7,4},{8,9},{9,10},{10,1... | collective-permute-start | bytes 294920 | tf_op jit(solution)/shard_map/ppermute | solution.py:486
  89.4 7.3 %collective-permute-start.1 = (bf16[16,24,128]{2,1,0:T(8,128)(2,1)S(1)}, bf16[16,24,128]{2,1,0:T(8,128)(2,1)S(1)}, u32[]{:S(2)}, u32[]{:S(2)}) collective-permute-start(bf16[16,24,128]{2,1,0:T(8,128)(2,1)S(1)} %copy-done.10), channel_id=1, source_target_pairs={{0,2},{1,3},{2,0},{3,1},{4,6},{5,7},{6,4},{7,5},{8,10},{9,11},{10,... | collective-permute-start | bytes 294920 | tf_op jit(solution)/shard_map/ppermute | solution.py:486
  90.9 6.2 %collective-permute-start.2 = (bf16[16,24,128]{2,1,0:T(8,128)(2,1)S(1)}, bf16[16,24,128]{2,1,0:T(8,128)(2,1)S(1)}, u32[]{:S(2)}, u32[]{:S(2)}) collective-permute-start(bf16[16,24,128]{2,1,0:T(8,128)(2,1)S(1)} %copy-done.9), channel_id=1, source_target_pairs={{0,3},{1,0},{2,1},{3,2},{4,7},{5,4},{6,5},{7,6},{8,11},{9,8},{10,9... | collective-permute-start | bytes 294920 | tf_op jit(solution)/shard_map/ppermute | solution.py:486
  91.9 24.3 %collective-permute-start.5 = (bf16[512,512]{1,0:T(8,128)(2,1)S(1)}, bf16[512,512]{1,0:T(8,128)(2,1)S(1)}, u32[]{:S(2)}, u32[]{:S(2)}) collective-permute-start(bf16[512,512]{1,0:T(8,128)(2,1)S(1)} %copy-done.4), channel_id=1, source_target_pairs={{0,3},{1,0},{2,1},{3,2},{4,7},{5,4},{6,5},{7,6},{8,11},{9,8},{10,9... | collective-permute-start | bytes 1572872 | tf_op jit(solution)/shard_map/ppermute | solution.py:486
  92.7 23.5 %collective-permute-start.4 = (bf16[512,512]{1,0:T(8,128)(2,1)S(1)}, bf16[512,512]{1,0:T(8,128)(2,1)S(1)}, u32[]{:S(2)}, u32[]{:S(2)}) collective-permute-start(bf16[512,512]{1,0:T(8,128)(2,1)S(1)} %copy-done.4), channel_id=1, source_target_pairs={{0,2},{1,3},{2,0},{3,1},{4,6},{5,7},{6,4},{7,5},{8,10},{9,11},{10,... | collective-permute-start | bytes 1572872 | tf_op jit(solution)/shard_map/ppermute | solution.py:486
  96.7 19.5 %collective-permute-start.3 = (bf16[512,512]{1,0:T(8,128)(2,1)S(1)}, bf16[512,512]{1,0:T(8,128)(2,1)S(1)}, u32[]{:S(2)}, u32[]{:S(2)}) collective-permute-start(bf16[512,512]{1,0:T(8,128)(2,1)S(1)} %copy-done.4), channel_id=1, source_target_pairs={{0,1},{1,2},{2,3},{3,0},{4,5},{5,6},{6,7},{7,4},{8,9},{9,10},{10,1... | collective-permute-start | bytes 1572872 | tf_op jit(solution)/shard_map/ppermute | solution.py:486
  111.5 18.9 %all-to-all-start.2 = ((bf16[32,96,128]{2,1,0:T(8,128)(2,1)}), bf16[32,96,128]{2,1,0:T(8,128)(2,1)S(1)}, u32[]{:S(2)}, u32[]{:S(2)}) async-start(bf16[32,96,128]{2,1,0:T(8,128)(2,1)} %pick.1), calls=%async_computation.2 | async-start | bytes 1572864 | tf_op jit(solution)/shard_map/all_to_all | solution.py:489
  119.1 13.4 %collective-permute-start.8 = (bf16[192,512]{1,0:T(8,128)(2,1)S(1)}, bf16[192,512]{1,0:T(8,128)(2,1)S(1)}, u32[]{:S(2)}, u32[]{:S(2)}) collective-permute-start(bf16[192,512]{1,0:T(8,128)(2,1)S(1)} %hidden.1.h0), channel_id=1, source_target_pairs={{0,3},{1,0},{2,1},{3,2},{4,7},{5,4},{6,5},{7,6},{8,11},{9,8},{10,9... | collective-permute-start | bytes 589832 | tf_op jit(solution)/shard_map/ppermute | solution.py:486
  124.8 7.7 %collective-permute-start.7 = (bf16[192,512]{1,0:T(8,128)(2,1)S(1)}, bf16[192,512]{1,0:T(8,128)(2,1)S(1)}, u32[]{:S(2)}, u32[]{:S(2)}) collective-permute-start(bf16[192,512]{1,0:T(8,128)(2,1)S(1)} %hidden.1.h0), channel_id=1, source_target_pairs={{0,2},{1,3},{2,0},{3,1},{4,6},{5,7},{6,4},{7,5},{8,10},{9,11},{10,... | collective-permute-start | bytes 589832 | tf_op jit(solution)/shard_map/ppermute | solution.py:486
  124.8 12.0 %collective-permute-start.6 = (bf16[192,512]{1,0:T(8,128)(2,1)S(1)}, bf16[192,512]{1,0:T(8,128)(2,1)S(1)}, u32[]{:S(2)}, u32[]{:S(2)}) collective-permute-start(bf16[192,512]{1,0:T(8,128)(2,1)S(1)} %hidden.1.h0), channel_id=1, source_target_pairs={{0,1},{1,2},{2,3},{3,0},{4,5},{5,6},{6,7},{7,4},{8,9},{9,10},{10,1... | collective-permute-start | bytes 589832 | tf_op jit(solution)/shard_map/ppermute | solution.py:486
  138.3 19.0 %all-to-all-start.4 = ((bf16[32,16,512]{2,1,0:T(8,128)(2,1)}), bf16[32,16,512]{2,1,0:T(8,128)(2,1)S(1)}, u32[]{:S(2)}, u32[]{:S(2)}) async-start(bf16[32,16,512]{2,1,0:T(8,128)(2,1)} %bitcast.9), calls=%async_computation.4 | async-start | bytes 1048576 | tf_op jit(solution)/shard_map/all_to_all | solution.py:489
  145.7 11.6 %copy-start.12 = (s32[1,256]{1,0:T(1,128)S(1)}, s32[1,256]{1,0:T(1,128)}, u32[]{:S(2)}) copy-start(s32[1,256]{1,0:T(1,128)} %get-tuple-element.21) | copy-start | bytes 3076

commit v5 on v4

--- a/solution.py
+++ b/solution.py
@@ -308,31 +308,33 @@
     )(place_cur, place_next, arrived, *states)
 
 
-def adam_full_kernel(pc_ref, arr_ref, ms, m1, m2, om, o1, o2, s0, s1):
+def adam_full_kernel(pc_ref, arr_ref, ms, m1, m2, *refs):
+    om, o1, o2, s0, s1 = refs[-5:]
     sum_experts(pc_ref, arr_ref, (s0, s1))
     for e in range(ms.shape[0]):
         om[e, 0], o1[e, 0], o2[e, 0] = adam_update(ms[e, 0], m1[e, 0], m2[e, 0], s0[e] + s1[e])
 
 
-def adam_full_call(place_cur, arrived, states):
+def adam_full_call(place_cur, arrived, states, first, count, held):
     slots = arrived.shape[0]
-    experts, count, lines, _ = states[0].shape
-    state = pl.BlockSpec((experts, 1, lines, LANES), lambda i: (0, i, 0, 0))
+    experts, _, lines, _ = states[0].shape
+    state = pl.BlockSpec((experts, 1, lines, LANES), lambda i: (0, first + i, 0, 0))
     return pl.pallas_call(
         adam_full_kernel,
         grid=(count,),
         in_specs=[
             pl.BlockSpec(memory_space=pltpu.SMEM),
-            pl.BlockSpec((slots, lines, LANES), lambda i: (0, i, 0)),
+            pl.BlockSpec((slots, lines, LANES), lambda i: (0, first + i, 0)),
             state, state, state,
-        ],
+        ]
+        + [pl.BlockSpec(memory_space=pl.ANY)] * len(held),
         out_specs=[state, state, state],
         out_shape=[jax.ShapeDtypeStruct(s.shape, F32) for s in states],
         scratch_shapes=[pltpu.VMEM((experts, lines, LANES), F32)] * 2,
+        input_output_aliases={5 + k: k for k in range(len(held))},
         cost_estimate=pl.CostEstimate(flops=20 << 20, bytes_accessed=6 << 20, transcendentals=0),
         compiler_params=limits(60),
-        name="adam_full",
-    )(place_cur, arrived, *states)
+    )(place_cur, arrived, *states, *held)
 
 
 def pick_kernel(pn_ref, p0, p1, p2, p3, out_ref):
@@ -513,10 +515,12 @@
     down = pick_call(place_next, pieces)
     down = exchange(down)
 
-    held = adam_full_call(place_cur, arrived, states)
+    held = adam_full_call(place_cur, arrived, states, 0, 2, [])
+    held = adam_full_call(place_cur, arrived, states, 2, 1, held)
 
     hidden = hidden_call(gate_up, all_rows)
-    hidden = [hidden] + [pass_on(hidden, k) for k in range(1, hid_count)]
+    far_hidden = pass_on(hidden, 2)
+    hidden = [hidden, pass_on(hidden, 1), far_hidden, pass_on(hidden, 3)]
     produced = down_call(unpack_call(down), hidden)
     returned = exchange(produced.reshape(slot_count, capacity, quarter))
     place_map = (

time: 159 us -> 158 us (level)
  starting transfers between devices: 28.2 us -> 26.2 us
    ppermute x9, waiting for transfers between devices: 8.63 us -> 11.4 us  [pass_on(): lax.ppermute(value, 'hid', [(i, (i + k) % hid_count) for i in range(hid_c...]
    all_to_all x3, waiting for transfers between devices: 20.5 us -> 18.3 us  [exchange(): lax.all_to_all(value, 'slot', split_axis=0, concat_axis=0, tiled=True)]
    ppermute x9, starting transfers between devices: 11.5 us -> 9.27 us  [pass_on(): lax.ppermute(value, 'hid', [(i, (i + k) % hid_count) for i in range(hid_c...]
    pallas_call x1 -> x2, Pallas kernels: 8.89 us -> 9.65 us  [adam_full_call(): pl.pallas_call(adam_full_kernel, grid=(count,), in_specs=[pl.BlockSpec(me...]
  transfers between devices with their start and end apart: 12 -> 12, of which waited for: 7 -> 8; matrix products, arithmetic and copies ran while one was open for 0% -> 0% of each run, Pallas kernels for 9% -> 9%
where the time goes in v5:
time: 158 us; the launch traced here: 157 us
  blocking collectives  66.3 us (42%)
  Pallas kernels  33.3 us (21%)
  waiting for transfers between devices  29.6 us (19%)
  starting transfers between devices  26.2 us (17%)
    all_to_all x1, blocking collectives, exchange(): lax.all_to_all(value, 'slot', split_axis=0, concat_axis=0, tiled=True)  40.7 us
    all_to_all x1, blocking collectives, shards(): lax.all_to_all(part, ('slot', 'hid'), split_axis=0, concat_axis=0, tiled=...  25.6 us
    all_to_all x3, waiting for transfers between devices, exchange(): lax.all_to_all(value, 'slot', split_axis=0, concat_axis=0, tiled=True)  18.3 us
    all_to_all x3, starting transfers between devices, exchange(): lax.all_to_all(value, 'slot', split_axis=0, concat_axis=0, tiled=True)  16.9 us
    ppermute x9, waiting for transfers between devices, pass_on(): lax.ppermute(value, 'hid', [(i, (i + k) % hid_count) for i in range(hid_c...  11.4 us
    pallas_call x2, Pallas kernels, adam_full_call(): pl.pallas_call(adam_full_kernel, grid=(count,), in_specs=[pl.BlockSpec(me...  9.65 us
    ppermute x9, starting transfers between devices, pass_on(): lax.ppermute(value, 'hid', [(i, (i + k) % hid_count) for i in range(hid_c...  9.27 us
    pallas_call x1, Pallas kernels, scores_call(): pl.pallas_call(scores_kernel, in_specs=[hbm, hbm, hbm, vmem, vmem, vmem],...  8.05 us
  transfers between devices with their start and end apart: 12, of which 8 were waited for; matrix products, arithmetic and copies ran while one was open for 0% of the time, Pallas kernels for 9%

profile of v5, /device:TPU:1, one launch (start us, length us, event | category | flops | bytes accessed | tf_op | source)
XLA Modules:
  0.0 157.4 jit_solution(166482706010777288)
XLA Ops:
  0.6 8.1 %scores.1 = (bf16[1024,2048]{1,0:T(8,128)(2,1)S(1)}, bf16[1024,2048]{1,0:T(8,128)(2,1)S(1)}, f32[192,1024]{1,0:T(8,128)S(1)}, f32[192,1024]{1,0:T(8,128)S(1)}, b...) custom-call(bf16[1024,2048]{1,0:T(8,128)(2,1)} %bitcast.25, ...), custom_call_target="tpu_custom_call" | custom-call | flops 2415919104 | bytes 14680064 | tf_op jit(solution)/shard_map/scores/pallas_call | solution.py:127
  8.7 25.6 %all_to_all.25.parts_ref = f32[128,8,128]{2,1,0:T(8,128)S(1)} all-to-all(f32[128,8,128]{2,1,0:T(8,128)} %get-tuple-element.25), channel_id=1, replica_groups=mesh['slot'=32,'hid'=4] {'slot','hid'}, dimensions={0} | all-to-all | bytes 1048576 | tf_op jit(solution)/shard_map/all_to_all | solution.py:500
  34.3 4.6 %grads.1 = bf16[32,352,128]{2,1,0:T(8,128)(2,1)S(1)} custom-call(f32[128,8,128]{2,1,0:T(8,128)S(1)} %all_to_all.25.parts_ref, s32[8,128]{1,0:T(8,128)S(1)} %bitcast.24, f32[192,1024]{1,0:T(8,128)S(1)} %get-tuple-element.26.a_ref, f32[192,1024]{1,0:T(8,128)S(1)} %get-tuple-element.27.b_ref, bf16[192,1024]{1,0:T(8,128)(2,1)S(1)} %get-tuple-element.28.h_ref, ...), custom_call_target="tpu_custom_call" | custom-call | flops 2415919104 | bytes 12582912 | tf_op jit(solution)/shard_map/grads/pallas_call | solution.py:202
  38.9 0.0 copy-start.1
  38.9 0.0 copy-start.2
  38.9 40.7 %all_to_all.26.arr_ref = bf16[32,352,128]{2,1,0:T(8,128)(2,1)S(1)} all-to-all(bf16[32,352,128]{2,1,0:T(8,128)(2,1)S(1)} %grads.1), channel_id=1, replica_groups=mesh['slot'=32,'hid'=4] {'slot'}, dimensions={0} | all-to-all | bytes 5767168 | tf_op jit(solution)/shard_map/all_to_all | solution.py:491
  79.7 4.5 %adam_pick.1 = (bf16[32,192,128]{2,1,0:T(8,128)(2,1)}, bf16[16,24,128]{2,1,0:T(8,128)(2,1)}, bf16[16,24,128]{2,1,0:T(8,128)(2,1)}, bf16[16,24,128]{2,1,0:T(8,128...) custom-call(s32[32]{0:T(128)S(1)} %copy-done.6, s32[32]{0:T(128)S(1)} %copy-done.8, ...), custom_call_target="tpu_custom_call" | custom-call | flops 20971520 | bytes 6291456 | tf_op jit(solution)/shard_map/adam_pick/pallas_call | solution.py:289
  84.2 4.6 %all-to-all-start.3 = ((bf16[32,192,128]{2,1,0:T(8,128)(2,1)}), bf16[32,192,128]{2,1,0:T(8,128)(2,1)}, u32[]{:S(2)}, u32[]{:S(2)}) async-start(bf16[32,192,128]{2,1,0:T(8,128)(2,1)} %get-tuple-element.36), calls=%async_computation.3 | async-start | bytes 3145728 | tf_op jit(solution)/shard_map/all_to_all | solution.py:491
  88.9 0.4 collective-permute-start
  89.3 1.4 collective-permute-start.1
  90.8 1.1 collective-permute-start.2
  91.8 0.5 collective-permute-start.3
  92.3 1.7 %collective-permute-start.4 = (bf16[512,512]{1,0:T(8,128)(2,1)S(1)}, bf16[512,512]{1,0:T(8,128)(2,1)S(1)}, u32[]{:S(2)}, u32[]{:S(2)}) collective-permute-start(bf16[512,512]{1,0:T(8,128)(2,1)S(1)} %copy-done.4), channel_id=1, source_target_pairs={{0,2},{1,3},{2,0},{3,1},{4,6},{5,7},{6,4},{7,5},{8,10},{9,11},{10,... | collective-permute-start | bytes 1572872 | tf_op jit(solution)/shard_map/ppermute | solution.py:488
  94.0 2.3 %collective-permute-done.p1 = bf16[16,24,128]{2,1,0:T(8,128)(2,1)S(1)} collective-permute-done((bf16[16,24,128]{2,1,0:T(8,128)(2,1)S(1)}, bf16[16,24,128]{2,1,0:T(8,128)(2,1)S(1)}, u32[]{:S(2)}, u32[]{:S(2)}) %collective-permute-start) | collective-permute-done | bytes 98336 | tf_op jit(solution)/shard_map/ppermute | solution.py:488
  96.4 0.6 collective-permute-done.2.p3
  97.0 1.6 pick.1
  98.6 12.8 %all-to-all-done.3.w_ref = bf16[32,192,128]{2,1,0:T(8,128)(2,1)} async-done(((bf16[32,192,128]{2,1,0:T(8,128)(2,1)}), bf16[32,192,128]{2,1,0:T(8,128)(2,1)}, u32[]{:S(2)}, u32[]{:S(2)}) %all-to-all-start.3) | async-done | bytes 1572896 | tf_op jit(solution)/shard_map/all_to_all | solution.py:491
  111.4 4.1 %all-to-all-start.2 = ((bf16[32,96,128]{2,1,0:T(8,128)(2,1)}), bf16[32,96,128]{2,1,0:T(8,128)(2,1)S(1)}, u32[]{:S(2)}, u32[]{:S(2)}) async-start(bf16[32,96,128]{2,1,0:T(8,128)(2,1)} %pick.1), calls=%async_computation.2 | async-start | bytes 1572864 | tf_op jit(solution)/shard_map/all_to_all | solution.py:491
  115.5 3.5 %collective-permute-done.3.r1 = bf16[512,512]{1,0:T(8,128)(2,1)S(1)} collective-permute-done((bf16[512,512]{1,0:T(8,128)(2,1)S(1)}, bf16[512,512]{1,0:T(8,128)(2,1)S(1)}, u32[]{:S(2)}, u32[]{:S(2)}) %collective-permute-start.3) | collective-permute-done | bytes 524320 | tf_op jit(solution)/shard_map/ppermute | solution.py:488
  119.0 0.3 collective-permute-done.5.r3
  119.4 2.9 %hidden.1.h0 = bf16[192,512]{1,0:T(8,128)(2,1)S(1)} custom-call(bf16[32,192,128]{2,1,0:T(8,128)(2,1)} %all-to-all-done.3.w_ref, bf16[512,512]{1,0:T(8,128)(2,1)S(1)} %copy-done.4, bf16[512,512]{1,0:T(8,128)(2,1)S(1)} %collective-permute-done.3.r1, bf16[512,512]{1,0:T(8,128)(2,1)S(1)} %collective-permute-done.4.r2, bf16[512,512]{1,0:T(8,128)(2,1)S(1)} %collective-permute-done.5.r3), custom_call_target="tpu_custom_call" | custom-call | flops 805306368 | bytes 4194304 | tf_op jit(solution)/shard_map/hidden/pallas_call | solution.py:399
  122.2 0.9 collective-permute-start.6
  123.1 3.3 %collective-permute-start.7 = (bf16[192,512]{1,0:T(8,128)(2,1)S(1)}, bf16[192,512]{1,0:T(8,128)(2,1)S(1)}, u32[]{:S(2)}, u32[]{:S(2)}) collective-permute-start(bf16[192,512]{1,0:T(8,128)(2,1)S(1)} %hidden.1.h0), channel_id=1, source_target_pairs={{0,2},{1,3},{2,0},{3,1},{4,6},{5,7},{6,4},{7,5},{8,10},{9,11},{10,... | collective-permute-start | bytes 589832 | tf_op jit(solution)/shard_map/ppermute | solution.py:488
  126.4 3.5 %all-to-all-done.2.w_ref = bf16[32,96,128]{2,1,0:T(8,128)(2,1)S(1)} async-done(((bf16[32,96,128]{2,1,0:T(8,128)(2,1)}), bf16[32,96,128]{2,1,0:T(8,128)(2,1)S(1)}, u32[]{:S(2)}, u32[]{:S(2)}) %all-to-all-start.2) | async-done | bytes 786464 | tf_op jit(solution)/shard_map/all_to_all | solution.py:491
  129.9 0.6 unpack.1.w_ref
  130.4 4.6 %collective-permute-done.7.h2 = bf16[192,512]{1,0:T(8,128)(2,1)S(1)} collective-permute-done((bf16[192,512]{1,0:T(8,128)(2,1)S(1)}, bf16[192,512]{1,0:T(8,128)(2,1)S(1)}, u32[]{:S(2)}, u32[]{:S(2)}) %collective-permute-start.7) | collective-permute-done | bytes 196640 | tf_op jit(solution)/shard_map/ppermute | solution.py:488
  135.0 1.6 down.1
  136.6 8.2 %all-to-all-start.4 = ((bf16[32,16,512]{2,1,0:T(8,128)(2,1)}), bf16[32,16,512]{2,1,0:T(8,128)(2,1)S(1)}, u32[]{:S(2)}, u32[]{:S(2)}) async-start(bf16[32,16,512]{2,1,0:T(8,128)(2,1)} %bitcast.9), calls=%async_computation.4 | async-start | bytes 1048576 | tf_op jit(solution)/shard_map/all_to_all | solution.py:491
  144.8 5.4 %shard_map.147 = (f32[16,3,96,128]{3,2,1,0:T(8,128)}, f32[16,3,96,128]{3,2,1,0:T(8,128)}, f32[16,3,96,128]{3,2,1,0:T(8,128)}) custom-call(s32[32]{0:T(128)} %pc_ref.5, bf16[32,352,128]{2,1,0:T(8,128)(2,1)} %copy-done, f32[16,3,96,128]{3,2,1,0:T(8,128)} %bitcast.15, f32[16,3,96,128]{3,2,1,0:T(8,128)} %bitcast.18, f32[16,3,96,128]{3,2,1,0:T(8,128)} %bitcast.21), custom_call_target="tpu_custom_call" | custom-call | flops 20971520 | bytes 6291456 | tf_op jit(solution)/shard_map/pallas_call | solution.py:322
  150.1 4.3 %shard_map.148 = (f32[16,3,96,128]{3,2,1,0:T(8,128)}, f32[16,3,96,128]{3,2,1,0:T(8,128)}, f32[16,3,96,128]{3,2,1,0:T(8,128)}) custom-call(s32[32]{0:T(128)} %pc_ref.5, bf16[32,352,128]{2,1,0:T(8,128)(2,1)} %copy-done, f32[16,3,96,128]{3,2,1,0:T(8,128)} %bitcast.16, ...), custom_call_target="tpu_custom_call", output_to_operand_aliasing={{0}: (5, {}), {1}: (6, {}), {2}: (7, {})} | custom-call | flops 20971520 | bytes 6291456 | tf_op jit(solution)/shard_map/pallas_call | solution.py:322
  154.4 1.9 %all-to-all-done.4 = bf16[32,16,512]{2,1,0:T(8,128)(2,1)S(1)} async-done(((bf16[32,16,512]{2,1,0:T(8,128)(2,1)}), bf16[32,16,512]{2,1,0:T(8,128)(2,1)S(1)}, u32[]{:S(2)}, u32[]{:S(2)}) %all-to-all-start.4) | async-done | bytes 524320 | tf_op jit(solution)/shard_map/all_to_all | solution.py:491
  156.4 1.1 convolution_convert_fusion
  (30 shorter events, 0.1 us)
Async XLA Ops:
  0.6 33.7 %copy-start.7 = (s32[1,1024]{1,0:T(1,128)S(1)}, s32[1,1024]{1,0:T(1,128)}, u32[]{:S(2)}) copy-start(s32[1,1024]{1,0:T(1,128)} %param.19) | copy-start | bytes 12292
  34.3 45.3 %copy-start.3 = (f32[16,3,1,12288]{3,2,1,0:T(1,128)S(1)}, f32[16,3,1,12288]{3,2,1,0:T(1,128)}, u32[]{:S(2)}) copy-start(f32[16,3,1,12288]{3,2,1,0:T(1,128)} %param.14) | copy-start | bytes 7077892
  38.9 40.8 %copy-start.1 = (f32[16,3,1,12288]{3,2,1,0:T(1,128)S(1)}, f32[16,3,1,12288]{3,2,1,0:T(1,128)}, u32[]{:S(2)}) copy-start(f32[16,3,1,12288]{3,2,1,0:T(1,128)} %param.12) | copy-start | bytes 7077892
  38.9 40.8 %copy-start.2 = (f32[16,3,1,12288]{3,2,1,0:T(1,128)S(1)}, f32[16,3,1,12288]{3,2,1,0:T(1,128)}, u32[]{:S(2)}) copy-start(f32[16,3,1,12288]{3,2,1,0:T(1,128)} %param.13) | copy-start | bytes 7077892
  38.9 40.8 %copy-start.6 = (s32[32]{0:T(128)S(1)}, s32[32]{0:T(128)}, u32[]{:S(2)}) copy-start(s32[32]{0:T(128)} %pc_ref.5) | copy-start | bytes 388
  38.9 40.7 %copy-start.8 = (s32[32]{0:T(128)S(1)}, s32[32]{0:T(128)}, u32[]{:S(2)}) copy-start(s32[32]{0:T(128)} %pn_ref.3) | copy-start | bytes 388
  79.6 4.5 %copy-start = (bf16[32,352,128]{2,1,0:T(8,128)(2,1)}, bf16[32,352,128]{2,1,0:T(8,128)(2,1)S(1)}, u32[]{:S(2)}) copy-start(bf16[32,352,128]{2,1,0:T(8,128)(2,1)S(1)} %all_to_all.26.arr_ref) | copy-start | bytes 8650756
  84.2 4.7 %copy-start.11 = (bf16[16,24,128]{2,1,0:T(8,128)(2,1)S(1)}, bf16[16,24,128]{2,1,0:T(8,128)(2,1)}, u32[]{:S(2)}) copy-start(bf16[16,24,128]{2,1,0:T(8,128)(2,1)} %get-tuple-element.33) | copy-start | bytes 294916
  84.2 5.1 %copy-start.10 = (bf16[16,24,128]{2,1,0:T(8,128)(2,1)S(1)}, bf16[16,24,128]{2,1,0:T(8,128)(2,1)}, u32[]{:S(2)}) copy-start(bf16[16,24,128]{2,1,0:T(8,128)(2,1)} %get-tuple-element.34) | copy-start | bytes 294916
  84.2 6.5 %copy-start.9 = (bf16[16,24,128]{2,1,0:T(8,128)(2,1)S(1)}, bf16[16,24,128]{2,1,0:T(8,128)(2,1)}, u32[]{:S(2)}) copy-start(bf16[16,24,128]{2,1,0:T(8,128)(2,1)} %get-tuple-element.35) | copy-start | bytes 294916
  84.2 7.6 %copy-start.4 = (bf16[512,512]{1,0:T(8,128)(2,1)S(1)}, bf16[512,512]{1,0:T(8,128)(2,1)}, u32[]{:S(2)}) copy-start(bf16[512,512]{1,0:T(8,128)(2,1)} %get-tuple-element.37.r0) | copy-start | bytes 1572868
  84.2 12.8 %copy-start.5 = (bf16[16,24,128]{2,1,0:T(8,128)(2,1)S(1)}, bf16[16,24,128]{2,1,0:T(8,128)(2,1)}, u32[]{:S(2)}) copy-start(bf16[16,24,128]{2,1,0:T(8,128)(2,1)} %get-tuple-element.32.p0) | copy-start | bytes 294916
  84.2 27.2 %all-to-all-start.3 = ((bf16[32,192,128]{2,1,0:T(8,128)(2,1)}), bf16[32,192,128]{2,1,0:T(8,128)(2,1)}, u32[]{:S(2)}, u32[]{:S(2)}) async-start(bf16[32,192,128]{2,1,0:T(8,128)(2,1)} %get-tuple-element.36), calls=%async_computation.3 | async-start | bytes 3145728 | tf_op jit(solution)/shard_map/all_to_all | solution.py:491
  88.9 7.5 %collective-permute-start = (bf16[16,24,128]{2,1,0:T(8,128)(2,1)S(1)}, bf16[16,24,128]{2,1,0:T(8,128)(2,1)S(1)}, u32[]{:S(2)}, u32[]{:S(2)}) collective-permute-start(bf16[16,24,128]{2,1,0:T(8,128)(2,1)S(1)} %copy-done.11), channel_id=1, source_target_pairs={{0,1},{1,2},{2,3},{3,0},{4,5},{5,6},{6,7},{7,4},{8,9},{9,10},{10,1... | collective-permute-start | bytes 294920 | tf_op jit(solution)/shard_map/ppermute | solution.py:488
  89.3 7.0 %collective-permute-start.1 = (bf16[16,24,128]{2,1,0:T(8,128)(2,1)S(1)}, bf16[16,24,128]{2,1,0:T(8,128)(2,1)S(1)}, u32[]{:S(2)}, u32[]{:S(2)}) collective-permute-start(bf16[16,24,128]{2,1,0:T(8,128)(2,1)S(1)} %copy-done.10), channel_id=1, source_target_pairs={{0,2},{1,3},{2,0},{3,1},{4,6},{5,7},{6,4},{7,5},{8,10},{9,11},{10,... | collective-permute-start | bytes 294920 | tf_op jit(solution)/shard_map/ppermute | solution.py:488
  90.8 6.2 %collective-permute-start.2 = (bf16[16,24,128]{2,1,0:T(8,128)(2,1)S(1)}, bf16[16,24,128]{2,1,0:T(8,128)(2,1)S(1)}, u32[]{:S(2)}, u32[]{:S(2)}) collective-permute-start(bf16[16,24,128]{2,1,0:T(8,128)(2,1)S(1)} %copy-done.9), channel_id=1, source_target_pairs={{0,3},{1,0},{2,1},{3,2},{4,7},{5,4},{6,5},{7,6},{8,11},{9,8},{10,9... | collective-permute-start | bytes 294920 | tf_op jit(solution)/shard_map/ppermute | solution.py:488
  91.8 27.2 %collective-permute-start.3 = (bf16[512,512]{1,0:T(8,128)(2,1)S(1)}, bf16[512,512]{1,0:T(8,128)(2,1)S(1)}, u32[]{:S(2)}, u32[]{:S(2)}) collective-permute-start(bf16[512,512]{1,0:T(8,128)(2,1)S(1)} %copy-done.4), channel_id=1, source_target_pairs={{0,1},{1,2},{2,3},{3,0},{4,5},{5,6},{6,7},{7,4},{8,9},{9,10},{10,1... | collective-permute-start | bytes 1572872 | tf_op jit(solution)/shard_map/ppermute | solution.py:488
  92.3 26.7 %collective-permute-start.4 = (bf16[512,512]{1,0:T(8,128)(2,1)S(1)}, bf16[512,512]{1,0:T(8,128)(2,1)S(1)}, u32[]{:S(2)}, u32[]{:S(2)}) collective-permute-start(bf16[512,512]{1,0:T(8,128)(2,1)S(1)} %copy-done.4), channel_id=1, source_target_pairs={{0,2},{1,3},{2,0},{3,1},{4,6},{5,7},{6,4},{7,5},{8,10},{9,11},{10,... | collective-permute-start | bytes 1572872 | tf_op jit(solution)/shard_map/ppermute | solution.py:488
  96.4 23.0 %collective-permute-start.5 = (bf16[512,512]{1,0:T(8,128)(2,1)S(1)}, bf16[512,512]{1,0:T(8,128)(2,1)S(1)}, u32[]{:S(2)}, u32[]{:S(2)}) collective-permute-start(bf16[512,512]{1,0:T(8,128)(2,1)S(1)} %copy-done.4), channel_id=1, source_target_pairs={{0,3},{1,0},{2,1},{3,2},{4,7},{5,4},{6,5},{7,6},{8,11},{9,8},{10,9... | collective-permute-start | bytes 1572872 | tf_op jit(solution)/shard_map/ppermute | solution.py:488
  111.4 18.4 %all-to-all-start.2 = ((bf16[32,96,128]{2,1,0:T(8,128)(2,1)}), bf16[32,96,128]{2,1,0:T(8,128)(2,1)S(1)}, u32[]{:S(2)}, u32[]{:S(2)}) async-start(bf16[32,96,128]{2,1,0:T(8,128)(2,1)} %pick.1), calls=%async_computation.2 | async-start | bytes 1572864 | tf_op jit(solution)/shard_map/all_to_all | solution.py:491
  122.2 8.2 %collective-permute-start.6 = (bf16[192,512]{1,0:T(8,128)(2,1)S(1)}, bf16[192,512]{1,0:T(8,128)(2,1)S(1)}, u32[]{:S(2)}, u32[]{:S(2)}) collective-permute-start(bf16[192,512]{1,0:T(8,128)(2,1)S(1)} %hidden.1.h0), channel_id=1, source_target_pairs={{0,1},{1,2},{2,3},{3,0},{4,5},{5,6},{6,7},{7,4},{8,9},{9,10},{10,1... | collective-permute-start | bytes 589832 | tf_op jit(solution)/shard_map/ppermute | solution.py:488
  123.1 11.9 %collective-permute-start.7 = (bf16[192,512]{1,0:T(8,128)(2,1)S(1)}, bf16[192,512]{1,0:T(8,128)(2,1)S(1)}, u32[]{:S(2)}, u32[]{:S(2)}) collective-permute-start(bf16[192,512]{1,0:T(8,128)(2,1)S(1)} %hidden.1.h0), channel_id=1, source_target_pairs={{0,2},{1,3},{2,0},{3,1},{4,6},{5,7},{6,4},{7,5},{8,10},{9,11},{10,... | collective-permute-start | bytes 589832 | tf_op jit(solution)/shard_map/ppermute | solution.py:488
  126.4 8.6 %collective-permute-start.8 = (bf16[192,512]{1,0:T(8,128)(2,1)S(1)}, bf16[192,512]{1,0:T(8,128)(2,1)S(1)}, u32[]{:S(2)}, u32[]{:S(2)}) collective-permute-start(bf16[192,512]{1,0:T(8,128)(2,1)S(1)} %hidden.1.h0), channel_id=1, source_target_pairs={{0,3},{1,0},{2,1},{3,2},{4,7},{5,4},{6,5},{7,6},{8,11},{9,8},{10,9... | collective-permute-start | bytes 589832 | tf_op jit(solution)/shard_map/ppermute | solution.py:488
  136.6 19.8 %all-to-all-start.4 = ((bf16[32,16,512]{2,1,0:T(8,128)(2,1)}), bf16[32,16,512]{2,1,0:T(8,128)(2,1)S(1)}, u32[]{:S(2)}, u32[]{:S(2)}) async-start(bf16[32,16,512]{2,1,0:T(8,128)(2,1)} %bitcast.9), calls=%async_computation.4 | async-start | bytes 1048576 | tf_op jit(solution)/shard_map/all_to_all | solution.py:491
  150.1 6.2 %copy-start.12 = (s32[1,256]{1,0:T(1,128)S(1)}, s32[1,256]{1,0:T(1,128)}, u32[]{:S(2)}) copy-start(s32[1,256]{1,0:T(1,128)} %get-tuple-element.24) | copy-start | bytes 3076

commit v6 on v5

--- a/solution.py
+++ b/solution.py
@@ -318,19 +318,23 @@
 def adam_full_call(place_cur, arrived, states, first, count, held):
     slots = arrived.shape[0]
     experts, _, lines, _ = states[0].shape
-    state = pl.BlockSpec((experts, 1, lines, LANES), lambda i: (0, first + i, 0, 0))
+    parts = 2 if count == 1 else 1
+    block = lines // parts
+    state = pl.BlockSpec(
+        (experts, 1, block, LANES), lambda i: (0, first + i // parts, i % parts, 0)
+    )
     return pl.pallas_call(
         adam_full_kernel,
-        grid=(count,),
+        grid=(parts * count,),
         in_specs=[
             pl.BlockSpec(memory_space=pltpu.SMEM),
-            pl.BlockSpec((slots, lines, LANES), lambda i: (0, first + i, 0)),
+            pl.BlockSpec((slots, block, LANES), lambda i: (0, parts * first + i, 0)),
             state, state, state,
         ]
         + [pl.BlockSpec(memory_space=pl.ANY)] * len(held),
         out_specs=[state, state, state],
         out_shape=[jax.ShapeDtypeStruct(s.shape, F32) for s in states],
-        scratch_shapes=[pltpu.VMEM((experts, lines, LANES), F32)] * 2,
+        scratch_shapes=[pltpu.VMEM((experts, block, LANES), F32)] * 2,
         input_output_aliases={5 + k: k for k in range(len(held))},
         cost_estimate=pl.CostEstimate(flops=20 << 20, bytes_accessed=6 << 20, transcendentals=0),
         compiler_params=limits(60),

time: 158 us -> 158 us (level)
  no operation moved by 1% of the time
where the time goes in v6:
time: 158 us; the launch traced here: 157 us
  blocking collectives  66.3 us (42%)
  Pallas kernels  32.5 us (21%)
  waiting for transfers between devices  30.4 us (19%)
  starting transfers between devices  26.2 us (17%)
    all_to_all x1, blocking collectives, exchange(): lax.all_to_all(value, 'slot', split_axis=0, concat_axis=0, tiled=True)  40.7 us
    all_to_all x1, blocking collectives, shards(): lax.all_to_all(part, ('slot', 'hid'), split_axis=0, concat_axis=0, tiled=...  25.6 us
    all_to_all x3, waiting for transfers between devices, exchange(): lax.all_to_all(value, 'slot', split_axis=0, concat_axis=0, tiled=True)  19.1 us
    all_to_all x3, starting transfers between devices, exchange(): lax.all_to_all(value, 'slot', split_axis=0, concat_axis=0, tiled=True)  16.9 us
    ppermute x9, waiting for transfers between devices, pass_on(): lax.ppermute(value, 'hid', [(i, (i + k) % hid_count) for i in range(hid_c...  11.4 us
    ppermute x9, starting transfers between devices, pass_on(): lax.ppermute(value, 'hid', [(i, (i + k) % hid_count) for i in range(hid_c...  9.27 us
    pallas_call x2, Pallas kernels, adam_full_call(): pl.pallas_call(adam_full_kernel, grid=(parts * count,), in_specs=[pl.Bloc...  8.84 us
    pallas_call x1, Pallas kernels, scores_call(): pl.pallas_call(scores_kernel, in_specs=[hbm, hbm, hbm, vmem, vmem, vmem],...  8.05 us
  transfers between devices with their start and end apart: 12, of which 8 were waited for; matrix products, arithmetic and copies ran while one was open for 0% of the time, Pallas kernels for 9%

profile of v6, /device:TPU:1, one launch (start us, length us, event | category | flops | bytes accessed | tf_op | source)
XLA Modules:
  0.0 157.4 jit_solution(3154966060244359248)
XLA Ops:
  0.6 8.1 %scores.1 = (bf16[1024,2048]{1,0:T(8,128)(2,1)S(1)}, bf16[1024,2048]{1,0:T(8,128)(2,1)S(1)}, f32[192,1024]{1,0:T(8,128)S(1)}, f32[192,1024]{1,0:T(8,128)S(1)}, b...) custom-call(bf16[1024,2048]{1,0:T(8,128)(2,1)} %bitcast.25, ...), custom_call_target="tpu_custom_call" | custom-call | flops 2415919104 | bytes 14680064 | tf_op jit(solution)/shard_map/scores/pallas_call | solution.py:127
  8.7 25.6 %all_to_all.25.parts_ref = f32[128,8,128]{2,1,0:T(8,128)S(1)} all-to-all(f32[128,8,128]{2,1,0:T(8,128)} %get-tuple-element.25), channel_id=1, replica_groups=mesh['slot'=32,'hid'=4] {'slot','hid'}, dimensions={0} | all-to-all | bytes 1048576 | tf_op jit(solution)/shard_map/all_to_all | solution.py:504
  34.3 4.6 %grads.1 = bf16[32,352,128]{2,1,0:T(8,128)(2,1)S(1)} custom-call(f32[128,8,128]{2,1,0:T(8,128)S(1)} %all_to_all.25.parts_ref, s32[8,128]{1,0:T(8,128)S(1)} %bitcast.24, f32[192,1024]{1,0:T(8,128)S(1)} %get-tuple-element.26.a_ref, f32[192,1024]{1,0:T(8,128)S(1)} %get-tuple-element.27.b_ref, bf16[192,1024]{1,0:T(8,128)(2,1)S(1)} %get-tuple-element.28.h_ref, ...), custom_call_target="tpu_custom_call" | custom-call | flops 2415919104 | bytes 12582912 | tf_op jit(solution)/shard_map/grads/pallas_call | solution.py:202
  38.9 0.0 copy-start.1
  38.9 0.0 copy-start.2
  38.9 40.7 %all_to_all.26.arr_ref = bf16[32,352,128]{2,1,0:T(8,128)(2,1)S(1)} all-to-all(bf16[32,352,128]{2,1,0:T(8,128)(2,1)S(1)} %grads.1), channel_id=1, replica_groups=mesh['slot'=32,'hid'=4] {'slot'}, dimensions={0} | all-to-all | bytes 5767168 | tf_op jit(solution)/shard_map/all_to_all | solution.py:495
  79.7 4.5 %adam_pick.1 = (bf16[32,192,128]{2,1,0:T(8,128)(2,1)}, bf16[16,24,128]{2,1,0:T(8,128)(2,1)}, bf16[16,24,128]{2,1,0:T(8,128)(2,1)}, bf16[16,24,128]{2,1,0:T(8,128...) custom-call(s32[32]{0:T(128)S(1)} %copy-done.6, s32[32]{0:T(128)S(1)} %copy-done.8, ...), custom_call_target="tpu_custom_call" | custom-call | flops 20971520 | bytes 6291456 | tf_op jit(solution)/shard_map/adam_pick/pallas_call | solution.py:289
  84.2 4.6 %all-to-all-start.3 = ((bf16[32,192,128]{2,1,0:T(8,128)(2,1)}), bf16[32,192,128]{2,1,0:T(8,128)(2,1)}, u32[]{:S(2)}, u32[]{:S(2)}) async-start(bf16[32,192,128]{2,1,0:T(8,128)(2,1)} %get-tuple-element.36), calls=%async_computation.3 | async-start | bytes 3145728 | tf_op jit(solution)/shard_map/all_to_all | solution.py:495
  88.9 0.4 collective-permute-start
  89.3 1.4 collective-permute-start.1
  90.8 1.1 collective-permute-start.2
  91.8 0.5 collective-permute-start.3
  92.3 1.7 %collective-permute-start.4 = (bf16[512,512]{1,0:T(8,128)(2,1)S(1)}, bf16[512,512]{1,0:T(8,128)(2,1)S(1)}, u32[]{:S(2)}, u32[]{:S(2)}) collective-permute-start(bf16[512,512]{1,0:T(8,128)(2,1)S(1)} %copy-done.4), channel_id=1, source_target_pairs={{0,2},{1,3},{2,0},{3,1},{4,6},{5,7},{6,4},{7,5},{8,10},{9,11},{10,... | collective-permute-start | bytes 1572872 | tf_op jit(solution)/shard_map/ppermute | solution.py:492
  94.0 2.3 %collective-permute-done.p1 = bf16[16,24,128]{2,1,0:T(8,128)(2,1)S(1)} collective-permute-done((bf16[16,24,128]{2,1,0:T(8,128)(2,1)S(1)}, bf16[16,24,128]{2,1,0:T(8,128)(2,1)S(1)}, u32[]{:S(2)}, u32[]{:S(2)}) %collective-permute-start) | collective-permute-done | bytes 98336 | tf_op jit(solution)/shard_map/ppermute | solution.py:492
  96.4 0.6 collective-permute-done.2.p3
  97.0 1.6 pick.1
  98.6 12.8 %all-to-all-done.3.w_ref = bf16[32,192,128]{2,1,0:T(8,128)(2,1)} async-done(((bf16[32,192,128]{2,1,0:T(8,128)(2,1)}), bf16[32,192,128]{2,1,0:T(8,128)(2,1)}, u32[]{:S(2)}, u32[]{:S(2)}) %all-to-all-start.3) | async-done | bytes 1572896 | tf_op jit(solution)/shard_map/all_to_all | solution.py:495
  111.4 4.1 %all-to-all-start.2 = ((bf16[32,96,128]{2,1,0:T(8,128)(2,1)}), bf16[32,96,128]{2,1,0:T(8,128)(2,1)S(1)}, u32[]{:S(2)}, u32[]{:S(2)}) async-start(bf16[32,96,128]{2,1,0:T(8,128)(2,1)} %pick.1), calls=%async_computation.2 | async-start | bytes 1572864 | tf_op jit(solution)/shard_map/all_to_all | solution.py:495
  115.5 3.5 %collective-permute-done.3.r1 = bf16[512,512]{1,0:T(8,128)(2,1)S(1)} collective-permute-done((bf16[512,512]{1,0:T(8,128)(2,1)S(1)}, bf16[512,512]{1,0:T(8,128)(2,1)S(1)}, u32[]{:S(2)}, u32[]{:S(2)}) %collective-permute-start.3) | collective-permute-done | bytes 524320 | tf_op jit(solution)/shard_map/ppermute | solution.py:492
  119.0 0.3 collective-permute-done.5.r3
  119.4 2.9 %hidden.1.h0 = bf16[192,512]{1,0:T(8,128)(2,1)S(1)} custom-call(bf16[32,192,128]{2,1,0:T(8,128)(2,1)} %all-to-all-done.3.w_ref, bf16[512,512]{1,0:T(8,128)(2,1)S(1)} %copy-done.4, bf16[512,512]{1,0:T(8,128)(2,1)S(1)} %collective-permute-done.3.r1, bf16[512,512]{1,0:T(8,128)(2,1)S(1)} %collective-permute-done.4.r2, bf16[512,512]{1,0:T(8,128)(2,1)S(1)} %collective-permute-done.5.r3), custom_call_target="tpu_custom_call" | custom-call | flops 805306368 | bytes 4194304 | tf_op jit(solution)/shard_map/hidden/pallas_call | solution.py:403
  122.2 0.9 collective-permute-start.6
  123.1 3.3 %collective-permute-start.7 = (bf16[192,512]{1,0:T(8,128)(2,1)S(1)}, bf16[192,512]{1,0:T(8,128)(2,1)S(1)}, u32[]{:S(2)}, u32[]{:S(2)}) collective-permute-start(bf16[192,512]{1,0:T(8,128)(2,1)S(1)} %hidden.1.h0), channel_id=1, source_target_pairs={{0,2},{1,3},{2,0},{3,1},{4,6},{5,7},{6,4},{7,5},{8,10},{9,11},{10,... | collective-permute-start | bytes 589832 | tf_op jit(solution)/shard_map/ppermute | solution.py:492
  126.4 3.5 %all-to-all-done.2.w_ref = bf16[32,96,128]{2,1,0:T(8,128)(2,1)S(1)} async-done(((bf16[32,96,128]{2,1,0:T(8,128)(2,1)}), bf16[32,96,128]{2,1,0:T(8,128)(2,1)S(1)}, u32[]{:S(2)}, u32[]{:S(2)}) %all-to-all-start.2) | async-done | bytes 786464 | tf_op jit(solution)/shard_map/all_to_all | solution.py:495
  129.9 0.6 unpack.1.w_ref
  130.4 4.6 %collective-permute-done.7.h2 = bf16[192,512]{1,0:T(8,128)(2,1)S(1)} collective-permute-done((bf16[192,512]{1,0:T(8,128)(2,1)S(1)}, bf16[192,512]{1,0:T(8,128)(2,1)S(1)}, u32[]{:S(2)}, u32[]{:S(2)}) %collective-permute-start.7) | collective-permute-done | bytes 196640 | tf_op jit(solution)/shard_map/ppermute | solution.py:492
  135.0 1.6 down.1
  136.6 8.2 %all-to-all-start.4 = ((bf16[32,16,512]{2,1,0:T(8,128)(2,1)}), bf16[32,16,512]{2,1,0:T(8,128)(2,1)S(1)}, u32[]{:S(2)}, u32[]{:S(2)}) async-start(bf16[32,16,512]{2,1,0:T(8,128)(2,1)} %bitcast.9), calls=%async_computation.4 | async-start | bytes 1048576 | tf_op jit(solution)/shard_map/all_to_all | solution.py:495
  144.8 5.4 %shard_map.147 = (f32[16,3,96,128]{3,2,1,0:T(8,128)}, f32[16,3,96,128]{3,2,1,0:T(8,128)}, f32[16,3,96,128]{3,2,1,0:T(8,128)}) custom-call(s32[32]{0:T(128)} %pc_ref.5, bf16[32,352,128]{2,1,0:T(8,128)(2,1)} %copy-done, f32[16,3,96,128]{3,2,1,0:T(8,128)} %bitcast.15, f32[16,3,96,128]{3,2,1,0:T(8,128)} %bitcast.18, f32[16,3,96,128]{3,2,1,0:T(8,128)} %bitcast.21), custom_call_target="tpu_custom_call" | custom-call | flops 20971520 | bytes 6291456 | tf_op jit(solution)/shard_map/pallas_call | solution.py:326
  150.1 3.5 %shard_map.148 = (f32[16,3,96,128]{3,2,1,0:T(8,128)}, f32[16,3,96,128]{3,2,1,0:T(8,128)}, f32[16,3,96,128]{3,2,1,0:T(8,128)}) custom-call(s32[32]{0:T(128)} %pc_ref.5, bf16[32,352,128]{2,1,0:T(8,128)(2,1)} %copy-done, f32[16,3,96,128]{3,2,1,0:T(8,128)} %bitcast.16, ...), custom_call_target="tpu_custom_call", output_to_operand_aliasing={{0}: (5, {}), {1}: (6, {}), {2}: (7, {})} | custom-call | flops 20971520 | bytes 6291456 | tf_op jit(solution)/shard_map/pallas_call | solution.py:326
  153.6 2.7 %all-to-all-done.4 = bf16[32,16,512]{2,1,0:T(8,128)(2,1)S(1)} async-done(((bf16[32,16,512]{2,1,0:T(8,128)(2,1)}), bf16[32,16,512]{2,1,0:T(8,128)(2,1)S(1)}, u32[]{:S(2)}, u32[]{:S(2)}) %all-to-all-start.4) | async-done | bytes 524320 | tf_op jit(solution)/shard_map/all_to_all | solution.py:495
  156.4 1.1 convolution_convert_fusion
  (30 shorter events, 0.1 us)
Async XLA Ops:
  0.6 33.7 %copy-start.7 = (s32[1,1024]{1,0:T(1,128)S(1)}, s32[1,1024]{1,0:T(1,128)}, u32[]{:S(2)}) copy-start(s32[1,1024]{1,0:T(1,128)} %param.19) | copy-start | bytes 12292
  34.3 45.3 %copy-start.3 = (f32[16,3,1,12288]{3,2,1,0:T(1,128)S(1)}, f32[16,3,1,12288]{3,2,1,0:T(1,128)}, u32[]{:S(2)}) copy-start(f32[16,3,1,12288]{3,2,1,0:T(1,128)} %param.14) | copy-start | bytes 7077892
  38.9 40.8 %copy-start.1 = (f32[16,3,1,12288]{3,2,1,0:T(1,128)S(1)}, f32[16,3,1,12288]{3,2,1,0:T(1,128)}, u32[]{:S(2)}) copy-start(f32[16,3,1,12288]{3,2,1,0:T(1,128)} %param.12) | copy-start | bytes 7077892
  38.9 40.8 %copy-start.2 = (f32[16,3,1,12288]{3,2,1,0:T(1,128)S(1)}, f32[16,3,1,12288]{3,2,1,0:T(1,128)}, u32[]{:S(2)}) copy-start(f32[16,3,1,12288]{3,2,1,0:T(1,128)} %param.13) | copy-start | bytes 7077892
  38.9 40.8 %copy-start.6 = (s32[32]{0:T(128)S(1)}, s32[32]{0:T(128)}, u32[]{:S(2)}) copy-start(s32[32]{0:T(128)} %pc_ref.5) | copy-start | bytes 388
  38.9 40.7 %copy-start.8 = (s32[32]{0:T(128)S(1)}, s32[32]{0:T(128)}, u32[]{:S(2)}) copy-start(s32[32]{0:T(128)} %pn_ref.3) | copy-start | bytes 388
  79.6 4.5 %copy-start = (bf16[32,352,128]{2,1,0:T(8,128)(2,1)}, bf16[32,352,128]{2,1,0:T(8,128)(2,1)S(1)}, u32[]{:S(2)}) copy-start(bf16[32,352,128]{2,1,0:T(8,128)(2,1)S(1)} %all_to_all.26.arr_ref) | copy-start | bytes 8650756
  84.2 4.7 %copy-start.11 = (bf16[16,24,128]{2,1,0:T(8,128)(2,1)S(1)}, bf16[16,24,128]{2,1,0:T(8,128)(2,1)}, u32[]{:S(2)}) copy-start(bf16[16,24,128]{2,1,0:T(8,128)(2,1)} %get-tuple-element.33) | copy-start | bytes 294916
  84.2 5.1 %copy-start.10 = (bf16[16,24,128]{2,1,0:T(8,128)(2,1)S(1)}, bf16[16,24,128]{2,1,0:T(8,128)(2,1)}, u32[]{:S(2)}) copy-start(bf16[16,24,128]{2,1,0:T(8,128)(2,1)} %get-tuple-element.34) | copy-start | bytes 294916
  84.2 6.5 %copy-start.9 = (bf16[16,24,128]{2,1,0:T(8,128)(2,1)S(1)}, bf16[16,24,128]{2,1,0:T(8,128)(2,1)}, u32[]{:S(2)}) copy-start(bf16[16,24,128]{2,1,0:T(8,128)(2,1)} %get-tuple-element.35) | copy-start | bytes 294916
  84.2 7.6 %copy-start.4 = (bf16[512,512]{1,0:T(8,128)(2,1)S(1)}, bf16[512,512]{1,0:T(8,128)(2,1)}, u32[]{:S(2)}) copy-start(bf16[512,512]{1,0:T(8,128)(2,1)} %get-tuple-element.37.r0) | copy-start | bytes 1572868
  84.2 12.8 %copy-start.5 = (bf16[16,24,128]{2,1,0:T(8,128)(2,1)S(1)}, bf16[16,24,128]{2,1,0:T(8,128)(2,1)}, u32[]{:S(2)}) copy-start(bf16[16,24,128]{2,1,0:T(8,128)(2,1)} %get-tuple-element.32.p0) | copy-start | bytes 294916
  84.2 27.2 %all-to-all-start.3 = ((bf16[32,192,128]{2,1,0:T(8,128)(2,1)}), bf16[32,192,128]{2,1,0:T(8,128)(2,1)}, u32[]{:S(2)}, u32[]{:S(2)}) async-start(bf16[32,192,128]{2,1,0:T(8,128)(2,1)} %get-tuple-element.36), calls=%async_computation.3 | async-start | bytes 3145728 | tf_op jit(solution)/shard_map/all_to_all | solution.py:495
  88.9 7.5 %collective-permute-start = (bf16[16,24,128]{2,1,0:T(8,128)(2,1)S(1)}, bf16[16,24,128]{2,1,0:T(8,128)(2,1)S(1)}, u32[]{:S(2)}, u32[]{:S(2)}) collective-permute-start(bf16[16,24,128]{2,1,0:T(8,128)(2,1)S(1)} %copy-done.11), channel_id=1, source_target_pairs={{0,1},{1,2},{2,3},{3,0},{4,5},{5,6},{6,7},{7,4},{8,9},{9,10},{10,1... | collective-permute-start | bytes 294920 | tf_op jit(solution)/shard_map/ppermute | solution.py:492
  89.3 7.0 %collective-permute-start.1 = (bf16[16,24,128]{2,1,0:T(8,128)(2,1)S(1)}, bf16[16,24,128]{2,1,0:T(8,128)(2,1)S(1)}, u32[]{:S(2)}, u32[]{:S(2)}) collective-permute-start(bf16[16,24,128]{2,1,0:T(8,128)(2,1)S(1)} %copy-done.10), channel_id=1, source_target_pairs={{0,2},{1,3},{2,0},{3,1},{4,6},{5,7},{6,4},{7,5},{8,10},{9,11},{10,... | collective-permute-start | bytes 294920 | tf_op jit(solution)/shard_map/ppermute | solution.py:492
  90.8 6.2 %collective-permute-start.2 = (bf16[16,24,128]{2,1,0:T(8,128)(2,1)S(1)}, bf16[16,24,128]{2,1,0:T(8,128)(2,1)S(1)}, u32[]{:S(2)}, u32[]{:S(2)}) collective-permute-start(bf16[16,24,128]{2,1,0:T(8,128)(2,1)S(1)} %copy-done.9), channel_id=1, source_target_pairs={{0,3},{1,0},{2,1},{3,2},{4,7},{5,4},{6,5},{7,6},{8,11},{9,8},{10,9... | collective-permute-start | bytes 294920 | tf_op jit(solution)/shard_map/ppermute | solution.py:492
  91.8 27.2 %collective-permute-start.3 = (bf16[512,512]{1,0:T(8,128)(2,1)S(1)}, bf16[512,512]{1,0:T(8,128)(2,1)S(1)}, u32[]{:S(2)}, u32[]{:S(2)}) collective-permute-start(bf16[512,512]{1,0:T(8,128)(2,1)S(1)} %copy-done.4), channel_id=1, source_target_pairs={{0,1},{1,2},{2,3},{3,0},{4,5},{5,6},{6,7},{7,4},{8,9},{9,10},{10,1... | collective-permute-start | bytes 1572872 | tf_op jit(solution)/shard_map/ppermute | solution.py:492
  92.3 26.7 %collective-permute-start.4 = (bf16[512,512]{1,0:T(8,128)(2,1)S(1)}, bf16[512,512]{1,0:T(8,128)(2,1)S(1)}, u32[]{:S(2)}, u32[]{:S(2)}) collective-permute-start(bf16[512,512]{1,0:T(8,128)(2,1)S(1)} %copy-done.4), channel_id=1, source_target_pairs={{0,2},{1,3},{2,0},{3,1},{4,6},{5,7},{6,4},{7,5},{8,10},{9,11},{10,... | collective-permute-start | bytes 1572872 | tf_op jit(solution)/shard_map/ppermute | solution.py:492
  96.4 23.0 %collective-permute-start.5 = (bf16[512,512]{1,0:T(8,128)(2,1)S(1)}, bf16[512,512]{1,0:T(8,128)(2,1)S(1)}, u32[]{:S(2)}, u32[]{:S(2)}) collective-permute-start(bf16[512,512]{1,0:T(8,128)(2,1)S(1)} %copy-done.4), channel_id=1, source_target_pairs={{0,3},{1,0},{2,1},{3,2},{4,7},{5,4},{6,5},{7,6},{8,11},{9,8},{10,9... | collective-permute-start | bytes 1572872 | tf_op jit(solution)/shard_map/ppermute | solution.py:492
  111.4 18.4 %all-to-all-start.2 = ((bf16[32,96,128]{2,1,0:T(8,128)(2,1)}), bf16[32,96,128]{2,1,0:T(8,128)(2,1)S(1)}, u32[]{:S(2)}, u32[]{:S(2)}) async-start(bf16[32,96,128]{2,1,0:T(8,128)(2,1)} %pick.1), calls=%async_computation.2 | async-start | bytes 1572864 | tf_op jit(solution)/shard_map/all_to_all | solution.py:495
  122.2 8.2 %collective-permute-start.6 = (bf16[192,512]{1,0:T(8,128)(2,1)S(1)}, bf16[192,512]{1,0:T(8,128)(2,1)S(1)}, u32[]{:S(2)}, u32[]{:S(2)}) collective-permute-start(bf16[192,512]{1,0:T(8,128)(2,1)S(1)} %hidden.1.h0), channel_id=1, source_target_pairs={{0,1},{1,2},{2,3},{3,0},{4,5},{5,6},{6,7},{7,4},{8,9},{9,10},{10,1... | collective-permute-start | bytes 589832 | tf_op jit(solution)/shard_map/ppermute | solution.py:492
  123.1 11.9 %collective-permute-start.7 = (bf16[192,512]{1,0:T(8,128)(2,1)S(1)}, bf16[192,512]{1,0:T(8,128)(2,1)S(1)}, u32[]{:S(2)}, u32[]{:S(2)}) collective-permute-start(bf16[192,512]{1,0:T(8,128)(2,1)S(1)} %hidden.1.h0), channel_id=1, source_target_pairs={{0,2},{1,3},{2,0},{3,1},{4,6},{5,7},{6,4},{7,5},{8,10},{9,11},{10,... | collective-permute-start | bytes 589832 | tf_op jit(solution)/shard_map/ppermute | solution.py:492
  126.4 8.6 %collective-permute-start.8 = (bf16[192,512]{1,0:T(8,128)(2,1)S(1)}, bf16[192,512]{1,0:T(8,128)(2,1)S(1)}, u32[]{:S(2)}, u32[]{:S(2)}) collective-permute-start(bf16[192,512]{1,0:T(8,128)(2,1)S(1)} %hidden.1.h0), channel_id=1, source_target_pairs={{0,3},{1,0},{2,1},{3,2},{4,7},{5,4},{6,5},{7,6},{8,11},{9,8},{10,9... | collective-permute-start | bytes 589832 | tf_op jit(solution)/shard_map/ppermute | solution.py:492
  136.6 19.8 %all-to-all-start.4 = ((bf16[32,16,512]{2,1,0:T(8,128)(2,1)}), bf16[32,16,512]{2,1,0:T(8,128)(2,1)S(1)}, u32[]{:S(2)}, u32[]{:S(2)}) async-start(bf16[32,16,512]{2,1,0:T(8,128)(2,1)} %bitcast.9), calls=%async_computation.4 | async-start | bytes 1048576 | tf_op jit(solution)/shard_map/all_to_all | solution.py:495
  150.1 6.2 %copy-start.12 = (s32[1,256]{1,0:T(1,128)S(1)}, s32[1,256]{1,0:T(1,128)}, u32[]{:S(2)}) copy-start(s32[1,256]{1,0:T(1,128)} %get-tuple-element.24) | copy-start | bytes 3076
